TPU v7x, 32 devices: a whole 2x2x4 slice. The times are simulated.
32 devices in a mesh: gx: 2 (over y), gy: 4 (over x, core), shot: 4 (over z).
Axes of the slice: x: 2, y: 2, z: 4, core: 2. Of those that a mesh axis runs over, the one named last changes fastest.
Arguments:
- adj_prev: float32 [4, 64, 64, 256], P('shot', 'gx', 'gy'), may hold values from -6 to 6
- adj_cur: float32 [4, 64, 64, 256], P('shot', 'gx', 'gy'), may hold values from -6 to 6
- fwd_accel: bfloat16 [4, 4, 64, 64, 256], P('shot', None, 'gx', 'gy'), may hold values from -6 to 6
- courant2: float32 [64, 64, 256], P('gx', 'gy'), may hold values from 0.05 to 0.18
- traces: bfloat16 [4, 4, 512], P('shot', None, ('gx', 'gy')), may hold values from -6 to 6
- weights: bfloat16 [2, 4, 64, 16, 256], P('gx', 'gy'), may hold values from -3 to 3
- rblock: int32 [2, 4, 64], P('gx', 'gy'), may hold values from 0 to 31
- column: int32 [2, 4, 64], P('gx', 'gy'), may hold values from 0 to 511
- counts: int32 [2, 4], P('gx', 'gy'), may hold values from 16 to 64
Outputs:
- adj_prev_out: float32 [4, 64, 64, 256], P('shot', 'gx', 'gy')
- adj_cur_out: float32 [4, 64, 64, 256], P('shot', 'gx', 'gy')
- gradient: float32 [32, 32, 128], P('gx', 'gy')
All inputs are finite; a program needn't handle non-finite values.
Results may differ from a plain program's by a relative error of at most 0.00045.
Values may be sent and summed in bfloat16 or wider, within the bound.
No kernel may reach another device: no remote copies, remote signals or barrier semaphores. Data moves between devices by JAX's collectives and lax.ppermute only.
A program may use at most 128 MiB of HBM per device.

v0:
```python
import functools

import jax
import jax.numpy as jnp
from jax import lax
from jax.experimental import pallas as pl
from jax.experimental.pallas import tpu as pltpu
from jax.sharding import PartitionSpec as P


LAPLACE_COEFS = (-205.0 / 72.0, 8.0 / 5.0, -1.0 / 5.0, 8.0 / 315.0, -1.0 / 560.0)
REACH = 4
VMEM_LIMIT = 16 << 20
F32 = jnp.float32
BF16 = jnp.bfloat16


def vmem_call(kernel, outs, args, scratch=(), flops=0, hbm_in=(), hbm_out=(), smem_in=()):
    in_specs = [
        pl.BlockSpec(memory_space=pltpu.HBM if i in hbm_in else pltpu.SMEM if i in smem_in else pltpu.VMEM)
        for i in range(len(args))
    ]
    args = [pltpu.with_memory_space_constraint(a, pltpu.HBM) if i in hbm_in else a for i, a in enumerate(args)]
    moved = sum(a.size * a.dtype.itemsize for a in args) + sum(o.size * o.dtype.itemsize for o in outs)
    return pl.pallas_call(
        kernel,
        out_shape=tuple(outs),
        in_specs=in_specs,
        out_specs=tuple(
            pl.BlockSpec(memory_space=pltpu.HBM if i in hbm_out else pltpu.VMEM) for i in range(len(outs))
        ),
        scratch_shapes=list(scratch),
        cost_estimate=pl.CostEstimate(flops=flops, bytes_accessed=moved, transcendentals=0),
        compiler_params=pltpu.CompilerParams(vmem_limit_bytes=VMEM_LIMIT),
    )(*args)


def sds(shape, dtype=F32):
    return jax.ShapeDtypeStruct(shape, dtype)


def even_pairs(n):
    pairs = []
    for i in range(0, n - 1, 2):
        pairs += [(i, i + 1), (i + 1, i)]
    return pairs


def odd_pairs(n):
    pairs = []
    for i in range(1, n - 1, 2):
        pairs += [(i, i + 1), (i + 1, i)]
    return pairs + [(0, n - 1), (n - 1, 0)]


def split2(v):
    hi = v.astype(BF16)
    return hi, (v - hi.astype(F32)).astype(BF16)


def dot(a, b):
    return jnp.dot(a, b, preferred_element_type=F32)


def put_y_face(cur, out, high):
    cx, cy, _ = cur.shape
    start = cy - REACH if high else 0
    for i in range(cx // 2):
        out[i, 0:REACH, :] = cur[2 * i, start : start + REACH, :]
        out[i, REACH : 2 * REACH, :] = cur[2 * i + 1, start : start + REACH, :]


def put_faces(cur, gx_index, gy_index, ye, yo, xe, xo):
    cx, cy, _ = cur.shape
    y_even = gy_index % 2 == 0
    x_even = gx_index % 2 == 0

    @pl.when(y_even)
    def _():
        put_y_face(cur, ye, True)
        if yo is not None:
            put_y_face(cur, yo, False)

    @pl.when(jnp.logical_not(y_even))
    def _():
        put_y_face(cur, ye, False)
        if yo is not None:
            put_y_face(cur, yo, True)

    half = cy // 8
    low = jnp.where(x_even, cx - REACH, 0)
    for r in range(REACH):
        for h in range(half):
            xe[r * half + h, :, :] = cur[low + r, 8 * h : 8 * h + 8, :]
            if xo is not None:
                xo[r * half + h, :, :] = cur[cx - REACH - low + r, 8 * h : 8 * h + 8, :]


def add_y_halo(nxt, c2, recv, high):
    cx, cy, nz = nxt.shape
    w = LAPLACE_COEFS
    row = lax.broadcasted_iota(jnp.int32, (8, nz), 0) % REACH
    coefs = {}
    for k in range(1, REACH + 1):
        shift = REACH - k
        keep = (row >= shift) if high else (row < k)
        coefs[k] = jnp.where(keep, w[k], 0.0)
    start = cy - REACH if high else 0
    for i in range(cx // 2):
        m = recv[i, :, :]
        total = w[REACH] * m
        for k in range(1, REACH):
            shift = REACH - k
            total = total + coefs[k] * pltpu.roll(m, shift if high else 8 - shift, 0)
        for h in range(2):
            rows = slice(start, start + REACH)
            nxt[2 * i + h, rows, :] = (
                nxt[2 * i + h, rows, :] + c2[2 * i + h, rows, :] * total[REACH * h : REACH * h + REACH, :]
            )


def add_x_halo(nxt, c2, recv, high):
    cx, cy, _ = nxt.shape
    w = LAPLACE_COEFS
    half = cy // 8
    for r in range(REACH):
        x = cx - 1 - r if high else r
        for h in range(half):
            total = None
            for k in range(r + 1, REACH + 1):
                row = (k - r - 1) if high else (REACH + r - k)
                term = w[k] * recv[row * half + h, :, :]
                total = term if total is None else total + term
            ys = slice(8 * h, 8 * h + 8)
            nxt[x, ys, :] = nxt[x, ys, :] + c2[x, ys, :] * total


def add_halos(nxt, c2, gx_index, gy_index, ye, yo, xe, xo):
    for axis, index, even, odd, add in (("gy", gy_index, ye, yo, add_y_halo), ("gx", gx_index, xe, xo, add_x_halo)):
        is_even = index % 2 == 0
        inner = jnp.logical_and(index > 0, index < lax.axis_size(axis) - 1)

        @pl.when(is_even)
        def _(even=even, add=add):
            add(nxt, c2, even, True)

        @pl.when(jnp.logical_not(is_even))
        def _(even=even, add=add):
            add(nxt, c2, even, False)

        if odd is not None:

            @pl.when(jnp.logical_and(inner, is_even))
            def _(odd=odd, add=add):
                add(nxt, c2, odd, False)

            @pl.when(jnp.logical_and(inner, jnp.logical_not(is_even)))
            def _(odd=odd, add=add):
                add(nxt, c2, odd, True)


def load_kernel(
    cur_in, prev_in, c2_in, weights_in, traces_in, col_in, rb_in, counts,
    cur, prev, c2, weights, ye, yo, xe, own, toeplitz, select, owners,
    traces, col, rb, sems,
    *, with_yo, each, rblk,
):
    gx_index, gy_index = lax.axis_index("gx"), lax.axis_index("gy")
    me = gx_index * lax.axis_size("gy") + gy_index
    pairs = (
        (cur_in, cur), (col_in, col), (rb_in, rb), (traces_in, traces), (prev_in, prev), (c2_in, c2), (weights_in, weights),
    )
    copies = [pltpu.make_async_copy(src, dst, sems.at[i]) for i, (src, dst) in enumerate(pairs)]
    for copy in copies:
        copy.start()
    nz = toeplitz.shape[1]
    distance = jnp.abs(
        lax.broadcasted_iota(jnp.int32, (nz, nz), 0) - lax.broadcasted_iota(jnp.int32, (nz, nz), 1)
    )
    band = jnp.where(distance == 0, 3.0 * LAPLACE_COEFS[0], 0.0)
    for k in range(1, REACH + 1):
        band = band + jnp.where(distance == k, LAPLACE_COEFS[k], 0.0)
    hi, lo = split2(band)
    toeplitz[0:nz, :] = hi
    toeplitz[nz : 2 * nz, :] = lo
    for copy in copies[1:4]:
        copy.wait()
    wide = jnp.concatenate([col[...]] * 3, axis=1)
    rows = lax.broadcasted_iota(jnp.int32, select.shape, 0)
    select[...] = jnp.where(rows == wide, 1.0, 0.0).astype(BF16)
    slots, lanes = owners.shape
    eye = lax.broadcasted_iota(jnp.int32, (slots, slots), 0) == lax.broadcasted_iota(jnp.int32, (slots, slots), 1)
    block_of = jnp.sum(jnp.where(eye, jnp.broadcast_to(rb[...], (slots, slots)), 0), axis=1, keepdims=True)
    owner = lax.div(block_of, jnp.int32(each))
    group = block_of - owner * each
    slot = lax.broadcasted_iota(jnp.int32, (slots, lanes), 0)
    lane = lax.broadcasted_iota(jnp.int32, (slots, lanes), 1)
    used = jnp.logical_and(slot < counts[0, 0], lax.div(lane, jnp.int32(rblk)) == group)
    owners[...] = jnp.where(used, jnp.bitwise_xor(owner, me), -1)
    steps, per = traces.shape
    own[...] = jnp.zeros(own.shape, F32)
    own[0, 0:steps, 0:per] = traces[...].astype(F32)
    copies[0].wait()
    put_faces(cur, gx_index, gy_index, ye, yo if with_yo else None, xe, None)
    for copy in copies[4:]:
        copy.wait()


def flush_kernel(a_in, b_in, a_out, b_out, sems):
    copies = [
        pltpu.make_async_copy(src, dst, sems.at[i]) for i, (src, dst) in enumerate(((a_in, a_out), (b_in, b_out)))
    ]
    for copy in copies:
        copy.start()
    for copy in copies:
        copy.wait()


def update(cur, prev, c2, toeplitz, out, ypad, source=None, fine=None):
    cx, cy, nz = cur.shape
    w = LAPLACE_COEFS
    zero = jnp.zeros((8, nz), F32)
    for x in range(cx):
        ypad[x, 0:8, :] = zero
        ypad[x, 8 : 8 + cy, :] = cur[x, :, :]
        ypad[x, 8 + cy : 16 + cy, :] = zero
    chunk = 8
    rows = chunk * cy
    t_hi = toeplitz[0:nz, :]
    t_lo = toeplitz[nz : 2 * nz, :]
    for m in range(cx // chunk):
        v = cur[m * chunk : (m + 1) * chunk, :, :].reshape(rows, nz)
        hi, lo = split2(v)
        lz = dot(hi, t_hi) + dot(lo, t_hi) + dot(hi, t_lo)
        if source is not None:
            select, contrib = source
            src = dot(select[m * rows : (m + 1) * rows, :], contrib)
        for j in range(chunk):
            x = m * chunk + j
            total = lz[j * cy : (j + 1) * cy, :]
            for k in range(1, REACH + 1):
                pair = ypad[x, 8 - k : 8 - k + cy, :] + ypad[x, 8 + k : 8 + k + cy, :]
                if x - k >= 0:
                    pair = pair + cur[x - k, :, :]
                if x + k < cx:
                    pair = pair + cur[x + k, :, :]
                total = total + w[k] * pair
            here = cur[x, :, :]
            value = (2.0 * here - prev[x, :, :]) + c2[x, :, :] * total
            if source is not None:
                value = value + src[j * cy : (j + 1) * cy, :]
            out[x, :, :] = value
            if fine is not None:
                fine_in, accel, fine_out = fine
                term = accel[x, :, :].astype(F32) * here
                fine_out[x, :, :] = term if fine_in is None else fine_in[x, :, :] + term


def first_update_kernel(cur, prev, c2, toeplitz, out, ypad):
    update(cur, prev, c2, toeplitz, out, ypad)


def update_kernel(cur, prev, c2, toeplitz, select, contrib, accel, *rest, step):
    if step == 1:
        out, fine_out, ypad = rest
        fine_in = None
    else:
        fine_in, out, fine_out, ypad = rest
    update(
        cur, prev, c2, toeplitz, out, ypad,
        source=(select, contrib[step]), fine=(fine_in, accel.at[step - 1], fine_out),
    )


def contributions(owners, weights, blocks, patterns, contrib, wide):
    slots, rblk, nz = weights.shape
    steps = contrib.shape[0]
    lanes = 128
    picked = [jnp.zeros((slots, lanes), F32) for _ in range(steps)]
    for tile, pattern in zip(blocks, patterns):
        mask = owners[...] == pattern
        for t in range(steps):
            picked[t] = jnp.where(mask, tile[t : t + 1, :], picked[t])
    spread = (
        lax.rem(lax.broadcasted_iota(jnp.int32, (lanes, lanes), 0), jnp.int32(rblk))
        == lax.rem(lax.broadcasted_iota(jnp.int32, (lanes, lanes), 1), jnp.int32(rblk))
    )
    spread = jnp.where(spread, 1.0, 0.0).astype(BF16)
    tiled = [dot(p.astype(BF16), spread) for p in picked]
    together = lanes // rblk
    diagonal = lax.broadcasted_iota(jnp.int32, (together, lanes), 0) == lax.div(
        lax.broadcasted_iota(jnp.int32, (together, lanes), 1), jnp.int32(rblk)
    )
    for q in range(slots // together):
        rows = slice(q * together, (q + 1) * together)
        left = jnp.concatenate([jnp.where(diagonal, v[rows, :], 0.0) for v in tiled], axis=0).astype(BF16)
        right = weights[q * together : (q + 1) * together, :, :].reshape(together * rblk, nz)
        got = dot(left, right)
        for t in range(steps):
            wide[t, rows, :] = got[t * together : (t + 1) * together, :]
    for t in range(steps):
        hi, mid = split2(wide[t, :, :])
        rest = wide[t, :, :] - hi.astype(F32) - mid.astype(F32)
        contrib[t, 0:slots, :] = hi
        contrib[t, slots : 2 * slots, :] = mid
        contrib[t, 2 * slots : 3 * slots, :] = rest.astype(BF16)


def unpack(refs, with_yo, with_xo):
    refs = list(refs)
    ye = refs.pop(0)
    yo = refs.pop(0) if with_yo else None
    xe = refs.pop(0)
    xo = refs.pop(0) if with_xo else None
    return ye, yo, xe, xo, refs


def first_correct_kernel(owners, weights, select, part, c2, *refs, with_yo, with_xo, holds, patterns):
    gx_index, gy_index = lax.axis_index("gx"), lax.axis_index("gy")
    ye, yo, xe, xo, refs = unpack(refs, with_yo, with_xo)
    held, refs = refs[:holds], refs[holds:]
    nxt, contrib, refs = refs[0], refs[1], refs[2:]
    oye, oyo, oxe, oxo, refs = unpack(refs, with_yo, with_xo)
    wide = refs[0]
    lanes = 128
    tiles = []
    for ref in held:
        for i in range(ref.shape[0]):
            tiles += [ref[i][:, 0:lanes], ref[i][:, lanes : 2 * lanes]]
    contributions(owners, weights, tiles, patterns, contrib, wide)
    cx, cy, nz = nxt.shape
    chunk = 8
    rows = chunk * cy
    for m in range(cx // chunk):
        src = dot(select[m * rows : (m + 1) * rows, :], contrib[0])
        at = slice(m * chunk, (m + 1) * chunk)
        nxt[at, :, :] = part[at, :, :] + src.reshape(chunk, cy, nz)
    add_halos(nxt, c2, gx_index, gy_index, ye, yo, xe, xo)
    put_faces(nxt, gx_index, gy_index, oye, oyo, oxe, oxo)


def correct_kernel(part, c2, *refs, with_yo, with_xo):
    gx_index, gy_index = lax.axis_index("gx"), lax.axis_index("gy")
    ye, yo, xe, xo, refs = unpack(refs, with_yo, with_xo)
    nxt, refs = refs[0], refs[1:]
    oye, oyo, oxe, oxo, refs = unpack(refs, with_yo, with_xo)
    nxt[...] = part[...]
    add_halos(nxt, c2, gx_index, gy_index, ye, yo, xe, xo)
    put_faces(nxt, gx_index, gy_index, oye, oyo, oxe, oxo)


def last_kernel(part, c2, accel, fine, *refs, with_yo, with_xo, step):
    gx_index, gy_index = lax.axis_index("gx"), lax.axis_index("gy")
    ye, yo, xe, xo, refs = unpack(refs, with_yo, with_xo)
    nxt, coarse, middle = refs
    cx, cy, nz = nxt.shape
    nxt[...] = part[...]
    add_halos(nxt, c2, gx_index, gy_index, ye, yo, xe, xo)
    pairs = lax.div(lax.broadcasted_iota(jnp.int32, (nz, nz // 2), 0), jnp.int32(2)) == lax.broadcasted_iota(
        jnp.int32, (nz, nz // 2), 1
    )
    pairs = jnp.where(pairs, 0.125, 0.0).astype(BF16)
    chunk = 8
    for m in range(cx // (2 * chunk)):
        summed = []
        for j in range(chunk):
            x = 2 * (m * chunk + j)
            a = fine[x, :, :] + accel[step, x, :, :].astype(F32) * nxt[x, :, :]
            b = fine[x + 1, :, :] + accel[step, x + 1, :, :].astype(F32) * nxt[x + 1, :, :]
            summed.append(a + b)
        hi, lo = split2(jnp.concatenate(summed, axis=0))
        got = dot(hi, pairs) + dot(lo, pairs)
        middle[m * chunk * cy : (m + 1) * chunk * cy, :] = got
    half = cx * cy // 4
    both = middle[pl.ds(0, half, 2), :] + middle[pl.ds(1, half, 2), :]
    coarse[...] = both.reshape(coarse.shape)


def local(adj_prev, adj_cur, fwd_accel, courant2, traces, weights, rblock, column, counts):
    accel = fwd_accel[0]
    cx, cy, nz = courant2.shape
    steps = accel.shape[0]
    slots, rblk = weights.shape[2:4]
    per = traces.shape[2]
    nx, ny, nshot = lax.axis_size("gx"), lax.axis_size("gy"), lax.axis_size("shot")
    with_yo, with_xo = ny > 2, nx > 2
    y_msg, x_msg = (cx // 2, 8, nz), (REACH * cy // 8, 8, nz)
    tile = (cx, cy, nz)
    cells = cx * cy * nz
    lanes = 128

    def xor(size, bit):
        return [(i, i ^ bit) for i in range(size)]

    theirs = lax.ppermute(traces[0], "gy", even_pairs(ny))
    cur, prev, c2, wts, ye, yo, xe, own, toeplitz, select, owners = vmem_call(
        functools.partial(load_kernel, with_yo=with_yo, each=per // rblk, rblk=rblk),
        [
            sds(tile), sds(tile), sds(tile), sds((slots, rblk, nz), BF16),
            sds(y_msg), sds(y_msg), sds(x_msg), sds((1, 8, lanes)),
            sds((2 * nz, nz), BF16), sds((cx * cy, 3 * slots), BF16), sds((slots, lanes), jnp.int32),
        ],
            [adj_cur[0], adj_prev[0], courant2, weights[0, 0], traces[0], column[0], rblock[0], counts],
        [
            pltpu.VMEM((steps, per), BF16), pltpu.VMEM((1, slots), jnp.int32), pltpu.VMEM((1, slots), jnp.int32),
            pltpu.SemaphoreType.DMA((7,)),
        ],
        hbm_in=tuple(range(7)),
        smem_in=(7,),
    )

    theirs = jnp.pad(theirs.astype(F32), ((0, 8 - steps), (0, lanes - per)))[None]
    pair = jnp.concatenate([own, theirs], axis=2)
    rxe = lax.ppermute(jnp.concatenate([xe, pair], axis=0), "gx", even_pairs(nx))
    ryo = lax.ppermute(yo, "gy", odd_pairs(ny)) if with_yo else None
    rxo = None
    if with_xo:
        low = cur[0:REACH].reshape(x_msg)
        high = cur[cx - REACH :].reshape(x_msg)
        rxo = lax.ppermute(jnp.where(lax.axis_index("gx") % 2 == 0, low, high), "gx", odd_pairs(nx))
    patterns = [0, 1, ny, ny + 1]
    now = jnp.concatenate([pair, rxe[x_msg[0] :]], axis=0)
    held = [now]
    for axis, size, stride in (("gy", ny, 1), ("gx", nx, ny)):
        bit = 2
        while bit < size:
            got = lax.ppermute(now, axis, xor(size, bit))
            held.append(got)
            patterns = patterns + [p ^ (bit * stride) for p in patterns]
            bit *= 2
            now = jnp.concatenate([now, got], axis=0)
    rye = lax.ppermute(ye, "gy", even_pairs(ny))

    ypad = pltpu.VMEM((cx, cy + 16, nz), F32)
    part = vmem_call(first_update_kernel, [sds(tile)], [cur, prev, c2, toeplitz], [ypad], flops=cells * 60)[0]

    def given(ye, yo, xe, xo):
        return [a for a in (ye, yo, xe, xo) if a is not None]

    def face_shapes():
        return given(sds(y_msg), sds(y_msg) if with_yo else None, sds(x_msg), sds(x_msg) if with_xo else None)

    def taken(faces):
        faces = list(faces)
        ye = faces.pop(0)
        yo = faces.pop(0) if with_yo else None
        xe = faces.pop(0)
        xo = faces.pop(0) if with_xo else None
        return ye, yo, xe, xo

    nxt, contrib, *faces = vmem_call(
        functools.partial(
            first_correct_kernel, with_yo=with_yo, with_xo=with_xo, holds=len(held), patterns=tuple(patterns)
        ),
        [sds(tile), sds((steps, 3 * slots, nz), BF16)] + face_shapes(),
        [owners, wts, select, part, c2] + given(rye, ryo, rxe, rxo) + held,
        [pltpu.VMEM((steps, slots, nz), F32)],
    )
    previous, current = cur, nxt
    fine = None
    for step in range(1, steps):
        ye, yo, xe, xo = taken(faces)
        ryo = lax.ppermute(yo, "gy", odd_pairs(ny)) if with_yo else None
        rxe = lax.ppermute(xe, "gx", even_pairs(nx))
        rxo = lax.ppermute(xo, "gx", odd_pairs(nx)) if with_xo else None
        rye = lax.ppermute(ye, "gy", even_pairs(ny))
        args = [current, previous, c2, toeplitz, select, contrib, accel]
        if fine is not None:
            args.append(fine)
        part, fine = vmem_call(
            functools.partial(update_kernel, step=step), [sds(tile), sds(tile)], args, [ypad],
            flops=cells * 60,
        )
        halos = given(rye, ryo, rxe, rxo)
        if step < steps - 1:
            nxt, *faces = vmem_call(
                functools.partial(correct_kernel, with_yo=with_yo, with_xo=with_xo),
                [sds(tile)] + face_shapes(),
                [part, c2] + halos,
            )
        else:
            nxt, coarse = vmem_call(
                functools.partial(last_kernel, with_yo=with_yo, with_xo=with_xo, step=step),
                [sds(tile), sds((cx // 2, cy // 2, nz // 2))],
                [part, c2, accel, fine] + halos,
                [pltpu.VMEM((cx * cy // 2, nz // 2), F32)],
            )
        previous, current = current, nxt
    bit = 1
    while bit < nshot:
        coarse = coarse + lax.ppermute(coarse, "shot", xor(nshot, bit))
        bit *= 2
    previous, current = vmem_call(
        flush_kernel, [sds(tile), sds(tile)], [previous, current], [pltpu.SemaphoreType.DMA((2,))],
        hbm_out=(0, 1),
    )
    return (previous[None], current[None], coarse)


def solution(mesh):
    return jax.shard_map(
        local,
        mesh=mesh,
        in_specs=(
            P("shot", "gx", "gy", None),
            P("shot", "gx", "gy", None),
            P("shot", None, "gx", "gy", None),
            P("gx", "gy", None),
            P("shot", None, ("gx", "gy")),
            P("gx", "gy", None, None, None),
            P("gx", "gy", None),
            P("gx", "gy", None),
            P("gx", "gy"),
        ),
        out_specs=(P("shot", "gx", "gy", None), P("shot", "gx", "gy", None), P("gx", "gy", None)),
        check_vma=False,
    )
```

profile of v0, /device:TPU:0, one launch (start us, length us, event | category | flops | bytes accessed | tf_op | source)
XLA Modules:
  0.0 42.8 jit_solution(7104130476450540381)
XLA Ops:
  2.5 1.6 %shard_map.112 = (f32[32,16,256]{2,1,0:T(8,128)S(1)}, f32[32,16,256]{2,1,0:T(8,128)S(1)}, f32[32,16,256]{2,1,0:T(8,128)S(1)}, bf16[64,16,256]{2,1,0:T(8,128)(2,1...) custom-call(f32[32,16,256]{2,1,0:T(8,128)} %bitcast.16, ...), custom_call_target="tpu_custom_call" | custom-call | bytes 5018628 | tf_op jit(solution)/shard_map/pallas_call | solution.py:25
  4.1 2.6 %collective-permute-start.3 = (f32[9,8,256]{2,1,0:T(8,128)S(1)}, f32[9,8,256]{2,1,0:T(8,128)S(1)}, u32[]{:S(2)}, u32[]{:S(2)}) collective-permute-start(f32[9,8,256]{2,1,0:T(8,128)S(1)} %maximum_maximum_fusion), channel_id=1, source_target_pairs={{0,16},{16,0},{1,17},{17,1},{2,18},{18,2},{3,19},{19,3},{4,20},{20... | collective-permute-start | bytes 221192 | tf_op jit(solution)/shard_map/ppermute | solution.py:414
  6.9 1.4 %collective-permute-start.1 = (f32[16,8,256]{2,1,0:T(8,128)S(1)}, f32[16,8,256]{2,1,0:T(8,128)S(1)}, u32[]{:S(2)}, u32[]{:S(2)}) collective-permute-start(f32[16,8,256]{2,1,0:T(8,128)S(1)} %get-tuple-element.45), channel_id=1, source_target_pairs={{4,8},{8,4},{0,12},{12,0},{5,9},{9,5},{1,13},{13,1},{6,10},{10,6},... | collective-permute-start | bytes 393224 | tf_op jit(solution)/shard_map/ppermute | solution.py:415
  8.3 1.3 %collective-permute-done.3.refs_2_ = f32[9,8,256]{2,1,0:T(8,128)S(1)} collective-permute-done((f32[9,8,256]{2,1,0:T(8,128)S(1)}, f32[9,8,256]{2,1,0:T(8,128)S(1)}, u32[]{:S(2)}, u32[]{:S(2)}) %collective-permute-start.3) | collective-permute-done | bytes 73760 | tf_op jit(solution)/shard_map/ppermute | solution.py:414
  9.7 1.7 %collective-permute-start.4 = (f32[2,8,256]{2,1,0:T(8,128)S(1)}, f32[2,8,256]{2,1,0:T(8,128)S(1)}, u32[]{:S(2)}, u32[]{:S(2)}) collective-permute-start(f32[2,8,256]{2,1,0:T(8,128)S(1)} %pad_maximum_fusion.refs_3_), channel_id=1, source_target_pairs={{0,8},{4,12},{8,0},{12,4},{1,9},{5,13},{9,1},{13,5},{2,10},{6,14},... | collective-permute-start | bytes 49160 | tf_op jit(solution)/shard_map/ppermute | solution.py:427
  11.4 1.3 %shard_map.113.part = f32[32,16,256]{2,1,0:T(8,128)S(1)} custom-call(f32[32,16,256]{2,1,0:T(8,128)S(1)} %get-tuple-element.40.cur.prev, f32[32,16,256]{2,1,0:T(8,128)S(1)} %get-tuple-element.41.prev, f32[32,16,256]{2,1,0:T(8,128)S(1)} %get-tuple-element.42.c2, bf16[512,256]{1,0:T(8,128)(2,1)S(1)} %get-tuple-element.43.toeplitz), custom_call_target="tpu_custom_call" | custom-call | flops 7864320 | bytes 2359296 | tf_op jit(solution)/shard_map/pallas_call | solution.py:25
  13.4 0.7 %shard_map.114 = (f32[32,16,256]{2,1,0:T(8,128)S(1)}, bf16[4,192,256]{2,1,0:T(8,128)(2,1)S(1)}, f32[16,8,256]{2,1,0:T(8,128)S(1)}, f32[16,8,256]{2,1,0:T(8,128)S(1)}, f32[8,8,256]{2,1,0:T(8,128)S(1)}) custom-call(s32[64,128]{1,0:T(8,128)S(1)} %get-tuple-element.37.owners, bf16[64,16,256]{2,1,0:T(8,128)(2,1)S(1)} %get-tuple-element.38.weights, ...), custom_call_target="tpu_custom_call" | custom-call | bytes 3416064 | tf_op jit(solution)/shard_map/pallas_call | solution.py:25
  14.2 1.9 %collective-permute-start.6 = (f32[16,8,256]{2,1,0:T(8,128)S(1)}, f32[16,8,256]{2,1,0:T(8,128)S(1)}, u32[]{:S(2)}, u32[]{:S(2)}) collective-permute-start(f32[16,8,256]{2,1,0:T(8,128)S(1)} %get-tuple-element.52), channel_id=1, source_target_pairs={{4,8},{8,4},{0,12},{12,0},{5,9},{9,5},{1,13},{13,1},{6,10},{10,6},... | collective-permute-start | bytes 393224 | tf_op jit(solution)/shard_map/ppermute | solution.py:463
  16.1 1.5 %collective-permute-start.7 = (f32[8,8,256]{2,1,0:T(8,128)S(1)}, f32[8,8,256]{2,1,0:T(8,128)S(1)}, u32[]{:S(2)}, u32[]{:S(2)}) collective-permute-start(f32[8,8,256]{2,1,0:T(8,128)S(1)} %get-tuple-element.53), channel_id=1, source_target_pairs={{0,16},{16,0},{1,17},{17,1},{2,18},{18,2},{3,19},{19,3},{4,20},{20... | collective-permute-start | bytes 196616 | tf_op jit(solution)/shard_map/ppermute | solution.py:464
  17.6 1.5 %shard_map.115 = (f32[32,16,256]{2,1,0:T(8,128)S(1)}, f32[32,16,256]{2,1,0:T(8,128)S(1)}) custom-call(f32[32,16,256]{2,1,0:T(8,128)S(1)} %get-tuple-element.48.cur.prev, f32[32,16,256]{2,1,0:T(8,128)S(1)} %get-tuple-element.40.cur.prev, f32[32,16,256]{2,1,0:T(8,128)S(1)} %get-tuple-element.42.c2, bf16[512,256]{1,0:T(8,128)(2,1)S(1)} %get-tuple-element.43.toeplitz, ...), custom_call_target="tpu_custom_call" | custom-call | flops 7864320 | bytes 4521984 | tf_op jit(solution)/shard_map/pallas_call | solution.py:25
  19.1 1.3 %collective-permute-done.7.refs_2_ = f32[8,8,256]{2,1,0:T(8,128)S(1)} collective-permute-done((f32[8,8,256]{2,1,0:T(8,128)S(1)}, f32[8,8,256]{2,1,0:T(8,128)S(1)}, u32[]{:S(2)}, u32[]{:S(2)}) %collective-permute-start.7) | collective-permute-done | bytes 65568 | tf_op jit(solution)/shard_map/ppermute | solution.py:464
  20.7 1.0 %collective-permute-start.9 = (f32[16,8,256]{2,1,0:T(8,128)S(1)}, f32[16,8,256]{2,1,0:T(8,128)S(1)}, u32[]{:S(2)}, u32[]{:S(2)}) collective-permute-start(f32[16,8,256]{2,1,0:T(8,128)S(1)} %get-tuple-element.58), channel_id=1, source_target_pairs={{4,8},{8,4},{0,12},{12,0},{5,9},{9,5},{1,13},{13,1},{6,10},{10,6},... | collective-permute-start | bytes 393224 | tf_op jit(solution)/shard_map/ppermute | solution.py:463
  21.7 1.5 %collective-permute-start.10 = (f32[8,8,256]{2,1,0:T(8,128)S(1)}, f32[8,8,256]{2,1,0:T(8,128)S(1)}, u32[]{:S(2)}, u32[]{:S(2)}) collective-permute-start(f32[8,8,256]{2,1,0:T(8,128)S(1)} %get-tuple-element.59), channel_id=1, source_target_pairs={{0,16},{16,0},{1,17},{17,1},{2,18},{18,2},{3,19},{19,3},{4,20},{20... | collective-permute-start | bytes 196616 | tf_op jit(solution)/shard_map/ppermute | solution.py:464
  23.2 1.4 %shard_map.117 = (f32[32,16,256]{2,1,0:T(8,128)S(1)}, f32[32,16,256]{2,1,0:T(8,128)S(1)}) custom-call(f32[32,16,256]{2,1,0:T(8,128)S(1)} %get-tuple-element.54.cur.prev, f32[32,16,256]{2,1,0:T(8,128)S(1)} %get-tuple-element.48.cur.prev, f32[32,16,256]{2,1,0:T(8,128)S(1)} %get-tuple-element.42.c2, bf16[512,256]{1,0:T(8,128)(2,1)S(1)} %get-tuple-element.43.toeplitz, ...), custom_call_target="tpu_custom_call" | custom-call | flops 7864320 | bytes 5046272 | tf_op jit(solution)/shard_map/pallas_call | solution.py:25
  24.7 1.4 %collective-permute-done.10.refs_2_ = f32[8,8,256]{2,1,0:T(8,128)S(1)} collective-permute-done((f32[8,8,256]{2,1,0:T(8,128)S(1)}, f32[8,8,256]{2,1,0:T(8,128)S(1)}, u32[]{:S(2)}, u32[]{:S(2)}) %collective-permute-start.10) | collective-permute-done | bytes 65568 | tf_op jit(solution)/shard_map/ppermute | solution.py:464
  26.7 1.2 %collective-permute-start.12 = (f32[16,8,256]{2,1,0:T(8,128)S(1)}, f32[16,8,256]{2,1,0:T(8,128)S(1)}, u32[]{:S(2)}, u32[]{:S(2)}) collective-permute-start(f32[16,8,256]{2,1,0:T(8,128)S(1)} %get-tuple-element.65), channel_id=1, source_target_pairs={{4,8},{8,4},{0,12},{12,0},{5,9},{9,5},{1,13},{13,1},{6,10},{10,6},... | collective-permute-start | bytes 393224 | tf_op jit(solution)/shard_map/ppermute | solution.py:463
  27.9 1.5 %collective-permute-start.13 = (f32[8,8,256]{2,1,0:T(8,128)S(1)}, f32[8,8,256]{2,1,0:T(8,128)S(1)}, u32[]{:S(2)}, u32[]{:S(2)}) collective-permute-start(f32[8,8,256]{2,1,0:T(8,128)S(1)} %get-tuple-element.66), channel_id=1, source_target_pairs={{0,16},{16,0},{1,17},{17,1},{2,18},{18,2},{3,19},{19,3},{4,20},{20... | collective-permute-start | bytes 196616 | tf_op jit(solution)/shard_map/ppermute | solution.py:464
  29.4 1.4 %shard_map.119 = (f32[32,16,256]{2,1,0:T(8,128)S(1)}, f32[32,16,256]{2,1,0:T(8,128)S(1)}) custom-call(f32[32,16,256]{2,1,0:T(8,128)S(1)} %get-tuple-element.60.cur.a_in, f32[32,16,256]{2,1,0:T(8,128)S(1)} %get-tuple-element.54.cur.prev, f32[32,16,256]{2,1,0:T(8,128)S(1)} %get-tuple-element.42.c2, bf16[512,256]{1,0:T(8,128)(2,1)S(1)} %get-tuple-element.43.toeplitz, ...), custom_call_target="tpu_custom_call" | custom-call | flops 7864320 | bytes 5046272 | tf_op jit(solution)/shard_map/pallas_call | solution.py:25
  30.8 1.3 %collective-permute-done.13.refs_2_ = f32[8,8,256]{2,1,0:T(8,128)S(1)} collective-permute-done((f32[8,8,256]{2,1,0:T(8,128)S(1)}, f32[8,8,256]{2,1,0:T(8,128)S(1)}, u32[]{:S(2)}, u32[]{:S(2)}) %collective-permute-start.13) | collective-permute-done | bytes 65568 | tf_op jit(solution)/shard_map/ppermute | solution.py:464
  32.6 1.7 %collective-permute-start.14 = (f32[16,8,128]{2,1,0:T(8,128)S(1)}, f32[16,8,128]{2,1,0:T(8,128)S(1)}, u32[]{:S(2)}, u32[]{:S(2)}) collective-permute-start(f32[16,8,128]{2,1,0:T(8,128)S(1)} %get-tuple-element.70), channel_id=1, source_target_pairs={{0,1},{1,0},{2,3},{3,2},{4,5},{5,4},{6,7},{7,6},{8,9},{9,8},{10,11... | collective-permute-start | bytes 196616 | tf_op jit(solution)/shard_map/ppermute | solution.py:491
  34.2 2.7 %collective-permute-done.14 = f32[16,8,128]{2,1,0:T(8,128)S(1)} collective-permute-done((f32[16,8,128]{2,1,0:T(8,128)S(1)}, f32[16,8,128]{2,1,0:T(8,128)S(1)}, u32[]{:S(2)}, u32[]{:S(2)}) %collective-permute-start.14) | collective-permute-done | bytes 65568 | tf_op jit(solution)/shard_map/ppermute | solution.py:491
  36.9 2.7 %collective-permute-start.15 = (f32[16,8,128]{2,1,0:T(8,128)S(1)}, f32[16,8,128]{2,1,0:T(8,128)S(1)}, u32[]{:S(2)}, u32[]{:S(2)}) collective-permute-start(f32[16,8,128]{2,1,0:T(8,128)S(1)} %add.8), channel_id=1, source_target_pairs={{0,2},{1,3},{2,0},{3,1},{4,6},{5,7},{6,4},{7,5},{8,10},{9,11},{10,... | collective-permute-start | bytes 196616 | tf_op jit(solution)/shard_map/ppermute | solution.py:491
  39.6 1.0 %shard_map.121 = (f32[32,16,256]{2,1,0:T(8,128)}, f32[32,16,256]{2,1,0:T(8,128)}) custom-call(f32[32,16,256]{2,1,0:T(8,128)S(1)} %get-tuple-element.60.cur.a_in, f32[32,16,256]{2,1,0:T(8,128)S(1)} %get-tuple-element.67.b_in), custom_call_target="tpu_custom_call" | custom-call | bytes 2097152 | tf_op jit(solution)/shard_map/pallas_call | solution.py:25
  40.6 1.6 %collective-permute-done.15 = f32[16,8,128]{2,1,0:T(8,128)S(1)} collective-permute-done((f32[16,8,128]{2,1,0:T(8,128)S(1)}, f32[16,8,128]{2,1,0:T(8,128)S(1)}, u32[]{:S(2)}, u32[]{:S(2)}) %collective-permute-start.15) | collective-permute-done | bytes 65568 | tf_op jit(solution)/shard_map/ppermute | solution.py:491
  (28 shorter events, 4.1 us)
Async XLA Ops:
  0.6 0.7 %copy-start.1 = (bf16[1,4,64]{2,1,0:T(4,128)(2,1)S(1)}, bf16[1,4,64]{2,1,0:T(4,128)(2,1)}, u32[]{:S(2)}) copy-start(bf16[1,4,64]{2,1,0:T(4,128)(2,1)} %param.13) | copy-start | bytes 1540
  1.3 2.8 %collective-permute-start.2 = (bf16[4,64]{1,0:T(4,128)(2,1)S(1)}, bf16[4,64]{1,0:T(4,128)(2,1)S(1)}, u32[]{:S(2)}, u32[]{:S(2)}) collective-permute-start(bf16[4,64]{1,0:T(4,128)(2,1)S(1)} %bitcast.20), channel_id=1, source_target_pairs={{0,4},{4,0},{8,12},{12,8},{1,5},{5,1},{9,13},{13,9},{2,6},{6,2},{1... | collective-permute-start | bytes 1544 | tf_op jit(solution)/shard_map/ppermute | solution.py:395
  4.1 5.5 %collective-permute-start.3 = (f32[9,8,256]{2,1,0:T(8,128)S(1)}, f32[9,8,256]{2,1,0:T(8,128)S(1)}, u32[]{:S(2)}, u32[]{:S(2)}) collective-permute-start(f32[9,8,256]{2,1,0:T(8,128)S(1)} %maximum_maximum_fusion), channel_id=1, source_target_pairs={{0,16},{16,0},{1,17},{17,1},{2,18},{18,2},{3,19},{19,3},{4,20},{20... | collective-permute-start | bytes 221192 | tf_op jit(solution)/shard_map/ppermute | solution.py:414
  6.7 6.7 %collective-permute-start = (f32[16,8,256]{2,1,0:T(8,128)S(1)}, f32[16,8,256]{2,1,0:T(8,128)S(1)}, u32[]{:S(2)}, u32[]{:S(2)}) collective-permute-start(f32[16,8,256]{2,1,0:T(8,128)S(1)} %get-tuple-element.44), channel_id=1, source_target_pairs={{0,4},{4,0},{8,12},{12,8},{1,5},{5,1},{9,13},{13,9},{2,6},{6,2},{1... | collective-permute-start | bytes 393224 | tf_op jit(solution)/shard_map/ppermute | solution.py:432
  6.9 6.5 %collective-permute-start.1 = (f32[16,8,256]{2,1,0:T(8,128)S(1)}, f32[16,8,256]{2,1,0:T(8,128)S(1)}, u32[]{:S(2)}, u32[]{:S(2)}) collective-permute-start(f32[16,8,256]{2,1,0:T(8,128)S(1)} %get-tuple-element.45), channel_id=1, source_target_pairs={{4,8},{8,4},{0,12},{12,0},{5,9},{9,5},{1,13},{13,1},{6,10},{10,6},... | collective-permute-start | bytes 393224 | tf_op jit(solution)/shard_map/ppermute | solution.py:415
  9.7 3.7 %collective-permute-start.4 = (f32[2,8,256]{2,1,0:T(8,128)S(1)}, f32[2,8,256]{2,1,0:T(8,128)S(1)}, u32[]{:S(2)}, u32[]{:S(2)}) collective-permute-start(f32[2,8,256]{2,1,0:T(8,128)S(1)} %pad_maximum_fusion.refs_3_), channel_id=1, source_target_pairs={{0,8},{4,12},{8,0},{12,4},{1,9},{5,13},{9,1},{13,5},{2,10},{6,14},... | collective-permute-start | bytes 49160 | tf_op jit(solution)/shard_map/ppermute | solution.py:427
  13.4 4.2 %copy-start = (bf16[1,4,32,16,256]{4,3,2,1,0:T(8,128)(2,1)S(1)}, bf16[1,4,32,16,256]{4,3,2,1,0:T(8,128)(2,1)}, u32[]{:S(2)}) copy-start(bf16[1,4,32,16,256]{4,3,2,1,0:T(8,128)(2,1)} %param.11) | copy-start | bytes 3145732
  14.2 6.2 %collective-permute-start.5 = (f32[16,8,256]{2,1,0:T(8,128)S(1)}, f32[16,8,256]{2,1,0:T(8,128)S(1)}, u32[]{:S(2)}, u32[]{:S(2)}) collective-permute-start(f32[16,8,256]{2,1,0:T(8,128)S(1)} %get-tuple-element.51), channel_id=1, source_target_pairs={{0,4},{4,0},{8,12},{12,8},{1,5},{5,1},{9,13},{13,9},{2,6},{6,2},{1... | collective-permute-start | bytes 393224 | tf_op jit(solution)/shard_map/ppermute | solution.py:466
  14.2 6.2 %collective-permute-start.6 = (f32[16,8,256]{2,1,0:T(8,128)S(1)}, f32[16,8,256]{2,1,0:T(8,128)S(1)}, u32[]{:S(2)}, u32[]{:S(2)}) collective-permute-start(f32[16,8,256]{2,1,0:T(8,128)S(1)} %get-tuple-element.52), channel_id=1, source_target_pairs={{4,8},{8,4},{0,12},{12,0},{5,9},{9,5},{1,13},{13,1},{6,10},{10,6},... | collective-permute-start | bytes 393224 | tf_op jit(solution)/shard_map/ppermute | solution.py:463
  16.1 4.3 %collective-permute-start.7 = (f32[8,8,256]{2,1,0:T(8,128)S(1)}, f32[8,8,256]{2,1,0:T(8,128)S(1)}, u32[]{:S(2)}, u32[]{:S(2)}) collective-permute-start(f32[8,8,256]{2,1,0:T(8,128)S(1)} %get-tuple-element.53), channel_id=1, source_target_pairs={{0,16},{16,0},{1,17},{17,1},{2,18},{18,2},{3,19},{19,3},{4,20},{20... | collective-permute-start | bytes 196616 | tf_op jit(solution)/shard_map/ppermute | solution.py:464
  20.6 5.5 %collective-permute-start.8 = (f32[16,8,256]{2,1,0:T(8,128)S(1)}, f32[16,8,256]{2,1,0:T(8,128)S(1)}, u32[]{:S(2)}, u32[]{:S(2)}) collective-permute-start(f32[16,8,256]{2,1,0:T(8,128)S(1)} %get-tuple-element.57), channel_id=1, source_target_pairs={{0,4},{4,0},{8,12},{12,8},{1,5},{5,1},{9,13},{13,9},{2,6},{6,2},{1... | collective-permute-start | bytes 393224 | tf_op jit(solution)/shard_map/ppermute | solution.py:466
  20.7 5.4 %collective-permute-start.9 = (f32[16,8,256]{2,1,0:T(8,128)S(1)}, f32[16,8,256]{2,1,0:T(8,128)S(1)}, u32[]{:S(2)}, u32[]{:S(2)}) collective-permute-start(f32[16,8,256]{2,1,0:T(8,128)S(1)} %get-tuple-element.58), channel_id=1, source_target_pairs={{4,8},{8,4},{0,12},{12,0},{5,9},{9,5},{1,13},{13,1},{6,10},{10,6},... | collective-permute-start | bytes 393224 | tf_op jit(solution)/shard_map/ppermute | solution.py:463
  21.7 4.4 %collective-permute-start.10 = (f32[8,8,256]{2,1,0:T(8,128)S(1)}, f32[8,8,256]{2,1,0:T(8,128)S(1)}, u32[]{:S(2)}, u32[]{:S(2)}) collective-permute-start(f32[8,8,256]{2,1,0:T(8,128)S(1)} %get-tuple-element.59), channel_id=1, source_target_pairs={{0,16},{16,0},{1,17},{17,1},{2,18},{18,2},{3,19},{19,3},{4,20},{20... | collective-permute-start | bytes 196616 | tf_op jit(solution)/shard_map/ppermute | solution.py:464
  26.3 5.9 %collective-permute-start.11 = (f32[16,8,256]{2,1,0:T(8,128)S(1)}, f32[16,8,256]{2,1,0:T(8,128)S(1)}, u32[]{:S(2)}, u32[]{:S(2)}) collective-permute-start(f32[16,8,256]{2,1,0:T(8,128)S(1)} %get-tuple-element.64), channel_id=1, source_target_pairs={{0,4},{4,0},{8,12},{12,8},{1,5},{5,1},{9,13},{13,9},{2,6},{6,2},{1... | collective-permute-start | bytes 393224 | tf_op jit(solution)/shard_map/ppermute | solution.py:466
  26.7 5.5 %collective-permute-start.12 = (f32[16,8,256]{2,1,0:T(8,128)S(1)}, f32[16,8,256]{2,1,0:T(8,128)S(1)}, u32[]{:S(2)}, u32[]{:S(2)}) collective-permute-start(f32[16,8,256]{2,1,0:T(8,128)S(1)} %get-tuple-element.65), channel_id=1, source_target_pairs={{4,8},{8,4},{0,12},{12,0},{5,9},{9,5},{1,13},{13,1},{6,10},{10,6},... | collective-permute-start | bytes 393224 | tf_op jit(solution)/shard_map/ppermute | solution.py:463
  27.9 4.3 %collective-permute-start.13 = (f32[8,8,256]{2,1,0:T(8,128)S(1)}, f32[8,8,256]{2,1,0:T(8,128)S(1)}, u32[]{:S(2)}, u32[]{:S(2)}) collective-permute-start(f32[8,8,256]{2,1,0:T(8,128)S(1)} %get-tuple-element.66), channel_id=1, source_target_pairs={{0,16},{16,0},{1,17},{17,1},{2,18},{18,2},{3,19},{19,3},{4,20},{20... | collective-permute-start | bytes 196616 | tf_op jit(solution)/shard_map/ppermute | solution.py:464
  32.6 4.3 %collective-permute-start.14 = (f32[16,8,128]{2,1,0:T(8,128)S(1)}, f32[16,8,128]{2,1,0:T(8,128)S(1)}, u32[]{:S(2)}, u32[]{:S(2)}) collective-permute-start(f32[16,8,128]{2,1,0:T(8,128)S(1)} %get-tuple-element.70), channel_id=1, source_target_pairs={{0,1},{1,0},{2,3},{3,2},{4,5},{5,4},{6,7},{7,6},{8,9},{9,8},{10,11... | collective-permute-start | bytes 196616 | tf_op jit(solution)/shard_map/ppermute | solution.py:491
  36.9 5.2 %collective-permute-start.15 = (f32[16,8,128]{2,1,0:T(8,128)S(1)}, f32[16,8,128]{2,1,0:T(8,128)S(1)}, u32[]{:S(2)}, u32[]{:S(2)}) collective-permute-start(f32[16,8,128]{2,1,0:T(8,128)S(1)} %add.8), channel_id=1, source_target_pairs={{0,2},{1,3},{2,0},{3,1},{4,6},{5,7},{6,4},{7,5},{8,10},{9,11},{10,... | collective-permute-start | bytes 196616 | tf_op jit(solution)/shard_map/ppermute | solution.py:491
where the time goes:
time: 43 us; the launch traced here: 42.8 us
  starting transfers between devices  19.9 us (46%)
  waiting for transfers between devices  10.3 us (24%)
  Pallas kernels  9.8 us (23%)
  between operations  1.42 us (3%)
  local copies, waits for them, and re-layouts  0.68 us (2%)
  other arithmetic  0.67 us (2%)
    pallas_call x10, Pallas kernels, vmem_call(): pl.pallas_call(kernel, out_shape=tuple(outs), in_specs=in_specs, out_spec...  9.8 us
    ppermute x4, starting transfers between devices, local(): ryo = lax.ppermute(yo, 'gy', odd_pairs(ny)) if with_yo else None  5.49 us
    ppermute x3, starting transfers between devices, local(): rxe = lax.ppermute(xe, 'gx', even_pairs(nx))  4.56 us
    ppermute x2, starting transfers between devices, local(): coarse = coarse + lax.ppermute(coarse, 'shot', xor(nshot, bit))  4.36 us
    ppermute x2, waiting for transfers between devices, local(): coarse = coarse + lax.ppermute(coarse, 'shot', xor(nshot, bit))  4.21 us
    ppermute x3, waiting for transfers between devices, local(): rxe = lax.ppermute(xe, 'gx', even_pairs(nx))  4 us
    ppermute x1, starting transfers between devices, local(): lax.ppermute(jnp.concatenate([xe, pair], axis=0), 'gx', even_pairs(nx))  2.57 us
    ppermute x1, starting transfers between devices, local(): got = lax.ppermute(now, axis, xor(size, bit))  1.71 us
  transfers between devices with their start and end apart: 16, of which 7 were waited for; matrix products, arithmetic and copies ran while one was open for 0% of the time, Pallas kernels for 19%

commit v1 on v0

--- a/solution.py
+++ b/solution.py
@@ -10,6 +10,7 @@
 
 LAPLACE_COEFS = (-205.0 / 72.0, 8.0 / 5.0, -1.0 / 5.0, 8.0 / 315.0, -1.0 / 560.0)
 REACH = 4
+CHUNK = 8
 VMEM_LIMIT = 16 << 20
 F32 = jnp.float32
 BF16 = jnp.bfloat16
@@ -46,11 +47,20 @@
     return pairs
 
 
-def odd_pairs(n):
+def odd_swap(x, axis):
+    n, shots = lax.axis_size(axis), lax.axis_size("shot")
+    if shots % 2:
+        pairs = [(0, n - 1), (n - 1, 0)]
+        for i in range(1, n - 1, 2):
+            pairs += [(i, i + 1), (i + 1, i)]
+        return lax.ppermute(x, axis, pairs)
     pairs = []
-    for i in range(1, n - 1, 2):
-        pairs += [(i, i + 1), (i + 1, i)]
-    return pairs + [(0, n - 1), (n - 1, 0)]
+    for s in range(shots):
+        for i in (0, n - 1):
+            pairs.append((i * shots + s, i * shots + (s ^ 1)))
+        for i in range(1, n - 1, 2):
+            pairs += [(i * shots + s, (i + 1) * shots + s), ((i + 1) * shots + s, i * shots + s)]
+    return lax.ppermute(x, (axis, "shot"), pairs)
 
 
 def split2(v):
@@ -160,16 +170,11 @@
 
 
 def load_kernel(
-    cur_in, prev_in, c2_in, weights_in, traces_in, col_in, rb_in, counts,
-    cur, prev, c2, weights, ye, yo, xe, own, toeplitz, select, owners,
-    traces, col, rb, sems,
+    cur_in, col_in, rb_in, traces_in, counts, cur, ye, yo, xe, toeplitz, select, owners, own, col, rb, traces, sems,
     *, with_yo, each, rblk,
 ):
     gx_index, gy_index = lax.axis_index("gx"), lax.axis_index("gy")
-    me = gx_index * lax.axis_size("gy") + gy_index
-    pairs = (
-        (cur_in, cur), (col_in, col), (rb_in, rb), (traces_in, traces), (prev_in, prev), (c2_in, c2), (weights_in, weights),
-    )
+    pairs = ((cur_in, cur), (col_in, col), (rb_in, rb), (traces_in, traces))
     copies = [pltpu.make_async_copy(src, dst, sems.at[i]) for i, (src, dst) in enumerate(pairs)]
     for copy in copies:
         copy.start()
@@ -183,27 +188,30 @@
     hi, lo = split2(band)
     toeplitz[0:nz, :] = hi
     toeplitz[nz : 2 * nz, :] = lo
-    for copy in copies[1:4]:
+    for copy in copies[1:]:
         copy.wait()
     wide = jnp.concatenate([col[...]] * 3, axis=1)
     rows = lax.broadcasted_iota(jnp.int32, select.shape, 0)
     select[...] = jnp.where(rows == wide, 1.0, 0.0).astype(BF16)
+    slot_owners(rb, counts, owners, each, rblk)
+    steps, per = traces.shape[1:]
+    own[...] = jnp.zeros(own.shape, F32)
+    own[0, 0:steps, 0:per] = traces[0].astype(F32)
+    copies[0].wait()
+    put_faces(cur, gx_index, gy_index, ye, yo if with_yo else None, xe, None)
+
+
+def slot_owners(rb, counts, owners, each, rblk):
+    me = lax.axis_index("gx") * lax.axis_size("gy") + lax.axis_index("gy")
     slots, lanes = owners.shape
     eye = lax.broadcasted_iota(jnp.int32, (slots, slots), 0) == lax.broadcasted_iota(jnp.int32, (slots, slots), 1)
     block_of = jnp.sum(jnp.where(eye, jnp.broadcast_to(rb[...], (slots, slots)), 0), axis=1, keepdims=True)
     owner = lax.div(block_of, jnp.int32(each))
     group = block_of - owner * each
-    slot = lax.broadcasted_iota(jnp.int32, (slots, lanes), 0)
     lane = lax.broadcasted_iota(jnp.int32, (slots, lanes), 1)
-    used = jnp.logical_and(slot < counts[0, 0], lax.div(lane, jnp.int32(rblk)) == group)
+    live = lax.broadcasted_iota(jnp.int32, (slots, lanes), 0) < counts[0, 0]
+    used = jnp.logical_and(live, lax.div(lane, jnp.int32(rblk)) == group)
     owners[...] = jnp.where(used, jnp.bitwise_xor(owner, me), -1)
-    steps, per = traces.shape
-    own[...] = jnp.zeros(own.shape, F32)
-    own[0, 0:steps, 0:per] = traces[...].astype(F32)
-    copies[0].wait()
-    put_faces(cur, gx_index, gy_index, ye, yo if with_yo else None, xe, None)
-    for copy in copies[4:]:
-        copy.wait()
 
 
 def flush_kernel(a_in, b_in, a_out, b_out, sems):
@@ -224,7 +232,7 @@
         ypad[x, 0:8, :] = zero
         ypad[x, 8 : 8 + cy, :] = cur[x, :, :]
         ypad[x, 8 + cy : 16 + cy, :] = zero
-    chunk = 8
+    chunk = CHUNK
     rows = chunk * cy
     t_hi = toeplitz[0:nz, :]
     t_lo = toeplitz[nz : 2 * nz, :]
@@ -245,6 +253,9 @@
                 if x + k < cx:
                     pair = pair + cur[x + k, :, :]
                 total = total + w[k] * pair
+            if prev is None:
+                out[x, :, :] = total
+                continue
             here = cur[x, :, :]
             value = (2.0 * here - prev[x, :, :]) + c2[x, :, :] * total
             if source is not None:
@@ -256,8 +267,19 @@
                 fine_out[x, :, :] = term if fine_in is None else fine_in[x, :, :] + term
 
 
-def first_update_kernel(cur, prev, c2, toeplitz, out, ypad):
-    update(cur, prev, c2, toeplitz, out, ypad)
+def first_update_kernel(cur, toeplitz, prev_in, c2_in, weights_in, out, prev, c2, weights, ypad, sems):
+    copies = [
+        pltpu.make_async_copy(src, dst, sems.at[i])
+        for i, (src, dst) in enumerate(((prev_in, prev), (c2_in, c2), (weights_in, weights)))
+    ]
+    for copy in copies:
+        copy.start()
+    update(cur, None, None, toeplitz, out, ypad)
+    copies[0].wait()
+    copies[1].wait()
+    for x in range(cur.shape[0]):
+        out[x, :, :] = (2.0 * cur[x, :, :] - prev[x, :, :]) + c2[x, :, :] * out[x, :, :]
+    copies[2].wait()
 
 
 def update_kernel(cur, prev, c2, toeplitz, select, contrib, accel, *rest, step):
@@ -315,18 +337,20 @@
     return ye, yo, xe, xo, refs
 
 
-def first_correct_kernel(owners, weights, select, part, c2, *refs, with_yo, with_xo, holds, patterns):
+def first_correct_kernel(owners, weights, select, part, c2, *refs, with_yo, with_xo, patterns):
     gx_index, gy_index = lax.axis_index("gx"), lax.axis_index("gy")
     ye, yo, xe, xo, refs = unpack(refs, with_yo, with_xo)
-    held, refs = refs[:holds], refs[holds:]
+    pairs, refs = refs[0], refs[1:]
     nxt, contrib, refs = refs[0], refs[1], refs[2:]
     oye, oyo, oxe, oxo, refs = unpack(refs, with_yo, with_xo)
     wide = refs[0]
     lanes = 128
     tiles = []
-    for ref in held:
-        for i in range(ref.shape[0]):
-            tiles += [ref[i][:, 0:lanes], ref[i][:, lanes : 2 * lanes]]
+    n = pairs.shape[0]
+    y_last, x_last = ye.shape[0] - n, xe.shape[0] - 2 * n
+    for ref, first in ((pairs, 0), (ye, y_last), (xe, x_last), (xe, x_last + n)):
+        for i in range(n):
+            tiles += [ref[first + i][:, 0:lanes], ref[first + i][:, lanes : 2 * lanes]]
     contributions(owners, weights, tiles, patterns, contrib, wide)
     cx, cy, nz = nxt.shape
     chunk = 8
@@ -389,50 +413,59 @@
     cells = cx * cy * nz
     lanes = 128
 
+    def swap(x, axis, pairs=None):
+        return odd_swap(x, axis) if pairs is None else lax.ppermute(x, axis, pairs)
+
     def xor(size, bit):
         return [(i, i ^ bit) for i in range(size)]
 
-    theirs = lax.ppermute(traces[0], "gy", even_pairs(ny))
-    cur, prev, c2, wts, ye, yo, xe, own, toeplitz, select, owners = vmem_call(
+    blocks, others, patterns = traces, [], [0]
+    for axis, size, stride in (("gy", ny, 1), ("gx", nx, ny)):
+        bit = 2
+        while bit < size:
+            got = swap(blocks, axis, xor(size, bit))
+            others.append(got)
+            patterns = patterns + [p ^ (bit * stride) for p in patterns]
+            bit *= 2
+            if bit < size or (axis == "gy" and nx > 2):
+                blocks = jnp.concatenate([blocks, got], axis=0)
+    if not others:
+        others, patterns = [jnp.zeros_like(traces)], [0, -2]
+    cur, ye, yo, xe, toeplitz, select, owners, own = vmem_call(
         functools.partial(load_kernel, with_yo=with_yo, each=per // rblk, rblk=rblk),
         [
-            sds(tile), sds(tile), sds(tile), sds((slots, rblk, nz), BF16),
-            sds(y_msg), sds(y_msg), sds(x_msg), sds((1, 8, lanes)),
-            sds((2 * nz, nz), BF16), sds((cx * cy, 3 * slots), BF16), sds((slots, lanes), jnp.int32),
+            sds(tile), sds(y_msg), sds(y_msg), sds(x_msg), sds((2 * nz, nz), BF16),
+            sds((cx * cy, 3 * slots), BF16), sds((slots, lanes), jnp.int32), sds((1, 8, lanes)),
         ],
-            [adj_cur[0], adj_prev[0], courant2, weights[0, 0], traces[0], column[0], rblock[0], counts],
+        [adj_cur[0], column[0], rblock[0], traces, counts],
         [
-            pltpu.VMEM((steps, per), BF16), pltpu.VMEM((1, slots), jnp.int32), pltpu.VMEM((1, slots), jnp.int32),
-            pltpu.SemaphoreType.DMA((7,)),
+            pltpu.VMEM((1, slots), jnp.int32), pltpu.VMEM((1, slots), jnp.int32), pltpu.VMEM((1, steps, per), BF16),
+            pltpu.SemaphoreType.DMA((4,)),
         ],
-        hbm_in=tuple(range(7)),
-        smem_in=(7,),
-    )
-
-    theirs = jnp.pad(theirs.astype(F32), ((0, 8 - steps), (0, lanes - per)))[None]
-    pair = jnp.concatenate([own, theirs], axis=2)
-    rxe = lax.ppermute(jnp.concatenate([xe, pair], axis=0), "gx", even_pairs(nx))
-    ryo = lax.ppermute(yo, "gy", odd_pairs(ny)) if with_yo else None
+        hbm_in=(0, 1, 2, 3), smem_in=(4,),
+    )
+    others = [jnp.pad(a.astype(F32), ((0, 0), (0, 8 - steps), (0, lanes - per))) for a in others]
+    tiles = jnp.concatenate([own] + others, axis=0)
+    pairs = jnp.concatenate([tiles[0::2], tiles[1::2]], axis=2)
+    rye = swap(jnp.concatenate([ye, pairs], axis=0), "gy", even_pairs(ny))
+    ryo = swap(yo, "gy") if with_yo else None
     rxo = None
     if with_xo:
         low = cur[0:REACH].reshape(x_msg)
         high = cur[cx - REACH :].reshape(x_msg)
-        rxo = lax.ppermute(jnp.where(lax.axis_index("gx") % 2 == 0, low, high), "gx", odd_pairs(nx))
-    patterns = [0, 1, ny, ny + 1]
-    now = jnp.concatenate([pair, rxe[x_msg[0] :]], axis=0)
-    held = [now]
-    for axis, size, stride in (("gy", ny, 1), ("gx", nx, ny)):
-        bit = 2
-        while bit < size:
-            got = lax.ppermute(now, axis, xor(size, bit))
-            held.append(got)
-            patterns = patterns + [p ^ (bit * stride) for p in patterns]
-            bit *= 2
-            now = jnp.concatenate([now, got], axis=0)
-    rye = lax.ppermute(ye, "gy", even_pairs(ny))
+        rxo = swap(jnp.where(lax.axis_index("gx") % 2 == 0, low, high), "gx")
+    rxe = swap(jnp.concatenate([xe, pairs, rye[y_msg[0] :]], axis=0), "gx", even_pairs(nx))
+    for stride in (1, ny):
+        patterns = patterns + [p ^ stride if p >= 0 else p for p in patterns]
 
     ypad = pltpu.VMEM((cx, cy + 16, nz), F32)
-    part = vmem_call(first_update_kernel, [sds(tile)], [cur, prev, c2, toeplitz], [ypad], flops=cells * 60)[0]
+    part, _, c2, wts = vmem_call(
+        first_update_kernel,
+        [sds(tile), sds(tile), sds(tile), sds((slots, rblk, nz), BF16)],
+        [cur, toeplitz, adj_prev[0], courant2, weights[0, 0]],
+        [ypad, pltpu.SemaphoreType.DMA((3,))],
+        hbm_in=(2, 3, 4), flops=cells * 60,
+    )
 
     def given(ye, yo, xe, xo):
         return [a for a in (ye, yo, xe, xo) if a is not None]
@@ -450,20 +483,20 @@
 
     nxt, contrib, *faces = vmem_call(
         functools.partial(
-            first_correct_kernel, with_yo=with_yo, with_xo=with_xo, holds=len(held), patterns=tuple(patterns)
+            first_correct_kernel, with_yo=with_yo, with_xo=with_xo, patterns=tuple(patterns)
         ),
         [sds(tile), sds((steps, 3 * slots, nz), BF16)] + face_shapes(),
-        [owners, wts, select, part, c2] + given(rye, ryo, rxe, rxo) + held,
+        [owners, wts, select, part, c2] + given(rye, ryo, rxe, rxo) + [pairs],
         [pltpu.VMEM((steps, slots, nz), F32)],
     )
     previous, current = cur, nxt
     fine = None
     for step in range(1, steps):
         ye, yo, xe, xo = taken(faces)
-        ryo = lax.ppermute(yo, "gy", odd_pairs(ny)) if with_yo else None
-        rxe = lax.ppermute(xe, "gx", even_pairs(nx))
-        rxo = lax.ppermute(xo, "gx", odd_pairs(nx)) if with_xo else None
-        rye = lax.ppermute(ye, "gy", even_pairs(ny))
+        ryo = swap(yo, "gy") if with_yo else None
+        rxe = swap(xe, "gx", even_pairs(nx))
+        rxo = swap(xo, "gx") if with_xo else None
+        rye = swap(ye, "gy", even_pairs(ny))
         args = [current, previous, c2, toeplitz, select, contrib, accel]
         if fine is not None:
             args.append(fine)
@@ -488,7 +521,7 @@
         previous, current = current, nxt
     bit = 1
     while bit < nshot:
-        coarse = coarse + lax.ppermute(coarse, "shot", xor(nshot, bit))
+        coarse = coarse + swap(coarse, "shot", xor(nshot, bit))
         bit *= 2
     previous, current = vmem_call(
         flush_kernel, [sds(tile), sds(tile)], [previous, current], [pltpu.SemaphoreType.DMA((2,))],

time: 43 us -> 43.3 us (level)
  waiting for transfers between devices: 10.3 us -> 11.5 us
  local copies, waits for them, and re-layouts: 0.68 us -> 0.01 us
    ppermute x16 -> x15, waiting for transfers between devices: 10.3 us -> 11.5 us  [the longest x11 11.5 us: swap(): return odd_swap(x, axis) if pairs is None else lax.ppermute(x, axis, pairs)]
    unnamed x4 -> x2, local copies, waits for them, and re-layouts: 0.68 us -> 0.01 us
    ppermute x16 -> x15, starting transfers between devices: 19.9 us -> 19.5 us  [the longest x11 14.5 us: swap(): return odd_swap(x, axis) if pairs is None else lax.ppermute(x, axis, pairs)]
  transfers between devices with their start and end apart: 16 -> 15, of which waited for: 7 -> 6; matrix products, arithmetic and copies ran while one was open for 0% -> 0% of each run, Pallas kernels for 19% -> 20%
where the time goes in v1:
time: 43.3 us; the launch traced here: 43.2 us
  starting transfers between devices  19.5 us (45%)
  waiting for transfers between devices  11.5 us (27%)
  Pallas kernels  10.1 us (23%)
  between operations  1.44 us (3%)
  other arithmetic  0.68 us (2%)
    ppermute x11, starting transfers between devices, swap(): return odd_swap(x, axis) if pairs is None else lax.ppermute(x, axis, pairs)  14.5 us
    ppermute x11, waiting for transfers between devices, swap(): return odd_swap(x, axis) if pairs is None else lax.ppermute(x, axis, pairs)  11.5 us
    pallas_call x10, Pallas kernels, vmem_call(): pl.pallas_call(kernel, out_shape=tuple(outs), in_specs=in_specs, out_spec...  10.1 us
    ppermute x4, starting transfers between devices, odd_swap(): return lax.ppermute(x, (axis, 'shot'), pairs)  4.98 us
  transfers between devices with their start and end apart: 15, of which 6 were waited for; matrix products, arithmetic and copies ran while one was open for 0% of the time, Pallas kernels for 20%

profile of v1, /device:TPU:0, one launch (start us, length us, event | category | flops | bytes accessed | tf_op | source)
XLA Modules:
  0.0 43.2 jit_solution(9160189161856566980)
XLA Ops:
  0.6 3.0 %collective-permute-start = (bf16[1,4,64]{2,1,0:T(4,128)(2,1)}, bf16[1,4,64]{2,1,0:T(4,128)(2,1)S(1)}, u32[]{:S(2)}, u32[]{:S(2)}) collective-permute-start(bf16[1,4,64]{2,1,0:T(4,128)(2,1)} %traces_in.1), channel_id=1, source_target_pairs={{0,8},{4,12},{8,0},{12,4},{1,9},{5,13},{9,1},{13,5},{2,10},{6,14},... | collective-permute-start | bytes 1544 | tf_op jit(solution)/shard_map/ppermute | solution.py:417
  4.3 1.2 %shard_map.112 = (f32[32,16,256]{2,1,0:T(8,128)S(1)}, f32[16,8,256]{2,1,0:T(8,128)S(1)}, f32[16,8,256]{2,1,0:T(8,128)S(1)}, f32[8,8,256]{2,1,0:T(8,128)S(1)}, bf...) custom-call(f32[32,16,256]{2,1,0:T(8,128)} %bitcast.12, ...), custom_call_target="tpu_custom_call" | custom-call | bytes 1872900 | tf_op jit(solution)/shard_map/pallas_call | solution.py:26
  5.6 2.1 %collective-permute-start.2 = (f32[16,8,256]{2,1,0:T(8,128)S(1)}, f32[16,8,256]{2,1,0:T(8,128)S(1)}, u32[]{:S(2)}, u32[]{:S(2)}) collective-permute-start(f32[16,8,256]{2,1,0:T(8,128)S(1)} %get-tuple-element.46), channel_id=1, source_target_pairs={{0,1},{12,13},{4,8},{8,4},{1,0},{13,12},{5,9},{9,5},{2,3},{14,15},... | collective-permute-start | bytes 393224 | tf_op jit(solution)/shard_map/ppermute | solution.py:63
  7.7 2.2 %shard_map.113 = (f32[32,16,256]{2,1,0:T(8,128)S(1)}, f32[32,16,256]{2,1,0:T(8,128)}, f32[32,16,256]{2,1,0:T(8,128)S(1)}, bf16[64,16,256]{2,1,0:T(8,128)(2,1)S(1)}) custom-call(f32[32,16,256]{2,1,0:T(8,128)S(1)} %get-tuple-element.38.cur.prev, bf16[512,256]{1,0:T(8,128)(2,1)S(1)} %get-tuple-element.39.toeplitz, f32[32,16,256]{2,1,0:T(8,128)} %bitcast.13, ...), custom_call_target="tpu_custom_call" | custom-call | flops 7864320 | bytes 4456448 | tf_op jit(solution)/shard_map/pallas_call | solution.py:26
  10.0 1.6 %collective-permute-start.3 = (f32[10,8,256]{2,1,0:T(8,128)S(1)}, f32[10,8,256]{2,1,0:T(8,128)S(1)}, u32[]{:S(2)}, u32[]{:S(2)}) collective-permute-start(f32[10,8,256]{2,1,0:T(8,128)S(1)} %pad_maximum_fusion), channel_id=1, source_target_pairs={{0,16},{16,0},{1,17},{17,1},{2,18},{18,2},{3,19},{19,3},{4,20},{20... | collective-permute-start | bytes 245768 | tf_op jit(solution)/shard_map/ppermute | solution.py:417
  11.5 2.9 %collective-permute-done.3.refs_2_ = f32[10,8,256]{2,1,0:T(8,128)S(1)} collective-permute-done((f32[10,8,256]{2,1,0:T(8,128)S(1)}, f32[10,8,256]{2,1,0:T(8,128)S(1)}, u32[]{:S(2)}, u32[]{:S(2)}) %collective-permute-start.3) | collective-permute-done | bytes 81952 | tf_op jit(solution)/shard_map/ppermute | solution.py:417
  14.5 0.7 %shard_map.114 = (f32[32,16,256]{2,1,0:T(8,128)S(1)}, bf16[4,192,256]{2,1,0:T(8,128)(2,1)S(1)}, f32[16,8,256]{2,1,0:T(8,128)S(1)}, f32[16,8,256]{2,1,0:T(8,128)S(1)}, f32[8,8,256]{2,1,0:T(8,128)S(1)}) custom-call(s32[64,128]{1,0:T(8,128)S(1)} %get-tuple-element.37.owners, bf16[64,16,256]{2,1,0:T(8,128)(2,1)S(1)} %get-tuple-element.40.weights, ...), custom_call_target="tpu_custom_call" | custom-call | bytes 3407872 | tf_op jit(solution)/shard_map/pallas_call | solution.py:26
  15.3 0.8 %collective-permute-start.5 = (f32[16,8,256]{2,1,0:T(8,128)S(1)}, f32[16,8,256]{2,1,0:T(8,128)S(1)}, u32[]{:S(2)}, u32[]{:S(2)}) collective-permute-start(f32[16,8,256]{2,1,0:T(8,128)S(1)} %get-tuple-element.52), channel_id=1, source_target_pairs={{0,1},{12,13},{4,8},{8,4},{1,0},{13,12},{5,9},{9,5},{2,3},{14,15},... | collective-permute-start | bytes 393224 | tf_op jit(solution)/shard_map/ppermute | solution.py:63
  16.1 2.1 %collective-permute-start.6 = (f32[8,8,256]{2,1,0:T(8,128)S(1)}, f32[8,8,256]{2,1,0:T(8,128)S(1)}, u32[]{:S(2)}, u32[]{:S(2)}) collective-permute-start(f32[8,8,256]{2,1,0:T(8,128)S(1)} %get-tuple-element.53), channel_id=1, source_target_pairs={{0,16},{16,0},{1,17},{17,1},{2,18},{18,2},{3,19},{19,3},{4,20},{20... | collective-permute-start | bytes 196616 | tf_op jit(solution)/shard_map/ppermute | solution.py:417
  18.1 1.4 %shard_map.115 = (f32[32,16,256]{2,1,0:T(8,128)S(1)}, f32[32,16,256]{2,1,0:T(8,128)S(1)}) custom-call(f32[32,16,256]{2,1,0:T(8,128)S(1)} %get-tuple-element.48.cur.prev, f32[32,16,256]{2,1,0:T(8,128)S(1)} %get-tuple-element.38.cur.prev, f32[32,16,256]{2,1,0:T(8,128)S(1)} %get-tuple-element.43.c2, bf16[512,256]{1,0:T(8,128)(2,1)S(1)} %get-tuple-element.39.toeplitz, ...), custom_call_target="tpu_custom_call" | custom-call | flops 7864320 | bytes 4521984 | tf_op jit(solution)/shard_map/pallas_call | solution.py:26
  19.5 1.0 %collective-permute-done.6.refs_2_ = f32[8,8,256]{2,1,0:T(8,128)S(1)} collective-permute-done((f32[8,8,256]{2,1,0:T(8,128)S(1)}, f32[8,8,256]{2,1,0:T(8,128)S(1)}, u32[]{:S(2)}, u32[]{:S(2)}) %collective-permute-start.6) | collective-permute-done | bytes 65568 | tf_op jit(solution)/shard_map/ppermute | solution.py:417
  20.8 1.2 %collective-permute-start.8 = (f32[16,8,256]{2,1,0:T(8,128)S(1)}, f32[16,8,256]{2,1,0:T(8,128)S(1)}, u32[]{:S(2)}, u32[]{:S(2)}) collective-permute-start(f32[16,8,256]{2,1,0:T(8,128)S(1)} %get-tuple-element.58), channel_id=1, source_target_pairs={{0,1},{12,13},{4,8},{8,4},{1,0},{13,12},{5,9},{9,5},{2,3},{14,15},... | collective-permute-start | bytes 393224 | tf_op jit(solution)/shard_map/ppermute | solution.py:63
  22.0 1.5 %collective-permute-start.9 = (f32[8,8,256]{2,1,0:T(8,128)S(1)}, f32[8,8,256]{2,1,0:T(8,128)S(1)}, u32[]{:S(2)}, u32[]{:S(2)}) collective-permute-start(f32[8,8,256]{2,1,0:T(8,128)S(1)} %get-tuple-element.59), channel_id=1, source_target_pairs={{0,16},{16,0},{1,17},{17,1},{2,18},{18,2},{3,19},{19,3},{4,20},{20... | collective-permute-start | bytes 196616 | tf_op jit(solution)/shard_map/ppermute | solution.py:417
  23.5 1.4 %shard_map.117 = (f32[32,16,256]{2,1,0:T(8,128)S(1)}, f32[32,16,256]{2,1,0:T(8,128)S(1)}) custom-call(f32[32,16,256]{2,1,0:T(8,128)S(1)} %get-tuple-element.54.cur.prev, f32[32,16,256]{2,1,0:T(8,128)S(1)} %get-tuple-element.48.cur.prev, f32[32,16,256]{2,1,0:T(8,128)S(1)} %get-tuple-element.43.c2, bf16[512,256]{1,0:T(8,128)(2,1)S(1)} %get-tuple-element.39.toeplitz, ...), custom_call_target="tpu_custom_call" | custom-call | flops 7864320 | bytes 5046272 | tf_op jit(solution)/shard_map/pallas_call | solution.py:26
  24.9 1.3 %collective-permute-done.9.refs_2_ = f32[8,8,256]{2,1,0:T(8,128)S(1)} collective-permute-done((f32[8,8,256]{2,1,0:T(8,128)S(1)}, f32[8,8,256]{2,1,0:T(8,128)S(1)}, u32[]{:S(2)}, u32[]{:S(2)}) %collective-permute-start.9) | collective-permute-done | bytes 65568 | tf_op jit(solution)/shard_map/ppermute | solution.py:417
  26.6 0.9 %collective-permute-start.11 = (f32[16,8,256]{2,1,0:T(8,128)S(1)}, f32[16,8,256]{2,1,0:T(8,128)S(1)}, u32[]{:S(2)}, u32[]{:S(2)}) collective-permute-start(f32[16,8,256]{2,1,0:T(8,128)S(1)} %get-tuple-element.65), channel_id=1, source_target_pairs={{0,1},{12,13},{4,8},{8,4},{1,0},{13,12},{5,9},{9,5},{2,3},{14,15},... | collective-permute-start | bytes 393224 | tf_op jit(solution)/shard_map/ppermute | solution.py:63
  27.5 1.9 %collective-permute-start.12 = (f32[8,8,256]{2,1,0:T(8,128)S(1)}, f32[8,8,256]{2,1,0:T(8,128)S(1)}, u32[]{:S(2)}, u32[]{:S(2)}) collective-permute-start(f32[8,8,256]{2,1,0:T(8,128)S(1)} %get-tuple-element.66), channel_id=1, source_target_pairs={{0,16},{16,0},{1,17},{17,1},{2,18},{18,2},{3,19},{19,3},{4,20},{20... | collective-permute-start | bytes 196616 | tf_op jit(solution)/shard_map/ppermute | solution.py:417
  29.4 1.4 %shard_map.119 = (f32[32,16,256]{2,1,0:T(8,128)S(1)}, f32[32,16,256]{2,1,0:T(8,128)S(1)}) custom-call(f32[32,16,256]{2,1,0:T(8,128)S(1)} %get-tuple-element.60.cur.a_in, f32[32,16,256]{2,1,0:T(8,128)S(1)} %get-tuple-element.54.cur.prev, f32[32,16,256]{2,1,0:T(8,128)S(1)} %get-tuple-element.43.c2, bf16[512,256]{1,0:T(8,128)(2,1)S(1)} %get-tuple-element.39.toeplitz, ...), custom_call_target="tpu_custom_call" | custom-call | flops 7864320 | bytes 5046272 | tf_op jit(solution)/shard_map/pallas_call | solution.py:26
  30.8 1.1 %collective-permute-done.12.refs_2_ = f32[8,8,256]{2,1,0:T(8,128)S(1)} collective-permute-done((f32[8,8,256]{2,1,0:T(8,128)S(1)}, f32[8,8,256]{2,1,0:T(8,128)S(1)}, u32[]{:S(2)}, u32[]{:S(2)}) %collective-permute-start.12) | collective-permute-done | bytes 65568 | tf_op jit(solution)/shard_map/ppermute | solution.py:417
  32.3 1.1 %collective-permute-start.13 = (f32[16,8,128]{2,1,0:T(8,128)S(1)}, f32[16,8,128]{2,1,0:T(8,128)S(1)}, u32[]{:S(2)}, u32[]{:S(2)}) collective-permute-start(f32[16,8,128]{2,1,0:T(8,128)S(1)} %get-tuple-element.70), channel_id=1, source_target_pairs={{0,1},{1,0},{2,3},{3,2},{4,5},{5,4},{6,7},{7,6},{8,9},{9,8},{10,11... | collective-permute-start | bytes 196616 | tf_op jit(solution)/shard_map/ppermute | solution.py:417
  33.4 3.2 %collective-permute-done.13 = f32[16,8,128]{2,1,0:T(8,128)S(1)} collective-permute-done((f32[16,8,128]{2,1,0:T(8,128)S(1)}, f32[16,8,128]{2,1,0:T(8,128)S(1)}, u32[]{:S(2)}, u32[]{:S(2)}) %collective-permute-start.13) | collective-permute-done | bytes 65568 | tf_op jit(solution)/shard_map/ppermute | solution.py:417
  36.6 2.9 %collective-permute-start.14 = (f32[16,8,128]{2,1,0:T(8,128)S(1)}, f32[16,8,128]{2,1,0:T(8,128)S(1)}, u32[]{:S(2)}, u32[]{:S(2)}) collective-permute-start(f32[16,8,128]{2,1,0:T(8,128)S(1)} %add.8), channel_id=1, source_target_pairs={{0,2},{1,3},{2,0},{3,1},{4,6},{5,7},{6,4},{7,5},{8,10},{9,11},{10,... | collective-permute-start | bytes 196616 | tf_op jit(solution)/shard_map/ppermute | solution.py:417
  39.5 1.0 %shard_map.121 = (f32[32,16,256]{2,1,0:T(8,128)}, f32[32,16,256]{2,1,0:T(8,128)}) custom-call(f32[32,16,256]{2,1,0:T(8,128)S(1)} %get-tuple-element.60.cur.a_in, f32[32,16,256]{2,1,0:T(8,128)S(1)} %get-tuple-element.67.b_in), custom_call_target="tpu_custom_call" | custom-call | bytes 2097152 | tf_op jit(solution)/shard_map/pallas_call | solution.py:26
  40.5 2.0 %collective-permute-done.14 = f32[16,8,128]{2,1,0:T(8,128)S(1)} collective-permute-done((f32[16,8,128]{2,1,0:T(8,128)S(1)}, f32[16,8,128]{2,1,0:T(8,128)S(1)}, u32[]{:S(2)}, u32[]{:S(2)}) %collective-permute-start.14) | collective-permute-done | bytes 65568 | tf_op jit(solution)/shard_map/ppermute | solution.py:417
  (25 shorter events, 1.8 us)
Async XLA Ops:
  0.6 4.8 %collective-permute-start = (bf16[1,4,64]{2,1,0:T(4,128)(2,1)}, bf16[1,4,64]{2,1,0:T(4,128)(2,1)S(1)}, u32[]{:S(2)}, u32[]{:S(2)}) collective-permute-start(bf16[1,4,64]{2,1,0:T(4,128)(2,1)} %traces_in.1), channel_id=1, source_target_pairs={{0,8},{4,12},{8,0},{12,4},{1,9},{5,13},{9,1},{13,5},{2,10},{6,14},... | collective-permute-start | bytes 1544 | tf_op jit(solution)/shard_map/ppermute | solution.py:417
  5.5 4.4 %collective-permute-start.1 = (f32[17,8,256]{2,1,0:T(8,128)S(1)}, f32[17,8,256]{2,1,0:T(8,128)S(1)}, u32[]{:S(2)}, u32[]{:S(2)}) collective-permute-start(f32[17,8,256]{2,1,0:T(8,128)S(1)} %maximum_maximum_fusion), channel_id=1, source_target_pairs={{0,4},{4,0},{8,12},{12,8},{1,5},{5,1},{9,13},{13,9},{2,6},{6,2},{1... | collective-permute-start | bytes 417800 | tf_op jit(solution)/shard_map/ppermute | solution.py:417
  5.6 5.9 %collective-permute-start.2 = (f32[16,8,256]{2,1,0:T(8,128)S(1)}, f32[16,8,256]{2,1,0:T(8,128)S(1)}, u32[]{:S(2)}, u32[]{:S(2)}) collective-permute-start(f32[16,8,256]{2,1,0:T(8,128)S(1)} %get-tuple-element.46), channel_id=1, source_target_pairs={{0,1},{12,13},{4,8},{8,4},{1,0},{13,12},{5,9},{9,5},{2,3},{14,15},... | collective-permute-start | bytes 393224 | tf_op jit(solution)/shard_map/ppermute | solution.py:63
  10.0 4.5 %collective-permute-start.3 = (f32[10,8,256]{2,1,0:T(8,128)S(1)}, f32[10,8,256]{2,1,0:T(8,128)S(1)}, u32[]{:S(2)}, u32[]{:S(2)}) collective-permute-start(f32[10,8,256]{2,1,0:T(8,128)S(1)} %pad_maximum_fusion), channel_id=1, source_target_pairs={{0,16},{16,0},{1,17},{17,1},{2,18},{18,2},{3,19},{19,3},{4,20},{20... | collective-permute-start | bytes 245768 | tf_op jit(solution)/shard_map/ppermute | solution.py:417
  14.5 3.6 %copy-start = (bf16[1,4,32,16,256]{4,3,2,1,0:T(8,128)(2,1)S(1)}, bf16[1,4,32,16,256]{4,3,2,1,0:T(8,128)(2,1)}, u32[]{:S(2)}) copy-start(bf16[1,4,32,16,256]{4,3,2,1,0:T(8,128)(2,1)} %param.11) | copy-start | bytes 3145732
  15.2 5.3 %collective-permute-start.4 = (f32[16,8,256]{2,1,0:T(8,128)S(1)}, f32[16,8,256]{2,1,0:T(8,128)S(1)}, u32[]{:S(2)}, u32[]{:S(2)}) collective-permute-start(f32[16,8,256]{2,1,0:T(8,128)S(1)} %get-tuple-element.51), channel_id=1, source_target_pairs={{0,4},{4,0},{8,12},{12,8},{1,5},{5,1},{9,13},{13,9},{2,6},{6,2},{1... | collective-permute-start | bytes 393224 | tf_op jit(solution)/shard_map/ppermute | solution.py:417
  15.3 5.2 %collective-permute-start.5 = (f32[16,8,256]{2,1,0:T(8,128)S(1)}, f32[16,8,256]{2,1,0:T(8,128)S(1)}, u32[]{:S(2)}, u32[]{:S(2)}) collective-permute-start(f32[16,8,256]{2,1,0:T(8,128)S(1)} %get-tuple-element.52), channel_id=1, source_target_pairs={{0,1},{12,13},{4,8},{8,4},{1,0},{13,12},{5,9},{9,5},{2,3},{14,15},... | collective-permute-start | bytes 393224 | tf_op jit(solution)/shard_map/ppermute | solution.py:63
  16.1 4.4 %collective-permute-start.6 = (f32[8,8,256]{2,1,0:T(8,128)S(1)}, f32[8,8,256]{2,1,0:T(8,128)S(1)}, u32[]{:S(2)}, u32[]{:S(2)}) collective-permute-start(f32[8,8,256]{2,1,0:T(8,128)S(1)} %get-tuple-element.53), channel_id=1, source_target_pairs={{0,16},{16,0},{1,17},{17,1},{2,18},{18,2},{3,19},{19,3},{4,20},{20... | collective-permute-start | bytes 196616 | tf_op jit(solution)/shard_map/ppermute | solution.py:417
  20.7 5.6 %collective-permute-start.7 = (f32[16,8,256]{2,1,0:T(8,128)S(1)}, f32[16,8,256]{2,1,0:T(8,128)S(1)}, u32[]{:S(2)}, u32[]{:S(2)}) collective-permute-start(f32[16,8,256]{2,1,0:T(8,128)S(1)} %get-tuple-element.57), channel_id=1, source_target_pairs={{0,4},{4,0},{8,12},{12,8},{1,5},{5,1},{9,13},{13,9},{2,6},{6,2},{1... | collective-permute-start | bytes 393224 | tf_op jit(solution)/shard_map/ppermute | solution.py:417
  20.8 5.5 %collective-permute-start.8 = (f32[16,8,256]{2,1,0:T(8,128)S(1)}, f32[16,8,256]{2,1,0:T(8,128)S(1)}, u32[]{:S(2)}, u32[]{:S(2)}) collective-permute-start(f32[16,8,256]{2,1,0:T(8,128)S(1)} %get-tuple-element.58), channel_id=1, source_target_pairs={{0,1},{12,13},{4,8},{8,4},{1,0},{13,12},{5,9},{9,5},{2,3},{14,15},... | collective-permute-start | bytes 393224 | tf_op jit(solution)/shard_map/ppermute | solution.py:63
  22.0 4.3 %collective-permute-start.9 = (f32[8,8,256]{2,1,0:T(8,128)S(1)}, f32[8,8,256]{2,1,0:T(8,128)S(1)}, u32[]{:S(2)}, u32[]{:S(2)}) collective-permute-start(f32[8,8,256]{2,1,0:T(8,128)S(1)} %get-tuple-element.59), channel_id=1, source_target_pairs={{0,16},{16,0},{1,17},{17,1},{2,18},{18,2},{3,19},{19,3},{4,20},{20... | collective-permute-start | bytes 196616 | tf_op jit(solution)/shard_map/ppermute | solution.py:417
  26.5 5.4 %collective-permute-start.10 = (f32[16,8,256]{2,1,0:T(8,128)S(1)}, f32[16,8,256]{2,1,0:T(8,128)S(1)}, u32[]{:S(2)}, u32[]{:S(2)}) collective-permute-start(f32[16,8,256]{2,1,0:T(8,128)S(1)} %get-tuple-element.64), channel_id=1, source_target_pairs={{0,4},{4,0},{8,12},{12,8},{1,5},{5,1},{9,13},{13,9},{2,6},{6,2},{1... | collective-permute-start | bytes 393224 | tf_op jit(solution)/shard_map/ppermute | solution.py:417
  26.6 5.3 %collective-permute-start.11 = (f32[16,8,256]{2,1,0:T(8,128)S(1)}, f32[16,8,256]{2,1,0:T(8,128)S(1)}, u32[]{:S(2)}, u32[]{:S(2)}) collective-permute-start(f32[16,8,256]{2,1,0:T(8,128)S(1)} %get-tuple-element.65), channel_id=1, source_target_pairs={{0,1},{12,13},{4,8},{8,4},{1,0},{13,12},{5,9},{9,5},{2,3},{14,15},... | collective-permute-start | bytes 393224 | tf_op jit(solution)/shard_map/ppermute | solution.py:63
  27.5 4.4 %collective-permute-start.12 = (f32[8,8,256]{2,1,0:T(8,128)S(1)}, f32[8,8,256]{2,1,0:T(8,128)S(1)}, u32[]{:S(2)}, u32[]{:S(2)}) collective-permute-start(f32[8,8,256]{2,1,0:T(8,128)S(1)} %get-tuple-element.66), channel_id=1, source_target_pairs={{0,16},{16,0},{1,17},{17,1},{2,18},{18,2},{3,19},{19,3},{4,20},{20... | collective-permute-start | bytes 196616 | tf_op jit(solution)/shard_map/ppermute | solution.py:417
  32.3 4.3 %collective-permute-start.13 = (f32[16,8,128]{2,1,0:T(8,128)S(1)}, f32[16,8,128]{2,1,0:T(8,128)S(1)}, u32[]{:S(2)}, u32[]{:S(2)}) collective-permute-start(f32[16,8,128]{2,1,0:T(8,128)S(1)} %get-tuple-element.70), channel_id=1, source_target_pairs={{0,1},{1,0},{2,3},{3,2},{4,5},{5,4},{6,7},{7,6},{8,9},{9,8},{10,11... | collective-permute-start | bytes 196616 | tf_op jit(solution)/shard_map/ppermute | solution.py:417
  36.6 5.9 %collective-permute-start.14 = (f32[16,8,128]{2,1,0:T(8,128)S(1)}, f32[16,8,128]{2,1,0:T(8,128)S(1)}, u32[]{:S(2)}, u32[]{:S(2)}) collective-permute-start(f32[16,8,128]{2,1,0:T(8,128)S(1)} %add.8), channel_id=1, source_target_pairs={{0,2},{1,3},{2,0},{3,1},{4,6},{5,7},{6,4},{7,5},{8,10},{9,11},{10,... | collective-permute-start | bytes 196616 | tf_op jit(solution)/shard_map/ppermute | solution.py:417

commit v2 on v1

--- a/solution.py
+++ b/solution.py
@@ -521,8 +521,15 @@
         previous, current = current, nxt
     bit = 1
     while bit < nshot:
-        coarse = coarse + swap(coarse, "shot", xor(nshot, bit))
-        bit *= 2
+        one = swap(coarse, "shot", xor(nshot, bit))
+        if nshot % (4 * bit) == 0:
+            two = swap(coarse, "shot", xor(nshot, 2 * bit))
+            three = swap(coarse, "shot", xor(nshot, 3 * bit))
+            coarse = (coarse + one) + (two + three)
+            bit *= 4
+        else:
+            coarse = coarse + one
+            bit *= 2
     previous, current = vmem_call(
         flush_kernel, [sds(tile), sds(tile)], [previous, current], [pltpu.SemaphoreType.DMA((2,))],
         hbm_out=(0, 1),

time: 43.3 us -> 42.4 us (0.979)
  waiting for transfers between devices: 11.5 us -> 10.2 us
    ppermute x11 -> x12, waiting for transfers between devices: 11.5 us -> 10.1 us  [swap(): return odd_swap(x, axis) if pairs is None else lax.ppermute(x, axis, pairs)]
    ppermute x11 -> x12, starting transfers between devices: 14.5 us -> 14.9 us  [swap(): return odd_swap(x, axis) if pairs is None else lax.ppermute(x, axis, pairs)]
  transfers between devices with their start and end apart: 15 -> 16, of which waited for: 6 -> 6; matrix products, arithmetic and copies ran while one was open for 0% -> 0% of each run, Pallas kernels for 20% -> 20%
where the time goes in v2:
time: 42.4 us; the launch traced here: 42.2 us
  starting transfers between devices  19.9 us (47%)
  waiting for transfers between devices  10.2 us (24%)
  Pallas kernels  10.1 us (24%)
  between operations  1.44 us (3%)
  other arithmetic  0.67 us (2%)
    ppermute x12, starting transfers between devices, swap(): return odd_swap(x, axis) if pairs is None else lax.ppermute(x, axis, pairs)  14.9 us
    ppermute x12, waiting for transfers between devices, swap(): return odd_swap(x, axis) if pairs is None else lax.ppermute(x, axis, pairs)  10.1 us
    pallas_call x10, Pallas kernels, vmem_call(): pl.pallas_call(kernel, out_shape=tuple(outs), in_specs=in_specs, out_spec...  10.1 us
    ppermute x4, starting transfers between devices, odd_swap(): return lax.ppermute(x, (axis, 'shot'), pairs)  4.98 us
  transfers between devices with their start and end apart: 16, of which 6 were waited for; matrix products, arithmetic and copies ran while one was open for 0% of the time, Pallas kernels for 20%

profile of v2, /device:TPU:0, one launch (start us, length us, event | category | flops | bytes accessed | tf_op | source)
XLA Modules:
  0.0 42.2 jit_solution(13492508742716828615)
XLA Ops:
  0.6 3.0 %collective-permute-start = (bf16[1,4,64]{2,1,0:T(4,128)(2,1)}, bf16[1,4,64]{2,1,0:T(4,128)(2,1)S(1)}, u32[]{:S(2)}, u32[]{:S(2)}) collective-permute-start(bf16[1,4,64]{2,1,0:T(4,128)(2,1)} %traces_in.1), channel_id=1, source_target_pairs={{0,8},{4,12},{8,0},{12,4},{1,9},{5,13},{9,1},{13,5},{2,10},{6,14},... | collective-permute-start | bytes 1544 | tf_op jit(solution)/shard_map/ppermute | solution.py:417
  4.3 1.2 %shard_map.112 = (f32[32,16,256]{2,1,0:T(8,128)S(1)}, f32[16,8,256]{2,1,0:T(8,128)S(1)}, f32[16,8,256]{2,1,0:T(8,128)S(1)}, f32[8,8,256]{2,1,0:T(8,128)S(1)}, bf...) custom-call(f32[32,16,256]{2,1,0:T(8,128)} %bitcast.12, ...), custom_call_target="tpu_custom_call" | custom-call | bytes 1872900 | tf_op jit(solution)/shard_map/pallas_call | solution.py:26
  5.6 2.1 %collective-permute-start.2 = (f32[16,8,256]{2,1,0:T(8,128)S(1)}, f32[16,8,256]{2,1,0:T(8,128)S(1)}, u32[]{:S(2)}, u32[]{:S(2)}) collective-permute-start(f32[16,8,256]{2,1,0:T(8,128)S(1)} %get-tuple-element.46), channel_id=1, source_target_pairs={{0,1},{12,13},{4,8},{8,4},{1,0},{13,12},{5,9},{9,5},{2,3},{14,15},... | collective-permute-start | bytes 393224 | tf_op jit(solution)/shard_map/ppermute | solution.py:63
  7.7 2.2 %shard_map.113 = (f32[32,16,256]{2,1,0:T(8,128)S(1)}, f32[32,16,256]{2,1,0:T(8,128)}, f32[32,16,256]{2,1,0:T(8,128)S(1)}, bf16[64,16,256]{2,1,0:T(8,128)(2,1)S(1)}) custom-call(f32[32,16,256]{2,1,0:T(8,128)S(1)} %get-tuple-element.38.cur.prev, bf16[512,256]{1,0:T(8,128)(2,1)S(1)} %get-tuple-element.39.toeplitz, f32[32,16,256]{2,1,0:T(8,128)} %bitcast.13, ...), custom_call_target="tpu_custom_call" | custom-call | flops 7864320 | bytes 4456448 | tf_op jit(solution)/shard_map/pallas_call | solution.py:26
  10.0 1.6 %collective-permute-start.3 = (f32[10,8,256]{2,1,0:T(8,128)S(1)}, f32[10,8,256]{2,1,0:T(8,128)S(1)}, u32[]{:S(2)}, u32[]{:S(2)}) collective-permute-start(f32[10,8,256]{2,1,0:T(8,128)S(1)} %pad_maximum_fusion), channel_id=1, source_target_pairs={{0,16},{16,0},{1,17},{17,1},{2,18},{18,2},{3,19},{19,3},{4,20},{20... | collective-permute-start | bytes 245768 | tf_op jit(solution)/shard_map/ppermute | solution.py:417
  11.5 2.9 %collective-permute-done.3.refs_2_ = f32[10,8,256]{2,1,0:T(8,128)S(1)} collective-permute-done((f32[10,8,256]{2,1,0:T(8,128)S(1)}, f32[10,8,256]{2,1,0:T(8,128)S(1)}, u32[]{:S(2)}, u32[]{:S(2)}) %collective-permute-start.3) | collective-permute-done | bytes 81952 | tf_op jit(solution)/shard_map/ppermute | solution.py:417
  14.5 0.7 %shard_map.114 = (f32[32,16,256]{2,1,0:T(8,128)S(1)}, bf16[4,192,256]{2,1,0:T(8,128)(2,1)S(1)}, f32[16,8,256]{2,1,0:T(8,128)S(1)}, f32[16,8,256]{2,1,0:T(8,128)S(1)}, f32[8,8,256]{2,1,0:T(8,128)S(1)}) custom-call(s32[64,128]{1,0:T(8,128)S(1)} %get-tuple-element.37.owners, bf16[64,16,256]{2,1,0:T(8,128)(2,1)S(1)} %get-tuple-element.40.weights, ...), custom_call_target="tpu_custom_call" | custom-call | bytes 3407872 | tf_op jit(solution)/shard_map/pallas_call | solution.py:26
  15.3 0.8 %collective-permute-start.5 = (f32[16,8,256]{2,1,0:T(8,128)S(1)}, f32[16,8,256]{2,1,0:T(8,128)S(1)}, u32[]{:S(2)}, u32[]{:S(2)}) collective-permute-start(f32[16,8,256]{2,1,0:T(8,128)S(1)} %get-tuple-element.52), channel_id=1, source_target_pairs={{0,1},{12,13},{4,8},{8,4},{1,0},{13,12},{5,9},{9,5},{2,3},{14,15},... | collective-permute-start | bytes 393224 | tf_op jit(solution)/shard_map/ppermute | solution.py:63
  16.1 2.1 %collective-permute-start.6 = (f32[8,8,256]{2,1,0:T(8,128)S(1)}, f32[8,8,256]{2,1,0:T(8,128)S(1)}, u32[]{:S(2)}, u32[]{:S(2)}) collective-permute-start(f32[8,8,256]{2,1,0:T(8,128)S(1)} %get-tuple-element.53), channel_id=1, source_target_pairs={{0,16},{16,0},{1,17},{17,1},{2,18},{18,2},{3,19},{19,3},{4,20},{20... | collective-permute-start | bytes 196616 | tf_op jit(solution)/shard_map/ppermute | solution.py:417
  18.1 1.4 %shard_map.115 = (f32[32,16,256]{2,1,0:T(8,128)S(1)}, f32[32,16,256]{2,1,0:T(8,128)S(1)}) custom-call(f32[32,16,256]{2,1,0:T(8,128)S(1)} %get-tuple-element.48.cur.prev, f32[32,16,256]{2,1,0:T(8,128)S(1)} %get-tuple-element.38.cur.prev, f32[32,16,256]{2,1,0:T(8,128)S(1)} %get-tuple-element.43.c2, bf16[512,256]{1,0:T(8,128)(2,1)S(1)} %get-tuple-element.39.toeplitz, ...), custom_call_target="tpu_custom_call" | custom-call | flops 7864320 | bytes 4521984 | tf_op jit(solution)/shard_map/pallas_call | solution.py:26
  19.5 1.0 %collective-permute-done.6.refs_2_ = f32[8,8,256]{2,1,0:T(8,128)S(1)} collective-permute-done((f32[8,8,256]{2,1,0:T(8,128)S(1)}, f32[8,8,256]{2,1,0:T(8,128)S(1)}, u32[]{:S(2)}, u32[]{:S(2)}) %collective-permute-start.6) | collective-permute-done | bytes 65568 | tf_op jit(solution)/shard_map/ppermute | solution.py:417
  20.8 1.2 %collective-permute-start.8 = (f32[16,8,256]{2,1,0:T(8,128)S(1)}, f32[16,8,256]{2,1,0:T(8,128)S(1)}, u32[]{:S(2)}, u32[]{:S(2)}) collective-permute-start(f32[16,8,256]{2,1,0:T(8,128)S(1)} %get-tuple-element.58), channel_id=1, source_target_pairs={{0,1},{12,13},{4,8},{8,4},{1,0},{13,12},{5,9},{9,5},{2,3},{14,15},... | collective-permute-start | bytes 393224 | tf_op jit(solution)/shard_map/ppermute | solution.py:63
  22.0 1.5 %collective-permute-start.9 = (f32[8,8,256]{2,1,0:T(8,128)S(1)}, f32[8,8,256]{2,1,0:T(8,128)S(1)}, u32[]{:S(2)}, u32[]{:S(2)}) collective-permute-start(f32[8,8,256]{2,1,0:T(8,128)S(1)} %get-tuple-element.59), channel_id=1, source_target_pairs={{0,16},{16,0},{1,17},{17,1},{2,18},{18,2},{3,19},{19,3},{4,20},{20... | collective-permute-start | bytes 196616 | tf_op jit(solution)/shard_map/ppermute | solution.py:417
  23.5 1.4 %shard_map.117 = (f32[32,16,256]{2,1,0:T(8,128)S(1)}, f32[32,16,256]{2,1,0:T(8,128)S(1)}) custom-call(f32[32,16,256]{2,1,0:T(8,128)S(1)} %get-tuple-element.54.cur.prev, f32[32,16,256]{2,1,0:T(8,128)S(1)} %get-tuple-element.48.cur.prev, f32[32,16,256]{2,1,0:T(8,128)S(1)} %get-tuple-element.43.c2, bf16[512,256]{1,0:T(8,128)(2,1)S(1)} %get-tuple-element.39.toeplitz, ...), custom_call_target="tpu_custom_call" | custom-call | flops 7864320 | bytes 5046272 | tf_op jit(solution)/shard_map/pallas_call | solution.py:26
  24.9 1.3 %collective-permute-done.9.refs_2_ = f32[8,8,256]{2,1,0:T(8,128)S(1)} collective-permute-done((f32[8,8,256]{2,1,0:T(8,128)S(1)}, f32[8,8,256]{2,1,0:T(8,128)S(1)}, u32[]{:S(2)}, u32[]{:S(2)}) %collective-permute-start.9) | collective-permute-done | bytes 65568 | tf_op jit(solution)/shard_map/ppermute | solution.py:417
  26.6 0.9 %collective-permute-start.11 = (f32[16,8,256]{2,1,0:T(8,128)S(1)}, f32[16,8,256]{2,1,0:T(8,128)S(1)}, u32[]{:S(2)}, u32[]{:S(2)}) collective-permute-start(f32[16,8,256]{2,1,0:T(8,128)S(1)} %get-tuple-element.65), channel_id=1, source_target_pairs={{0,1},{12,13},{4,8},{8,4},{1,0},{13,12},{5,9},{9,5},{2,3},{14,15},... | collective-permute-start | bytes 393224 | tf_op jit(solution)/shard_map/ppermute | solution.py:63
  27.5 1.9 %collective-permute-start.12 = (f32[8,8,256]{2,1,0:T(8,128)S(1)}, f32[8,8,256]{2,1,0:T(8,128)S(1)}, u32[]{:S(2)}, u32[]{:S(2)}) collective-permute-start(f32[8,8,256]{2,1,0:T(8,128)S(1)} %get-tuple-element.66), channel_id=1, source_target_pairs={{0,16},{16,0},{1,17},{17,1},{2,18},{18,2},{3,19},{19,3},{4,20},{20... | collective-permute-start | bytes 196616 | tf_op jit(solution)/shard_map/ppermute | solution.py:417
  29.4 1.4 %shard_map.119 = (f32[32,16,256]{2,1,0:T(8,128)S(1)}, f32[32,16,256]{2,1,0:T(8,128)S(1)}) custom-call(f32[32,16,256]{2,1,0:T(8,128)S(1)} %get-tuple-element.60.cur.a_in, f32[32,16,256]{2,1,0:T(8,128)S(1)} %get-tuple-element.54.cur.prev, f32[32,16,256]{2,1,0:T(8,128)S(1)} %get-tuple-element.43.c2, bf16[512,256]{1,0:T(8,128)(2,1)S(1)} %get-tuple-element.39.toeplitz, ...), custom_call_target="tpu_custom_call" | custom-call | flops 7864320 | bytes 5046272 | tf_op jit(solution)/shard_map/pallas_call | solution.py:26
  30.8 1.1 %collective-permute-done.12.refs_2_ = f32[8,8,256]{2,1,0:T(8,128)S(1)} collective-permute-done((f32[8,8,256]{2,1,0:T(8,128)S(1)}, f32[8,8,256]{2,1,0:T(8,128)S(1)}, u32[]{:S(2)}, u32[]{:S(2)}) %collective-permute-start.12) | collective-permute-done | bytes 65568 | tf_op jit(solution)/shard_map/ppermute | solution.py:417
  32.3 3.2 %collective-permute-start.15 = (f32[16,8,128]{2,1,0:T(8,128)S(1)}, f32[16,8,128]{2,1,0:T(8,128)S(1)}, u32[]{:S(2)}, u32[]{:S(2)}) collective-permute-start(f32[16,8,128]{2,1,0:T(8,128)S(1)} %get-tuple-element.70), channel_id=1, source_target_pairs={{0,3},{1,2},{2,1},{3,0},{4,7},{5,6},{6,5},{7,4},{8,11},{9,10},{10,... | collective-permute-start | bytes 196616 | tf_op jit(solution)/shard_map/ppermute | solution.py:417
  35.5 1.3 %collective-permute-start.13 = (f32[16,8,128]{2,1,0:T(8,128)S(1)}, f32[16,8,128]{2,1,0:T(8,128)S(1)}, u32[]{:S(2)}, u32[]{:S(2)}) collective-permute-start(f32[16,8,128]{2,1,0:T(8,128)S(1)} %get-tuple-element.70), channel_id=1, source_target_pairs={{0,1},{1,0},{2,3},{3,2},{4,5},{5,4},{6,7},{7,6},{8,9},{9,8},{10,11... | collective-permute-start | bytes 196616 | tf_op jit(solution)/shard_map/ppermute | solution.py:417
  36.7 1.0 %shard_map.121 = (f32[32,16,256]{2,1,0:T(8,128)}, f32[32,16,256]{2,1,0:T(8,128)}) custom-call(f32[32,16,256]{2,1,0:T(8,128)S(1)} %get-tuple-element.60.cur.a_in, f32[32,16,256]{2,1,0:T(8,128)S(1)} %get-tuple-element.67.b_in), custom_call_target="tpu_custom_call" | custom-call | bytes 2097152 | tf_op jit(solution)/shard_map/pallas_call | solution.py:26
  37.7 1.0 %collective-permute-done.15 = f32[16,8,128]{2,1,0:T(8,128)S(1)} collective-permute-done((f32[16,8,128]{2,1,0:T(8,128)S(1)}, f32[16,8,128]{2,1,0:T(8,128)S(1)}, u32[]{:S(2)}, u32[]{:S(2)}) %collective-permute-start.15) | collective-permute-done | bytes 65568 | tf_op jit(solution)/shard_map/ppermute | solution.py:417
  38.7 2.9 %collective-permute-done.14 = f32[16,8,128]{2,1,0:T(8,128)S(1)} collective-permute-done((f32[16,8,128]{2,1,0:T(8,128)S(1)}, f32[16,8,128]{2,1,0:T(8,128)S(1)}, u32[]{:S(2)}, u32[]{:S(2)}) %collective-permute-start.14) | collective-permute-done | bytes 65568 | tf_op jit(solution)/shard_map/ppermute | solution.py:417
  (26 shorter events, 1.8 us)
Async XLA Ops:
  0.6 4.8 %collective-permute-start = (bf16[1,4,64]{2,1,0:T(4,128)(2,1)}, bf16[1,4,64]{2,1,0:T(4,128)(2,1)S(1)}, u32[]{:S(2)}, u32[]{:S(2)}) collective-permute-start(bf16[1,4,64]{2,1,0:T(4,128)(2,1)} %traces_in.1), channel_id=1, source_target_pairs={{0,8},{4,12},{8,0},{12,4},{1,9},{5,13},{9,1},{13,5},{2,10},{6,14},... | collective-permute-start | bytes 1544 | tf_op jit(solution)/shard_map/ppermute | solution.py:417
  5.5 4.4 %collective-permute-start.1 = (f32[17,8,256]{2,1,0:T(8,128)S(1)}, f32[17,8,256]{2,1,0:T(8,128)S(1)}, u32[]{:S(2)}, u32[]{:S(2)}) collective-permute-start(f32[17,8,256]{2,1,0:T(8,128)S(1)} %maximum_maximum_fusion), channel_id=1, source_target_pairs={{0,4},{4,0},{8,12},{12,8},{1,5},{5,1},{9,13},{13,9},{2,6},{6,2},{1... | collective-permute-start | bytes 417800 | tf_op jit(solution)/shard_map/ppermute | solution.py:417
  5.6 5.9 %collective-permute-start.2 = (f32[16,8,256]{2,1,0:T(8,128)S(1)}, f32[16,8,256]{2,1,0:T(8,128)S(1)}, u32[]{:S(2)}, u32[]{:S(2)}) collective-permute-start(f32[16,8,256]{2,1,0:T(8,128)S(1)} %get-tuple-element.46), channel_id=1, source_target_pairs={{0,1},{12,13},{4,8},{8,4},{1,0},{13,12},{5,9},{9,5},{2,3},{14,15},... | collective-permute-start | bytes 393224 | tf_op jit(solution)/shard_map/ppermute | solution.py:63
  10.0 4.5 %collective-permute-start.3 = (f32[10,8,256]{2,1,0:T(8,128)S(1)}, f32[10,8,256]{2,1,0:T(8,128)S(1)}, u32[]{:S(2)}, u32[]{:S(2)}) collective-permute-start(f32[10,8,256]{2,1,0:T(8,128)S(1)} %pad_maximum_fusion), channel_id=1, source_target_pairs={{0,16},{16,0},{1,17},{17,1},{2,18},{18,2},{3,19},{19,3},{4,20},{20... | collective-permute-start | bytes 245768 | tf_op jit(solution)/shard_map/ppermute | solution.py:417
  14.5 3.6 %copy-start = (bf16[1,4,32,16,256]{4,3,2,1,0:T(8,128)(2,1)S(1)}, bf16[1,4,32,16,256]{4,3,2,1,0:T(8,128)(2,1)}, u32[]{:S(2)}) copy-start(bf16[1,4,32,16,256]{4,3,2,1,0:T(8,128)(2,1)} %param.11) | copy-start | bytes 3145732
  15.2 5.3 %collective-permute-start.4 = (f32[16,8,256]{2,1,0:T(8,128)S(1)}, f32[16,8,256]{2,1,0:T(8,128)S(1)}, u32[]{:S(2)}, u32[]{:S(2)}) collective-permute-start(f32[16,8,256]{2,1,0:T(8,128)S(1)} %get-tuple-element.51), channel_id=1, source_target_pairs={{0,4},{4,0},{8,12},{12,8},{1,5},{5,1},{9,13},{13,9},{2,6},{6,2},{1... | collective-permute-start | bytes 393224 | tf_op jit(solution)/shard_map/ppermute | solution.py:417
  15.3 5.2 %collective-permute-start.5 = (f32[16,8,256]{2,1,0:T(8,128)S(1)}, f32[16,8,256]{2,1,0:T(8,128)S(1)}, u32[]{:S(2)}, u32[]{:S(2)}) collective-permute-start(f32[16,8,256]{2,1,0:T(8,128)S(1)} %get-tuple-element.52), channel_id=1, source_target_pairs={{0,1},{12,13},{4,8},{8,4},{1,0},{13,12},{5,9},{9,5},{2,3},{14,15},... | collective-permute-start | bytes 393224 | tf_op jit(solution)/shard_map/ppermute | solution.py:63
  16.1 4.4 %collective-permute-start.6 = (f32[8,8,256]{2,1,0:T(8,128)S(1)}, f32[8,8,256]{2,1,0:T(8,128)S(1)}, u32[]{:S(2)}, u32[]{:S(2)}) collective-permute-start(f32[8,8,256]{2,1,0:T(8,128)S(1)} %get-tuple-element.53), channel_id=1, source_target_pairs={{0,16},{16,0},{1,17},{17,1},{2,18},{18,2},{3,19},{19,3},{4,20},{20... | collective-permute-start | bytes 196616 | tf_op jit(solution)/shard_map/ppermute | solution.py:417
  20.7 5.6 %collective-permute-start.7 = (f32[16,8,256]{2,1,0:T(8,128)S(1)}, f32[16,8,256]{2,1,0:T(8,128)S(1)}, u32[]{:S(2)}, u32[]{:S(2)}) collective-permute-start(f32[16,8,256]{2,1,0:T(8,128)S(1)} %get-tuple-element.57), channel_id=1, source_target_pairs={{0,4},{4,0},{8,12},{12,8},{1,5},{5,1},{9,13},{13,9},{2,6},{6,2},{1... | collective-permute-start | bytes 393224 | tf_op jit(solution)/shard_map/ppermute | solution.py:417
  20.8 5.5 %collective-permute-start.8 = (f32[16,8,256]{2,1,0:T(8,128)S(1)}, f32[16,8,256]{2,1,0:T(8,128)S(1)}, u32[]{:S(2)}, u32[]{:S(2)}) collective-permute-start(f32[16,8,256]{2,1,0:T(8,128)S(1)} %get-tuple-element.58), channel_id=1, source_target_pairs={{0,1},{12,13},{4,8},{8,4},{1,0},{13,12},{5,9},{9,5},{2,3},{14,15},... | collective-permute-start | bytes 393224 | tf_op jit(solution)/shard_map/ppermute | solution.py:63
  22.0 4.3 %collective-permute-start.9 = (f32[8,8,256]{2,1,0:T(8,128)S(1)}, f32[8,8,256]{2,1,0:T(8,128)S(1)}, u32[]{:S(2)}, u32[]{:S(2)}) collective-permute-start(f32[8,8,256]{2,1,0:T(8,128)S(1)} %get-tuple-element.59), channel_id=1, source_target_pairs={{0,16},{16,0},{1,17},{17,1},{2,18},{18,2},{3,19},{19,3},{4,20},{20... | collective-permute-start | bytes 196616 | tf_op jit(solution)/shard_map/ppermute | solution.py:417
  26.5 5.4 %collective-permute-start.10 = (f32[16,8,256]{2,1,0:T(8,128)S(1)}, f32[16,8,256]{2,1,0:T(8,128)S(1)}, u32[]{:S(2)}, u32[]{:S(2)}) collective-permute-start(f32[16,8,256]{2,1,0:T(8,128)S(1)} %get-tuple-element.64), channel_id=1, source_target_pairs={{0,4},{4,0},{8,12},{12,8},{1,5},{5,1},{9,13},{13,9},{2,6},{6,2},{1... | collective-permute-start | bytes 393224 | tf_op jit(solution)/shard_map/ppermute | solution.py:417
  26.6 5.3 %collective-permute-start.11 = (f32[16,8,256]{2,1,0:T(8,128)S(1)}, f32[16,8,256]{2,1,0:T(8,128)S(1)}, u32[]{:S(2)}, u32[]{:S(2)}) collective-permute-start(f32[16,8,256]{2,1,0:T(8,128)S(1)} %get-tuple-element.65), channel_id=1, source_target_pairs={{0,1},{12,13},{4,8},{8,4},{1,0},{13,12},{5,9},{9,5},{2,3},{14,15},... | collective-permute-start | bytes 393224 | tf_op jit(solution)/shard_map/ppermute | solution.py:63
  27.5 4.4 %collective-permute-start.12 = (f32[8,8,256]{2,1,0:T(8,128)S(1)}, f32[8,8,256]{2,1,0:T(8,128)S(1)}, u32[]{:S(2)}, u32[]{:S(2)}) collective-permute-start(f32[8,8,256]{2,1,0:T(8,128)S(1)} %get-tuple-element.66), channel_id=1, source_target_pairs={{0,16},{16,0},{1,17},{17,1},{2,18},{18,2},{3,19},{19,3},{4,20},{20... | collective-permute-start | bytes 196616 | tf_op jit(solution)/shard_map/ppermute | solution.py:417
  32.3 6.4 %collective-permute-start.15 = (f32[16,8,128]{2,1,0:T(8,128)S(1)}, f32[16,8,128]{2,1,0:T(8,128)S(1)}, u32[]{:S(2)}, u32[]{:S(2)}) collective-permute-start(f32[16,8,128]{2,1,0:T(8,128)S(1)} %get-tuple-element.70), channel_id=1, source_target_pairs={{0,3},{1,2},{2,1},{3,0},{4,7},{5,6},{6,5},{7,4},{8,11},{9,10},{10,... | collective-permute-start | bytes 196616 | tf_op jit(solution)/shard_map/ppermute | solution.py:417
  35.5 6.1 %collective-permute-start.14 = (f32[16,8,128]{2,1,0:T(8,128)S(1)}, f32[16,8,128]{2,1,0:T(8,128)S(1)}, u32[]{:S(2)}, u32[]{:S(2)}) collective-permute-start(f32[16,8,128]{2,1,0:T(8,128)S(1)} %get-tuple-element.70), channel_id=1, source_target_pairs={{0,2},{1,3},{2,0},{3,1},{4,6},{5,7},{6,4},{7,5},{8,10},{9,11},{10,... | collective-permute-start | bytes 196616 | tf_op jit(solution)/shard_map/ppermute | solution.py:417
  35.5 6.1 %collective-permute-start.13 = (f32[16,8,128]{2,1,0:T(8,128)S(1)}, f32[16,8,128]{2,1,0:T(8,128)S(1)}, u32[]{:S(2)}, u32[]{:S(2)}) collective-permute-start(f32[16,8,128]{2,1,0:T(8,128)S(1)} %get-tuple-element.70), channel_id=1, source_target_pairs={{0,1},{1,0},{2,3},{3,2},{4,5},{5,4},{6,7},{7,6},{8,9},{9,8},{10,11... | collective-permute-start | bytes 196616 | tf_op jit(solution)/shard_map/ppermute | solution.py:417

commit v3 on v2

--- a/solution.py
+++ b/solution.py
@@ -72,43 +72,55 @@
     return jnp.dot(a, b, preferred_element_type=F32)
 
 
-def put_y_face(cur, out, high):
+def put_y_face(cur, out, stage, high):
     cx, cy, _ = cur.shape
     start = cy - REACH if high else 0
-    for i in range(cx // 2):
-        out[i, 0:REACH, :] = cur[2 * i, start : start + REACH, :]
-        out[i, REACH : 2 * REACH, :] = cur[2 * i + 1, start : start + REACH, :]
-
-
-def put_faces(cur, gx_index, gy_index, ye, yo, xe, xo):
+    for h in range(stage.shape[0]):
+        at = slice(h * 128, (h + 1) * 128)
+        for x in range(cx):
+            stage[h, REACH * x : REACH * (x + 1), :] = cur[x, start : start + REACH, at]
+        out[0 : REACH * cx, at] = stage[h, :, :].astype(BF16)
+        near = stage[h, pl.ds(REACH - 1 if high else 0, cx, REACH), :]
+        out[REACH * cx : (REACH + 1) * cx, at] = split2(near)[1]
+
+
+def put_x_face(cur, out, high):
     cx, cy, _ = cur.shape
+    low = jnp.where(high, cx - REACH, 0)
+    for r in range(REACH):
+        out[r * cy : (r + 1) * cy, :] = cur[low + r, :, :].astype(BF16)
+    out[REACH * cy : (REACH + 1) * cy, :] = split2(cur[jnp.where(high, cx - 1, 0), :, :])[1]
+
+
+def put_faces(cur, gx_index, gy_index, ye, yo, xe, xo, stage):
     y_even = gy_index % 2 == 0
     x_even = gx_index % 2 == 0
 
     @pl.when(y_even)
     def _():
-        put_y_face(cur, ye, True)
+        put_y_face(cur, ye, stage, True)
         if yo is not None:
-            put_y_face(cur, yo, False)
+            put_y_face(cur, yo, stage, False)
 
     @pl.when(jnp.logical_not(y_even))
     def _():
-        put_y_face(cur, ye, False)
+        put_y_face(cur, ye, stage, False)
         if yo is not None:
-            put_y_face(cur, yo, True)
-
-    half = cy // 8
-    low = jnp.where(x_even, cx - REACH, 0)
-    for r in range(REACH):
-        for h in range(half):
-            xe[r * half + h, :, :] = cur[low + r, 8 * h : 8 * h + 8, :]
-            if xo is not None:
-                xo[r * half + h, :, :] = cur[cx - REACH - low + r, 8 * h : 8 * h + 8, :]
-
-
-def add_y_halo(nxt, c2, recv, high):
+            put_y_face(cur, yo, stage, True)
+
+    put_x_face(cur, xe, x_even)
+    if xo is not None:
+        put_x_face(cur, xo, jnp.logical_not(x_even))
+
+
+def add_y_halo(nxt, c2, recv, stage, high):
     cx, cy, nz = nxt.shape
     w = LAPLACE_COEFS
+    near = pl.ds(0 if high else REACH - 1, cx, REACH)
+    for h in range(stage.shape[0]):
+        at = slice(h * 128, (h + 1) * 128)
+        stage[h, :, :] = recv[0 : REACH * cx, at].astype(F32)
+        stage[h, near, :] = stage[h, near, :] + recv[REACH * cx : (REACH + 1) * cx, at].astype(F32)
     row = lax.broadcasted_iota(jnp.int32, (8, nz), 0) % REACH
     coefs = {}
     for k in range(1, REACH + 1):
@@ -117,7 +129,7 @@
         coefs[k] = jnp.where(keep, w[k], 0.0)
     start = cy - REACH if high else 0
     for i in range(cx // 2):
-        m = recv[i, :, :]
+        m = jnp.concatenate([stage[h, 8 * i : 8 * i + 8, :] for h in range(stage.shape[0])], axis=1)
         total = w[REACH] * m
         for k in range(1, REACH):
             shift = REACH - k
@@ -129,50 +141,50 @@
             )
 
 
-def add_x_halo(nxt, c2, recv, high):
+def add_x_halo(nxt, c2, recv, stage, high):
     cx, cy, _ = nxt.shape
     w = LAPLACE_COEFS
-    half = cy // 8
+    layers = [recv[r * cy : (r + 1) * cy, :].astype(F32) for r in range(REACH + 1)]
+    near = 0 if high else REACH - 1
+    layers[near] = layers[near] + layers[REACH]
     for r in range(REACH):
         x = cx - 1 - r if high else r
-        for h in range(half):
-            total = None
-            for k in range(r + 1, REACH + 1):
-                row = (k - r - 1) if high else (REACH + r - k)
-                term = w[k] * recv[row * half + h, :, :]
-                total = term if total is None else total + term
-            ys = slice(8 * h, 8 * h + 8)
-            nxt[x, ys, :] = nxt[x, ys, :] + c2[x, ys, :] * total
-
-
-def add_halos(nxt, c2, gx_index, gy_index, ye, yo, xe, xo):
+        total = None
+        for k in range(r + 1, REACH + 1):
+            term = w[k] * layers[(k - r - 1) if high else (REACH + r - k)]
+            total = term if total is None else total + term
+        nxt[x, :, :] = nxt[x, :, :] + c2[x, :, :] * total
+
+
+def add_halos(nxt, c2, gx_index, gy_index, ye, yo, xe, xo, stage):
     for axis, index, even, odd, add in (("gy", gy_index, ye, yo, add_y_halo), ("gx", gx_index, xe, xo, add_x_halo)):
         is_even = index % 2 == 0
         inner = jnp.logical_and(index > 0, index < lax.axis_size(axis) - 1)
 
         @pl.when(is_even)
         def _(even=even, add=add):
-            add(nxt, c2, even, True)
+            add(nxt, c2, even, stage, True)
 
         @pl.when(jnp.logical_not(is_even))
         def _(even=even, add=add):
-            add(nxt, c2, even, False)
+            add(nxt, c2, even, stage, False)
 
         if odd is not None:
 
             @pl.when(jnp.logical_and(inner, is_even))
             def _(odd=odd, add=add):
-                add(nxt, c2, odd, False)
+                add(nxt, c2, odd, stage, False)
 
             @pl.when(jnp.logical_and(inner, jnp.logical_not(is_even)))
             def _(odd=odd, add=add):
-                add(nxt, c2, odd, True)
+                add(nxt, c2, odd, stage, True)
 
 
 def load_kernel(
-    cur_in, col_in, rb_in, traces_in, counts, cur, ye, yo, xe, toeplitz, select, owners, own, col, rb, traces, sems,
-    *, with_yo, each, rblk,
+    cur_in, col_in, rb_in, traces_in, counts, cur, toeplitz, select, owners, own, *refs,
+    with_yo, with_xo, each, rblk,
 ):
+    ye, yo, xe, xo, (col, rb, traces, stage, sems) = unpack(refs, with_yo, with_xo)
     gx_index, gy_index = lax.axis_index("gx"), lax.axis_index("gy")
     pairs = ((cur_in, cur), (col_in, col), (rb_in, rb), (traces_in, traces))
     copies = [pltpu.make_async_copy(src, dst, sems.at[i]) for i, (src, dst) in enumerate(pairs)]
@@ -198,7 +210,7 @@
     own[...] = jnp.zeros(own.shape, F32)
     own[0, 0:steps, 0:per] = traces[0].astype(F32)
     copies[0].wait()
-    put_faces(cur, gx_index, gy_index, ye, yo if with_yo else None, xe, None)
+    put_faces(cur, gx_index, gy_index, ye, yo, xe, xo, stage)
 
 
 def slot_owners(rb, counts, owners, each, rblk):
@@ -343,14 +355,15 @@
     pairs, refs = refs[0], refs[1:]
     nxt, contrib, refs = refs[0], refs[1], refs[2:]
     oye, oyo, oxe, oxo, refs = unpack(refs, with_yo, with_xo)
-    wide = refs[0]
+    wide, stage = refs
     lanes = 128
     tiles = []
-    n = pairs.shape[0]
-    y_last, x_last = ye.shape[0] - n, xe.shape[0] - 2 * n
-    for ref, first in ((pairs, 0), (ye, y_last), (xe, x_last), (xe, x_last + n)):
-        for i in range(n):
-            tiles += [ref[first + i][:, 0:lanes], ref[first + i][:, lanes : 2 * lanes]]
+    rows = pairs.shape[0]
+    y_last, x_last = ye.shape[0] - rows, xe.shape[0] - 2 * rows
+    for block in (pairs[...], ye[y_last : y_last + rows, :], xe[x_last : x_last + 2 * rows, :]):
+        block = block.astype(F32)
+        for i in range(0, block.shape[0], 8):
+            tiles += [block[i : i + 8, 0:lanes], block[i : i + 8, lanes : 2 * lanes]]
     contributions(owners, weights, tiles, patterns, contrib, wide)
     cx, cy, nz = nxt.shape
     chunk = 8
@@ -359,27 +372,27 @@
         src = dot(select[m * rows : (m + 1) * rows, :], contrib[0])
         at = slice(m * chunk, (m + 1) * chunk)
         nxt[at, :, :] = part[at, :, :] + src.reshape(chunk, cy, nz)
-    add_halos(nxt, c2, gx_index, gy_index, ye, yo, xe, xo)
-    put_faces(nxt, gx_index, gy_index, oye, oyo, oxe, oxo)
+    add_halos(nxt, c2, gx_index, gy_index, ye, yo, xe, xo, stage)
+    put_faces(nxt, gx_index, gy_index, oye, oyo, oxe, oxo, stage)
 
 
 def correct_kernel(part, c2, *refs, with_yo, with_xo):
     gx_index, gy_index = lax.axis_index("gx"), lax.axis_index("gy")
     ye, yo, xe, xo, refs = unpack(refs, with_yo, with_xo)
     nxt, refs = refs[0], refs[1:]
-    oye, oyo, oxe, oxo, refs = unpack(refs, with_yo, with_xo)
+    oye, oyo, oxe, oxo, (stage,) = unpack(refs, with_yo, with_xo)
     nxt[...] = part[...]
-    add_halos(nxt, c2, gx_index, gy_index, ye, yo, xe, xo)
-    put_faces(nxt, gx_index, gy_index, oye, oyo, oxe, oxo)
+    add_halos(nxt, c2, gx_index, gy_index, ye, yo, xe, xo, stage)
+    put_faces(nxt, gx_index, gy_index, oye, oyo, oxe, oxo, stage)
 
 
 def last_kernel(part, c2, accel, fine, *refs, with_yo, with_xo, step):
     gx_index, gy_index = lax.axis_index("gx"), lax.axis_index("gy")
     ye, yo, xe, xo, refs = unpack(refs, with_yo, with_xo)
-    nxt, coarse, middle = refs
+    nxt, coarse, middle, stage = refs
     cx, cy, nz = nxt.shape
     nxt[...] = part[...]
-    add_halos(nxt, c2, gx_index, gy_index, ye, yo, xe, xo)
+    add_halos(nxt, c2, gx_index, gy_index, ye, yo, xe, xo, stage)
     pairs = lax.div(lax.broadcasted_iota(jnp.int32, (nz, nz // 2), 0), jnp.int32(2)) == lax.broadcasted_iota(
         jnp.int32, (nz, nz // 2), 1
     )
@@ -408,7 +421,7 @@
     per = traces.shape[2]
     nx, ny, nshot = lax.axis_size("gx"), lax.axis_size("gy"), lax.axis_size("shot")
     with_yo, with_xo = ny > 2, nx > 2
-    y_msg, x_msg = (cx // 2, 8, nz), (REACH * cy // 8, 8, nz)
+    y_msg, x_msg = ((REACH + 1) * cx, nz), ((REACH + 1) * cy, nz)
     tile = (cx, cy, nz)
     cells = cx * cy * nz
     lanes = 128
@@ -418,6 +431,21 @@
 
     def xor(size, bit):
         return [(i, i ^ bit) for i in range(size)]
+
+    def given(ye, yo, xe, xo):
+        return [a for a in (ye, yo, xe, xo) if a is not None]
+
+    def face_shapes():
+        y, x = sds(y_msg, BF16), sds(x_msg, BF16)
+        return given(y, y if with_yo else None, x, x if with_xo else None)
+
+    def taken(faces):
+        faces = list(faces)
+        ye = faces.pop(0)
+        yo = faces.pop(0) if with_yo else None
+        xe = faces.pop(0)
+        xo = faces.pop(0) if with_xo else None
+        return ye, yo, xe, xo
 
     blocks, others, patterns = traces, [], [0]
     for axis, size, stride in (("gy", ny, 1), ("gx", nx, ny)):
@@ -431,29 +459,27 @@
                 blocks = jnp.concatenate([blocks, got], axis=0)
     if not others:
         others, patterns = [jnp.zeros_like(traces)], [0, -2]
-    cur, ye, yo, xe, toeplitz, select, owners, own = vmem_call(
-        functools.partial(load_kernel, with_yo=with_yo, each=per // rblk, rblk=rblk),
+    stage = pltpu.VMEM((nz // lanes, REACH * cx, lanes), F32)
+    cur, toeplitz, select, owners, own, *faces = vmem_call(
+        functools.partial(load_kernel, with_yo=with_yo, with_xo=with_xo, each=per // rblk, rblk=rblk),
         [
-            sds(tile), sds(y_msg), sds(y_msg), sds(x_msg), sds((2 * nz, nz), BF16),
-            sds((cx * cy, 3 * slots), BF16), sds((slots, lanes), jnp.int32), sds((1, 8, lanes)),
-        ],
+            sds(tile), sds((2 * nz, nz), BF16), sds((cx * cy, 3 * slots), BF16), sds((slots, lanes), jnp.int32),
+            sds((1, 8, lanes)),
+        ] + face_shapes(),
         [adj_cur[0], column[0], rblock[0], traces, counts],
         [
             pltpu.VMEM((1, slots), jnp.int32), pltpu.VMEM((1, slots), jnp.int32), pltpu.VMEM((1, steps, per), BF16),
-            pltpu.SemaphoreType.DMA((4,)),
+            stage, pltpu.SemaphoreType.DMA((4,)),
         ],
         hbm_in=(0, 1, 2, 3), smem_in=(4,),
     )
+    ye, yo, xe, xo = taken(faces)
     others = [jnp.pad(a.astype(F32), ((0, 0), (0, 8 - steps), (0, lanes - per))) for a in others]
     tiles = jnp.concatenate([own] + others, axis=0)
-    pairs = jnp.concatenate([tiles[0::2], tiles[1::2]], axis=2)
+    pairs = jnp.concatenate([tiles[0::2], tiles[1::2]], axis=2).astype(BF16).reshape(-1, nz)
     rye = swap(jnp.concatenate([ye, pairs], axis=0), "gy", even_pairs(ny))
     ryo = swap(yo, "gy") if with_yo else None
-    rxo = None
-    if with_xo:
-        low = cur[0:REACH].reshape(x_msg)
-        high = cur[cx - REACH :].reshape(x_msg)
-        rxo = swap(jnp.where(lax.axis_index("gx") % 2 == 0, low, high), "gx")
+    rxo = swap(xo, "gx") if with_xo else None
     rxe = swap(jnp.concatenate([xe, pairs, rye[y_msg[0] :]], axis=0), "gx", even_pairs(nx))
     for stride in (1, ny):
         patterns = patterns + [p ^ stride if p >= 0 else p for p in patterns]
@@ -467,27 +493,13 @@
         hbm_in=(2, 3, 4), flops=cells * 60,
     )
 
-    def given(ye, yo, xe, xo):
-        return [a for a in (ye, yo, xe, xo) if a is not None]
-
-    def face_shapes():
-        return given(sds(y_msg), sds(y_msg) if with_yo else None, sds(x_msg), sds(x_msg) if with_xo else None)
-
-    def taken(faces):
-        faces = list(faces)
-        ye = faces.pop(0)
-        yo = faces.pop(0) if with_yo else None
-        xe = faces.pop(0)
-        xo = faces.pop(0) if with_xo else None
-        return ye, yo, xe, xo
-
     nxt, contrib, *faces = vmem_call(
         functools.partial(
             first_correct_kernel, with_yo=with_yo, with_xo=with_xo, patterns=tuple(patterns)
         ),
         [sds(tile), sds((steps, 3 * slots, nz), BF16)] + face_shapes(),
         [owners, wts, select, part, c2] + given(rye, ryo, rxe, rxo) + [pairs],
-        [pltpu.VMEM((steps, slots, nz), F32)],
+        [pltpu.VMEM((steps, slots, nz), F32), stage],
     )
     previous, current = cur, nxt
     fine = None
@@ -510,13 +522,14 @@
                 functools.partial(correct_kernel, with_yo=with_yo, with_xo=with_xo),
                 [sds(tile)] + face_shapes(),
                 [part, c2] + halos,
+                [stage],
             )
         else:
             nxt, coarse = vmem_call(
                 functools.partial(last_kernel, with_yo=with_yo, with_xo=with_xo, step=step),
                 [sds(tile), sds((cx // 2, cy // 2, nz // 2))],
                 [part, c2, accel, fine] + halos,
-                [pltpu.VMEM((cx * cy // 2, nz // 2), F32)],
+                [pltpu.VMEM((cx * cy // 2, nz // 2), F32), stage],
             )
         previous, current = current, nxt
     bit = 1

time: 42.4 us -> 41.2 us (0.972)
  waiting for transfers between devices: 10.2 us -> 8.91 us
    ppermute x12, waiting for transfers between devices: 10.1 us -> 8.89 us  [swap(): return odd_swap(x, axis) if pairs is None else lax.ppermute(x, axis, pairs)]
  transfers between devices with their start and end apart: 16 -> 16, of which waited for: 6 -> 6; matrix products, arithmetic and copies ran while one was open for 0% -> 0% of each run, Pallas kernels for 20% -> 21%
where the time goes in v3:
time: 41.2 us; the launch traced here: 41.1 us
  starting transfers between devices  19.5 us (47%)
  Pallas kernels  10.5 us (25%)
  waiting for transfers between devices  8.91 us (22%)
  between operations  1.43 us (3%)
  other arithmetic  0.67 us (2%)
    ppermute x12, starting transfers between devices, swap(): return odd_swap(x, axis) if pairs is None else lax.ppermute(x, axis, pairs)  14.9 us
    pallas_call x10, Pallas kernels, vmem_call(): pl.pallas_call(kernel, out_shape=tuple(outs), in_specs=in_specs, out_spec...  10.5 us
    ppermute x12, waiting for transfers between devices, swap(): return odd_swap(x, axis) if pairs is None else lax.ppermute(x, axis, pairs)  8.89 us
    ppermute x4, starting transfers between devices, odd_swap(): return lax.ppermute(x, (axis, 'shot'), pairs)  4.67 us
  transfers between devices with their start and end apart: 16, of which 6 were waited for; matrix products, arithmetic and copies ran while one was open for 0% of the time, Pallas kernels for 21%

profile of v3, /device:TPU:0, one launch (start us, length us, event | category | flops | bytes accessed | tf_op | source)
XLA Modules:
  0.0 41.1 jit_solution(3493984139165556784)
XLA Ops:
  0.6 3.0 %collective-permute-start = (bf16[1,4,64]{2,1,0:T(4,128)(2,1)}, bf16[1,4,64]{2,1,0:T(4,128)(2,1)S(1)}, u32[]{:S(2)}, u32[]{:S(2)}) collective-permute-start(bf16[1,4,64]{2,1,0:T(4,128)(2,1)} %traces_in.1), channel_id=1, source_target_pairs={{0,8},{4,12},{8,0},{12,4},{1,9},{5,13},{9,1},{13,5},{2,10},{6,14},... | collective-permute-start | bytes 1544 | tf_op jit(solution)/shard_map/ppermute | solution.py:430
  4.3 1.2 %shard_map.112 = (f32[32,16,256]{2,1,0:T(8,128)S(1)}, bf16[512,256]{1,0:T(8,128)(2,1)S(1)}, bf16[512,192]{1,0:T(8,128)(2,1)S(1)}, s32[64,128]{1,0:T(8,128)S(1)},...) custom-call(f32[32,16,256]{2,1,0:T(8,128)} %bitcast.16, ...), custom_call_target="tpu_custom_call" | custom-call | bytes 1750020 | tf_op jit(solution)/shard_map/pallas_call | solution.py:26
  5.7 2.0 %collective-permute-start.2 = (bf16[160,256]{1,0:T(8,128)(2,1)S(1)}, bf16[160,256]{1,0:T(8,128)(2,1)S(1)}, u32[]{:S(2)}, u32[]{:S(2)}) collective-permute-start(bf16[160,256]{1,0:T(8,128)(2,1)S(1)} %get-tuple-element.46), channel_id=1, source_target_pairs={{0,1},{12,13},{4,8},{8,4},{1,0},{13,12},{5,9},{9,5},{2,3},{14,15},... | collective-permute-start | bytes 245768 | tf_op jit(solution)/shard_map/ppermute | solution.py:63
  7.7 2.2 %shard_map.113 = (f32[32,16,256]{2,1,0:T(8,128)S(1)}, f32[32,16,256]{2,1,0:T(8,128)}, f32[32,16,256]{2,1,0:T(8,128)S(1)}, bf16[64,16,256]{2,1,0:T(8,128)(2,1)S(1)}) custom-call(f32[32,16,256]{2,1,0:T(8,128)S(1)} %get-tuple-element.38.cur.prev, bf16[512,256]{1,0:T(8,128)(2,1)S(1)} %get-tuple-element.39.toeplitz, f32[32,16,256]{2,1,0:T(8,128)} %bitcast.17, ...), custom_call_target="tpu_custom_call" | custom-call | flops 7864320 | bytes 4456448 | tf_op jit(solution)/shard_map/pallas_call | solution.py:26
  9.9 1.6 %collective-permute-start.3 = (bf16[96,256]{1,0:T(8,128)(2,1)S(1)}, bf16[96,256]{1,0:T(8,128)(2,1)S(1)}, u32[]{:S(2)}, u32[]{:S(2)}) collective-permute-start(bf16[96,256]{1,0:T(8,128)(2,1)S(1)} %pad_maximum_fusion), channel_id=1, source_target_pairs={{0,16},{16,0},{1,17},{17,1},{2,18},{18,2},{3,19},{19,3},{4,20},{20... | collective-permute-start | bytes 147464 | tf_op jit(solution)/shard_map/ppermute | solution.py:430
  11.5 2.6 %collective-permute-done.3.refs_2_ = bf16[96,256]{1,0:T(8,128)(2,1)S(1)} collective-permute-done((bf16[96,256]{1,0:T(8,128)(2,1)S(1)}, bf16[96,256]{1,0:T(8,128)(2,1)S(1)}, u32[]{:S(2)}, u32[]{:S(2)}) %collective-permute-start.3) | collective-permute-done | bytes 49184 | tf_op jit(solution)/shard_map/ppermute | solution.py:430
  14.1 0.8 %shard_map.114 = (f32[32,16,256]{2,1,0:T(8,128)S(1)}, bf16[4,192,256]{2,1,0:T(8,128)(2,1)S(1)}, bf16[160,256]{1,0:T(8,128)(2,1)S(1)}, bf16[160,256]{1,0:T(8,128)(2,1)S(1)}, bf16[80,256]{1,0:T(8,128)(2,1)S(1)}) custom-call(s32[64,128]{1,0:T(8,128)S(1)} %get-tuple-element.37.owners, bf16[64,16,256]{2,1,0:T(8,128)(2,1)S(1)} %get-tuple-element.40.weights, ...), custom_call_target="tpu_custom_call" | custom-call | bytes 3145728 | tf_op jit(solution)/shard_map/pallas_call | solution.py:26
  15.5 2.0 %collective-permute-start.6 = (bf16[80,256]{1,0:T(8,128)(2,1)S(1)}, bf16[80,256]{1,0:T(8,128)(2,1)S(1)}, u32[]{:S(2)}, u32[]{:S(2)}) collective-permute-start(bf16[80,256]{1,0:T(8,128)(2,1)S(1)} %get-tuple-element.53), channel_id=1, source_target_pairs={{0,16},{16,0},{1,17},{17,1},{2,18},{18,2},{3,19},{19,3},{4,20},{20... | collective-permute-start | bytes 122888 | tf_op jit(solution)/shard_map/ppermute | solution.py:430
  17.5 1.5 %shard_map.115 = (f32[32,16,256]{2,1,0:T(8,128)S(1)}, f32[32,16,256]{2,1,0:T(8,128)S(1)}) custom-call(f32[32,16,256]{2,1,0:T(8,128)S(1)} %get-tuple-element.48.cur.prev, f32[32,16,256]{2,1,0:T(8,128)S(1)} %get-tuple-element.38.cur.prev, f32[32,16,256]{2,1,0:T(8,128)S(1)} %get-tuple-element.43.c2, bf16[512,256]{1,0:T(8,128)(2,1)S(1)} %get-tuple-element.39.toeplitz, ...), custom_call_target="tpu_custom_call" | custom-call | flops 7864320 | bytes 4521984 | tf_op jit(solution)/shard_map/pallas_call | solution.py:26
  19.0 0.6 %collective-permute-done.6.refs_2_ = bf16[80,256]{1,0:T(8,128)(2,1)S(1)} collective-permute-done((bf16[80,256]{1,0:T(8,128)(2,1)S(1)}, bf16[80,256]{1,0:T(8,128)(2,1)S(1)}, u32[]{:S(2)}, u32[]{:S(2)}) %collective-permute-start.6) | collective-permute-done | bytes 40992 | tf_op jit(solution)/shard_map/ppermute | solution.py:430
  20.1 1.5 %collective-permute-start.8 = (bf16[160,256]{1,0:T(8,128)(2,1)S(1)}, bf16[160,256]{1,0:T(8,128)(2,1)S(1)}, u32[]{:S(2)}, u32[]{:S(2)}) collective-permute-start(bf16[160,256]{1,0:T(8,128)(2,1)S(1)} %get-tuple-element.58), channel_id=1, source_target_pairs={{0,1},{12,13},{4,8},{8,4},{1,0},{13,12},{5,9},{9,5},{2,3},{14,15},... | collective-permute-start | bytes 245768 | tf_op jit(solution)/shard_map/ppermute | solution.py:63
  21.5 1.5 %collective-permute-start.9 = (bf16[80,256]{1,0:T(8,128)(2,1)S(1)}, bf16[80,256]{1,0:T(8,128)(2,1)S(1)}, u32[]{:S(2)}, u32[]{:S(2)}) collective-permute-start(bf16[80,256]{1,0:T(8,128)(2,1)S(1)} %get-tuple-element.59), channel_id=1, source_target_pairs={{0,16},{16,0},{1,17},{17,1},{2,18},{18,2},{3,19},{19,3},{4,20},{20... | collective-permute-start | bytes 122888 | tf_op jit(solution)/shard_map/ppermute | solution.py:430
  23.1 1.4 %shard_map.117 = (f32[32,16,256]{2,1,0:T(8,128)S(1)}, f32[32,16,256]{2,1,0:T(8,128)S(1)}) custom-call(f32[32,16,256]{2,1,0:T(8,128)S(1)} %get-tuple-element.54.cur.prev, f32[32,16,256]{2,1,0:T(8,128)S(1)} %get-tuple-element.48.cur.prev, f32[32,16,256]{2,1,0:T(8,128)S(1)} %get-tuple-element.43.c2, bf16[512,256]{1,0:T(8,128)(2,1)S(1)} %get-tuple-element.39.toeplitz, ...), custom_call_target="tpu_custom_call" | custom-call | flops 7864320 | bytes 5046272 | tf_op jit(solution)/shard_map/pallas_call | solution.py:26
  24.5 1.0 %collective-permute-done.9.refs_2_ = bf16[80,256]{1,0:T(8,128)(2,1)S(1)} collective-permute-done((bf16[80,256]{1,0:T(8,128)(2,1)S(1)}, bf16[80,256]{1,0:T(8,128)(2,1)S(1)}, u32[]{:S(2)}, u32[]{:S(2)}) %collective-permute-start.9) | collective-permute-done | bytes 40992 | tf_op jit(solution)/shard_map/ppermute | solution.py:430
  25.9 0.6 %collective-permute-start.11 = (bf16[160,256]{1,0:T(8,128)(2,1)S(1)}, bf16[160,256]{1,0:T(8,128)(2,1)S(1)}, u32[]{:S(2)}, u32[]{:S(2)}) collective-permute-start(bf16[160,256]{1,0:T(8,128)(2,1)S(1)} %get-tuple-element.65), channel_id=1, source_target_pairs={{0,1},{12,13},{4,8},{8,4},{1,0},{13,12},{5,9},{9,5},{2,3},{14,15},... | collective-permute-start | bytes 245768 | tf_op jit(solution)/shard_map/ppermute | solution.py:63
  26.5 1.8 %collective-permute-start.12 = (bf16[80,256]{1,0:T(8,128)(2,1)S(1)}, bf16[80,256]{1,0:T(8,128)(2,1)S(1)}, u32[]{:S(2)}, u32[]{:S(2)}) collective-permute-start(bf16[80,256]{1,0:T(8,128)(2,1)S(1)} %get-tuple-element.66), channel_id=1, source_target_pairs={{0,16},{16,0},{1,17},{17,1},{2,18},{18,2},{3,19},{19,3},{4,20},{20... | collective-permute-start | bytes 122888 | tf_op jit(solution)/shard_map/ppermute | solution.py:430
  28.4 1.4 %shard_map.119 = (f32[32,16,256]{2,1,0:T(8,128)S(1)}, f32[32,16,256]{2,1,0:T(8,128)S(1)}) custom-call(f32[32,16,256]{2,1,0:T(8,128)S(1)} %get-tuple-element.60.cur.a_in, f32[32,16,256]{2,1,0:T(8,128)S(1)} %get-tuple-element.54.cur.prev, f32[32,16,256]{2,1,0:T(8,128)S(1)} %get-tuple-element.43.c2, bf16[512,256]{1,0:T(8,128)(2,1)S(1)} %get-tuple-element.39.toeplitz, ...), custom_call_target="tpu_custom_call" | custom-call | flops 7864320 | bytes 5046272 | tf_op jit(solution)/shard_map/pallas_call | solution.py:26
  29.8 0.7 %collective-permute-done.12.refs_2_ = bf16[80,256]{1,0:T(8,128)(2,1)S(1)} collective-permute-done((bf16[80,256]{1,0:T(8,128)(2,1)S(1)}, bf16[80,256]{1,0:T(8,128)(2,1)S(1)}, u32[]{:S(2)}, u32[]{:S(2)}) %collective-permute-start.12) | collective-permute-done | bytes 40992 | tf_op jit(solution)/shard_map/ppermute | solution.py:430
  31.0 3.5 %collective-permute-start.15 = (f32[16,8,128]{2,1,0:T(8,128)S(1)}, f32[16,8,128]{2,1,0:T(8,128)S(1)}, u32[]{:S(2)}, u32[]{:S(2)}) collective-permute-start(f32[16,8,128]{2,1,0:T(8,128)S(1)} %get-tuple-element.70), channel_id=1, source_target_pairs={{0,3},{1,2},{2,1},{3,0},{4,7},{5,6},{6,5},{7,4},{8,11},{9,10},{10,... | collective-permute-start | bytes 196616 | tf_op jit(solution)/shard_map/ppermute | solution.py:430
  34.5 0.9 %collective-permute-start.13 = (f32[16,8,128]{2,1,0:T(8,128)S(1)}, f32[16,8,128]{2,1,0:T(8,128)S(1)}, u32[]{:S(2)}, u32[]{:S(2)}) collective-permute-start(f32[16,8,128]{2,1,0:T(8,128)S(1)} %get-tuple-element.70), channel_id=1, source_target_pairs={{0,1},{1,0},{2,3},{3,2},{4,5},{5,4},{6,7},{7,6},{8,9},{9,8},{10,11... | collective-permute-start | bytes 196616 | tf_op jit(solution)/shard_map/ppermute | solution.py:430
  35.4 1.0 %shard_map.121 = (f32[32,16,256]{2,1,0:T(8,128)}, f32[32,16,256]{2,1,0:T(8,128)}) custom-call(f32[32,16,256]{2,1,0:T(8,128)S(1)} %get-tuple-element.60.cur.a_in, f32[32,16,256]{2,1,0:T(8,128)S(1)} %get-tuple-element.67.b_in), custom_call_target="tpu_custom_call" | custom-call | bytes 2097152 | tf_op jit(solution)/shard_map/pallas_call | solution.py:26
  36.4 0.9 %collective-permute-done.15 = f32[16,8,128]{2,1,0:T(8,128)S(1)} collective-permute-done((f32[16,8,128]{2,1,0:T(8,128)S(1)}, f32[16,8,128]{2,1,0:T(8,128)S(1)}, u32[]{:S(2)}, u32[]{:S(2)}) %collective-permute-start.15) | collective-permute-done | bytes 65568 | tf_op jit(solution)/shard_map/ppermute | solution.py:430
  37.3 3.1 %collective-permute-done.14 = f32[16,8,128]{2,1,0:T(8,128)S(1)} collective-permute-done((f32[16,8,128]{2,1,0:T(8,128)S(1)}, f32[16,8,128]{2,1,0:T(8,128)S(1)}, u32[]{:S(2)}, u32[]{:S(2)}) %collective-permute-start.14) | collective-permute-done | bytes 65568 | tf_op jit(solution)/shard_map/ppermute | solution.py:430
  40.4 0.6 %add_add_fusion = f32[16,8,128]{2,1,0:T(8,128)} fusion(f32[16,8,128]{2,1,0:T(8,128)S(1)} %collective-permute-done.14, f32[16,8,128]{2,1,0:T(8,128)S(1)} %collective-permute-done.15, f32[16,8,128]{2,1,0:T(8,128)S(1)} %get-tuple-element.70, f32[16,8,128]{2,1,0:T(8,128)S(1)} %collective-permute-done.13), kind=kLoop, calls=%fused_computation.1 | loop fusion | flops 49152 | bytes 327680 | tf_op jit(solution)/shard_map/add | solution.py:541
  (27 shorter events, 2.0 us)
Async XLA Ops:
  0.6 4.9 %collective-permute-start = (bf16[1,4,64]{2,1,0:T(4,128)(2,1)}, bf16[1,4,64]{2,1,0:T(4,128)(2,1)S(1)}, u32[]{:S(2)}, u32[]{:S(2)}) collective-permute-start(bf16[1,4,64]{2,1,0:T(4,128)(2,1)} %traces_in.1), channel_id=1, source_target_pairs={{0,8},{4,12},{8,0},{12,4},{1,9},{5,13},{9,1},{13,5},{2,10},{6,14},... | collective-permute-start | bytes 1544 | tf_op jit(solution)/shard_map/ppermute | solution.py:430
  5.6 4.3 %collective-permute-start.1 = (bf16[168,256]{1,0:T(8,128)(2,1)S(1)}, bf16[168,256]{1,0:T(8,128)(2,1)S(1)}, u32[]{:S(2)}, u32[]{:S(2)}) collective-permute-start(bf16[168,256]{1,0:T(8,128)(2,1)S(1)} %maximum_maximum_fusion), channel_id=1, source_target_pairs={{0,4},{4,0},{8,12},{12,8},{1,5},{5,1},{9,13},{13,9},{2,6},{6,2},{1... | collective-permute-start | bytes 258056 | tf_op jit(solution)/shard_map/ppermute | solution.py:430
  5.7 5.9 %collective-permute-start.2 = (bf16[160,256]{1,0:T(8,128)(2,1)S(1)}, bf16[160,256]{1,0:T(8,128)(2,1)S(1)}, u32[]{:S(2)}, u32[]{:S(2)}) collective-permute-start(bf16[160,256]{1,0:T(8,128)(2,1)S(1)} %get-tuple-element.46), channel_id=1, source_target_pairs={{0,1},{12,13},{4,8},{8,4},{1,0},{13,12},{5,9},{9,5},{2,3},{14,15},... | collective-permute-start | bytes 245768 | tf_op jit(solution)/shard_map/ppermute | solution.py:63
  9.9 4.2 %collective-permute-start.3 = (bf16[96,256]{1,0:T(8,128)(2,1)S(1)}, bf16[96,256]{1,0:T(8,128)(2,1)S(1)}, u32[]{:S(2)}, u32[]{:S(2)}) collective-permute-start(bf16[96,256]{1,0:T(8,128)(2,1)S(1)} %pad_maximum_fusion), channel_id=1, source_target_pairs={{0,16},{16,0},{1,17},{17,1},{2,18},{18,2},{3,19},{19,3},{4,20},{20... | collective-permute-start | bytes 147464 | tf_op jit(solution)/shard_map/ppermute | solution.py:430
  14.1 3.4 %copy-start = (bf16[1,4,32,16,256]{4,3,2,1,0:T(8,128)(2,1)S(1)}, bf16[1,4,32,16,256]{4,3,2,1,0:T(8,128)(2,1)}, u32[]{:S(2)}) copy-start(bf16[1,4,32,16,256]{4,3,2,1,0:T(8,128)(2,1)} %param.11) | copy-start | bytes 3145732
  14.9 4.6 %collective-permute-start.4 = (bf16[160,256]{1,0:T(8,128)(2,1)S(1)}, bf16[160,256]{1,0:T(8,128)(2,1)S(1)}, u32[]{:S(2)}, u32[]{:S(2)}) collective-permute-start(bf16[160,256]{1,0:T(8,128)(2,1)S(1)} %get-tuple-element.51), channel_id=1, source_target_pairs={{0,4},{4,0},{8,12},{12,8},{1,5},{5,1},{9,13},{13,9},{2,6},{6,2},{1... | collective-permute-start | bytes 245768 | tf_op jit(solution)/shard_map/ppermute | solution.py:430
  15.0 4.5 %collective-permute-start.5 = (bf16[160,256]{1,0:T(8,128)(2,1)S(1)}, bf16[160,256]{1,0:T(8,128)(2,1)S(1)}, u32[]{:S(2)}, u32[]{:S(2)}) collective-permute-start(bf16[160,256]{1,0:T(8,128)(2,1)S(1)} %get-tuple-element.52), channel_id=1, source_target_pairs={{0,1},{12,13},{4,8},{8,4},{1,0},{13,12},{5,9},{9,5},{2,3},{14,15},... | collective-permute-start | bytes 245768 | tf_op jit(solution)/shard_map/ppermute | solution.py:63
  15.5 4.0 %collective-permute-start.6 = (bf16[80,256]{1,0:T(8,128)(2,1)S(1)}, bf16[80,256]{1,0:T(8,128)(2,1)S(1)}, u32[]{:S(2)}, u32[]{:S(2)}) collective-permute-start(bf16[80,256]{1,0:T(8,128)(2,1)S(1)} %get-tuple-element.53), channel_id=1, source_target_pairs={{0,16},{16,0},{1,17},{17,1},{2,18},{18,2},{3,19},{19,3},{4,20},{20... | collective-permute-start | bytes 122888 | tf_op jit(solution)/shard_map/ppermute | solution.py:430
  19.8 5.7 %collective-permute-start.7 = (bf16[160,256]{1,0:T(8,128)(2,1)S(1)}, bf16[160,256]{1,0:T(8,128)(2,1)S(1)}, u32[]{:S(2)}, u32[]{:S(2)}) collective-permute-start(bf16[160,256]{1,0:T(8,128)(2,1)S(1)} %get-tuple-element.57), channel_id=1, source_target_pairs={{0,4},{4,0},{8,12},{12,8},{1,5},{5,1},{9,13},{13,9},{2,6},{6,2},{1... | collective-permute-start | bytes 245768 | tf_op jit(solution)/shard_map/ppermute | solution.py:430
  20.1 5.5 %collective-permute-start.8 = (bf16[160,256]{1,0:T(8,128)(2,1)S(1)}, bf16[160,256]{1,0:T(8,128)(2,1)S(1)}, u32[]{:S(2)}, u32[]{:S(2)}) collective-permute-start(bf16[160,256]{1,0:T(8,128)(2,1)S(1)} %get-tuple-element.58), channel_id=1, source_target_pairs={{0,1},{12,13},{4,8},{8,4},{1,0},{13,12},{5,9},{9,5},{2,3},{14,15},... | collective-permute-start | bytes 245768 | tf_op jit(solution)/shard_map/ppermute | solution.py:63
  21.5 4.0 %collective-permute-start.9 = (bf16[80,256]{1,0:T(8,128)(2,1)S(1)}, bf16[80,256]{1,0:T(8,128)(2,1)S(1)}, u32[]{:S(2)}, u32[]{:S(2)}) collective-permute-start(bf16[80,256]{1,0:T(8,128)(2,1)S(1)} %get-tuple-element.59), channel_id=1, source_target_pairs={{0,16},{16,0},{1,17},{17,1},{2,18},{18,2},{3,19},{19,3},{4,20},{20... | collective-permute-start | bytes 122888 | tf_op jit(solution)/shard_map/ppermute | solution.py:430
  25.8 4.7 %collective-permute-start.10 = (bf16[160,256]{1,0:T(8,128)(2,1)S(1)}, bf16[160,256]{1,0:T(8,128)(2,1)S(1)}, u32[]{:S(2)}, u32[]{:S(2)}) collective-permute-start(bf16[160,256]{1,0:T(8,128)(2,1)S(1)} %get-tuple-element.64), channel_id=1, source_target_pairs={{0,4},{4,0},{8,12},{12,8},{1,5},{5,1},{9,13},{13,9},{2,6},{6,2},{1... | collective-permute-start | bytes 245768 | tf_op jit(solution)/shard_map/ppermute | solution.py:430
  25.9 4.7 %collective-permute-start.11 = (bf16[160,256]{1,0:T(8,128)(2,1)S(1)}, bf16[160,256]{1,0:T(8,128)(2,1)S(1)}, u32[]{:S(2)}, u32[]{:S(2)}) collective-permute-start(bf16[160,256]{1,0:T(8,128)(2,1)S(1)} %get-tuple-element.65), channel_id=1, source_target_pairs={{0,1},{12,13},{4,8},{8,4},{1,0},{13,12},{5,9},{9,5},{2,3},{14,15},... | collective-permute-start | bytes 245768 | tf_op jit(solution)/shard_map/ppermute | solution.py:63
  26.5 4.0 %collective-permute-start.12 = (bf16[80,256]{1,0:T(8,128)(2,1)S(1)}, bf16[80,256]{1,0:T(8,128)(2,1)S(1)}, u32[]{:S(2)}, u32[]{:S(2)}) collective-permute-start(bf16[80,256]{1,0:T(8,128)(2,1)S(1)} %get-tuple-element.66), channel_id=1, source_target_pairs={{0,16},{16,0},{1,17},{17,1},{2,18},{18,2},{3,19},{19,3},{4,20},{20... | collective-permute-start | bytes 122888 | tf_op jit(solution)/shard_map/ppermute | solution.py:430
  31.0 6.3 %collective-permute-start.15 = (f32[16,8,128]{2,1,0:T(8,128)S(1)}, f32[16,8,128]{2,1,0:T(8,128)S(1)}, u32[]{:S(2)}, u32[]{:S(2)}) collective-permute-start(f32[16,8,128]{2,1,0:T(8,128)S(1)} %get-tuple-element.70), channel_id=1, source_target_pairs={{0,3},{1,2},{2,1},{3,0},{4,7},{5,6},{6,5},{7,4},{8,11},{9,10},{10,... | collective-permute-start | bytes 196616 | tf_op jit(solution)/shard_map/ppermute | solution.py:430
  34.5 5.9 %collective-permute-start.14 = (f32[16,8,128]{2,1,0:T(8,128)S(1)}, f32[16,8,128]{2,1,0:T(8,128)S(1)}, u32[]{:S(2)}, u32[]{:S(2)}) collective-permute-start(f32[16,8,128]{2,1,0:T(8,128)S(1)} %get-tuple-element.70), channel_id=1, source_target_pairs={{0,2},{1,3},{2,0},{3,1},{4,6},{5,7},{6,4},{7,5},{8,10},{9,11},{10,... | collective-permute-start | bytes 196616 | tf_op jit(solution)/shard_map/ppermute | solution.py:430
  34.5 5.9 %collective-permute-start.13 = (f32[16,8,128]{2,1,0:T(8,128)S(1)}, f32[16,8,128]{2,1,0:T(8,128)S(1)}, u32[]{:S(2)}, u32[]{:S(2)}) collective-permute-start(f32[16,8,128]{2,1,0:T(8,128)S(1)} %get-tuple-element.70), channel_id=1, source_target_pairs={{0,1},{1,0},{2,3},{3,2},{4,5},{5,4},{6,7},{7,6},{8,9},{9,8},{10,11... | collective-permute-start | bytes 196616 | tf_op jit(solution)/shard_map/ppermute | solution.py:430

commit v4 on v3

--- a/solution.py
+++ b/solution.py
@@ -180,8 +180,22 @@
                 add(nxt, c2, odd, stage, True)
 
 
+def put_band(out, size, span, centre):
+    row = lax.broadcasted_iota(jnp.int32, (size, size), 0)
+    column = lax.broadcasted_iota(jnp.int32, (size, size), 1)
+    distance = jnp.abs(row - column)
+    band = jnp.where(distance == 0, centre, 0.0)
+    for k in range(1, REACH + 1):
+        band = band + jnp.where(distance == k, LAPLACE_COEFS[k], 0.0)
+    if span < size:
+        band = jnp.where(lax.div(row, jnp.int32(span)) == lax.div(column, jnp.int32(span)), band, 0.0)
+    hi, lo = split2(band)
+    out[0:size, :] = hi
+    out[size : 2 * size, :] = lo
+
+
 def load_kernel(
-    cur_in, col_in, rb_in, traces_in, counts, cur, toeplitz, select, owners, own, *refs,
+    cur_in, col_in, rb_in, traces_in, counts, cur, toeplitz, blocks, select, owners, own, *refs,
     with_yo, with_xo, each, rblk,
 ):
     ye, yo, xe, xo, (col, rb, traces, stage, sems) = unpack(refs, with_yo, with_xo)
@@ -190,16 +204,9 @@
     copies = [pltpu.make_async_copy(src, dst, sems.at[i]) for i, (src, dst) in enumerate(pairs)]
     for copy in copies:
         copy.start()
-    nz = toeplitz.shape[1]
-    distance = jnp.abs(
-        lax.broadcasted_iota(jnp.int32, (nz, nz), 0) - lax.broadcasted_iota(jnp.int32, (nz, nz), 1)
-    )
-    band = jnp.where(distance == 0, 3.0 * LAPLACE_COEFS[0], 0.0)
-    for k in range(1, REACH + 1):
-        band = band + jnp.where(distance == k, LAPLACE_COEFS[k], 0.0)
-    hi, lo = split2(band)
-    toeplitz[0:nz, :] = hi
-    toeplitz[nz : 2 * nz, :] = lo
+    nz, rows, cy = toeplitz.shape[1], blocks.shape[1], cur.shape[1]
+    put_band(toeplitz, nz, nz, 3.0 * LAPLACE_COEFS[0])
+    put_band(blocks, rows, cy, 0.0)
     for copy in copies[1:]:
         copy.wait()
     wide = jnp.concatenate([col[...]] * 3, axis=1)
@@ -236,22 +243,20 @@
         copy.wait()
 
 
-def update(cur, prev, c2, toeplitz, out, ypad, source=None, fine=None):
+def update(cur, prev, c2, toeplitz, blocks, out, source=None, fine=None):
     cx, cy, nz = cur.shape
     w = LAPLACE_COEFS
-    zero = jnp.zeros((8, nz), F32)
-    for x in range(cx):
-        ypad[x, 0:8, :] = zero
-        ypad[x, 8 : 8 + cy, :] = cur[x, :, :]
-        ypad[x, 8 + cy : 16 + cy, :] = zero
     chunk = CHUNK
     rows = chunk * cy
     t_hi = toeplitz[0:nz, :]
     t_lo = toeplitz[nz : 2 * nz, :]
+    b_hi = blocks[0:rows, :]
+    b_lo = blocks[rows : 2 * rows, :]
     for m in range(cx // chunk):
         v = cur[m * chunk : (m + 1) * chunk, :, :].reshape(rows, nz)
         hi, lo = split2(v)
         lz = dot(hi, t_hi) + dot(lo, t_hi) + dot(hi, t_lo)
+        lz = lz + dot(b_hi, hi) + dot(b_hi, lo) + dot(b_lo, hi)
         if source is not None:
             select, contrib = source
             src = dot(select[m * rows : (m + 1) * rows, :], contrib)
@@ -259,12 +264,9 @@
             x = m * chunk + j
             total = lz[j * cy : (j + 1) * cy, :]
             for k in range(1, REACH + 1):
-                pair = ypad[x, 8 - k : 8 - k + cy, :] + ypad[x, 8 + k : 8 + k + cy, :]
-                if x - k >= 0:
-                    pair = pair + cur[x - k, :, :]
-                if x + k < cx:
-                    pair = pair + cur[x + k, :, :]
-                total = total + w[k] * pair
+                near = [cur[i, :, :] for i in (x - k, x + k) if 0 <= i < cx]
+                if near:
+                    total = total + w[k] * (near[0] if len(near) == 1 else near[0] + near[1])
             if prev is None:
                 out[x, :, :] = total
                 continue
@@ -279,14 +281,14 @@
                 fine_out[x, :, :] = term if fine_in is None else fine_in[x, :, :] + term
 
 
-def first_update_kernel(cur, toeplitz, prev_in, c2_in, weights_in, out, prev, c2, weights, ypad, sems):
+def first_update_kernel(cur, toeplitz, blocks, prev_in, c2_in, weights_in, out, prev, c2, weights, sems):
     copies = [
         pltpu.make_async_copy(src, dst, sems.at[i])
         for i, (src, dst) in enumerate(((prev_in, prev), (c2_in, c2), (weights_in, weights)))
     ]
     for copy in copies:
         copy.start()
-    update(cur, None, None, toeplitz, out, ypad)
+    update(cur, None, None, toeplitz, blocks, out)
     copies[0].wait()
     copies[1].wait()
     for x in range(cur.shape[0]):
@@ -294,14 +296,14 @@
     copies[2].wait()
 
 
-def update_kernel(cur, prev, c2, toeplitz, select, contrib, accel, *rest, step):
+def update_kernel(cur, prev, c2, toeplitz, blocks, select, contrib, accel, *rest, step):
     if step == 1:
-        out, fine_out, ypad = rest
+        out, fine_out = rest
         fine_in = None
     else:
-        fine_in, out, fine_out, ypad = rest
+        fine_in, out, fine_out = rest
     update(
-        cur, prev, c2, toeplitz, out, ypad,
+        cur, prev, c2, toeplitz, blocks, out,
         source=(select, contrib[step]), fine=(fine_in, accel.at[step - 1], fine_out),
     )
 
@@ -460,11 +462,11 @@
     if not others:
         others, patterns = [jnp.zeros_like(traces)], [0, -2]
     stage = pltpu.VMEM((nz // lanes, REACH * cx, lanes), F32)
-    cur, toeplitz, select, owners, own, *faces = vmem_call(
+    cur, toeplitz, bands, select, owners, own, *faces = vmem_call(
         functools.partial(load_kernel, with_yo=with_yo, with_xo=with_xo, each=per // rblk, rblk=rblk),
         [
-            sds(tile), sds((2 * nz, nz), BF16), sds((cx * cy, 3 * slots), BF16), sds((slots, lanes), jnp.int32),
-            sds((1, 8, lanes)),
+            sds(tile), sds((2 * nz, nz), BF16), sds((2 * CHUNK * cy, CHUNK * cy), BF16),
+            sds((cx * cy, 3 * slots), BF16), sds((slots, lanes), jnp.int32), sds((1, 8, lanes)),
         ] + face_shapes(),
         [adj_cur[0], column[0], rblock[0], traces, counts],
         [
@@ -484,13 +486,12 @@
     for stride in (1, ny):
         patterns = patterns + [p ^ stride if p >= 0 else p for p in patterns]
 
-    ypad = pltpu.VMEM((cx, cy + 16, nz), F32)
     part, _, c2, wts = vmem_call(
         first_update_kernel,
         [sds(tile), sds(tile), sds(tile), sds((slots, rblk, nz), BF16)],
-        [cur, toeplitz, adj_prev[0], courant2, weights[0, 0]],
-        [ypad, pltpu.SemaphoreType.DMA((3,))],
-        hbm_in=(2, 3, 4), flops=cells * 60,
+        [cur, toeplitz, bands, adj_prev[0], courant2, weights[0, 0]],
+        [pltpu.SemaphoreType.DMA((3,))],
+        hbm_in=(3, 4, 5), flops=cells * 60,
     )
 
     nxt, contrib, *faces = vmem_call(
@@ -509,11 +510,11 @@
         rxe = swap(xe, "gx", even_pairs(nx))
         rxo = swap(xo, "gx") if with_xo else None
         rye = swap(ye, "gy", even_pairs(ny))
-        args = [current, previous, c2, toeplitz, select, contrib, accel]
+        args = [current, previous, c2, toeplitz, bands, select, contrib, accel]
         if fine is not None:
             args.append(fine)
         part, fine = vmem_call(
-            functools.partial(update_kernel, step=step), [sds(tile), sds(tile)], args, [ypad],
+            functools.partial(update_kernel, step=step), [sds(tile), sds(tile)], args,
             flops=cells * 60,
         )
         halos = given(rye, ryo, rxe, rxo)

time: 41.2 us -> 41.2 us (level)
  waiting for transfers between devices: 8.91 us -> 10.8 us
  Pallas kernels: 10.5 us -> 8.64 us
    ppermute x12, waiting for transfers between devices: 8.89 us -> 10.8 us  [swap(): return odd_swap(x, axis) if pairs is None else lax.ppermute(x, axis, pairs)]
    pallas_call x10, Pallas kernels: 10.5 us -> 8.64 us  [vmem_call(): pl.pallas_call(kernel, out_shape=tuple(outs), in_specs=in_specs, out_spec...]
  transfers between devices with their start and end apart: 16 -> 16, of which waited for: 6 -> 6; matrix products, arithmetic and copies ran while one was open for 0% -> 0% of each run, Pallas kernels for 21% -> 17%
where the time goes in v4:
time: 41.2 us; the launch traced here: 41.1 us
  starting transfers between devices  19.5 us (47%)
  waiting for transfers between devices  10.8 us (26%)
  Pallas kernels  8.64 us (21%)
  between operations  1.43 us (3%)
  other arithmetic  0.67 us (2%)
    ppermute x12, starting transfers between devices, swap(): return odd_swap(x, axis) if pairs is None else lax.ppermute(x, axis, pairs)  14.9 us
    ppermute x12, waiting for transfers between devices, swap(): return odd_swap(x, axis) if pairs is None else lax.ppermute(x, axis, pairs)  10.8 us
    pallas_call x10, Pallas kernels, vmem_call(): pl.pallas_call(kernel, out_shape=tuple(outs), in_specs=in_specs, out_spec...  8.64 us
    ppermute x4, starting transfers between devices, odd_swap(): return lax.ppermute(x, (axis, 'shot'), pairs)  4.67 us
  transfers between devices with their start and end apart: 16, of which 6 were waited for; matrix products, arithmetic and copies ran while one was open for 0% of the time, Pallas kernels for 17%

profile of v4, /device:TPU:0, one launch (start us, length us, event | category | flops | bytes accessed | tf_op | source)
XLA Modules:
  0.0 41.1 jit_solution(7697802757521065958)
XLA Ops:
  0.6 3.0 %collective-permute-start = (bf16[1,4,64]{2,1,0:T(4,128)(2,1)}, bf16[1,4,64]{2,1,0:T(4,128)(2,1)S(1)}, u32[]{:S(2)}, u32[]{:S(2)}) collective-permute-start(bf16[1,4,64]{2,1,0:T(4,128)(2,1)} %traces_in.1), channel_id=1, source_target_pairs={{0,8},{4,12},{8,0},{12,4},{1,9},{5,13},{9,1},{13,5},{2,10},{6,14},... | collective-permute-start | bytes 1544 | tf_op jit(solution)/shard_map/ppermute | solution.py:432
  4.3 1.2 %shard_map.112 = (f32[32,16,256]{2,1,0:T(8,128)S(1)}, bf16[512,256]{1,0:T(8,128)(2,1)S(1)}, bf16[256,128]{1,0:T(8,128)(2,1)S(1)}, bf16[512,192]{1,0:T(8,128)(2,1...) custom-call(f32[32,16,256]{2,1,0:T(8,128)} %bitcast.18, ...), custom_call_target="tpu_custom_call" | custom-call | bytes 1815556 | tf_op jit(solution)/shard_map/pallas_call | solution.py:26
  5.7 2.0 %collective-permute-start.2 = (bf16[160,256]{1,0:T(8,128)(2,1)S(1)}, bf16[160,256]{1,0:T(8,128)(2,1)S(1)}, u32[]{:S(2)}, u32[]{:S(2)}) collective-permute-start(bf16[160,256]{1,0:T(8,128)(2,1)S(1)} %get-tuple-element.48), channel_id=1, source_target_pairs={{0,1},{12,13},{4,8},{8,4},{1,0},{13,12},{5,9},{9,5},{2,3},{14,15},... | collective-permute-start | bytes 245768 | tf_op jit(solution)/shard_map/ppermute | solution.py:63
  7.7 2.2 %shard_map.113 = (f32[32,16,256]{2,1,0:T(8,128)S(1)}, f32[32,16,256]{2,1,0:T(8,128)}, f32[32,16,256]{2,1,0:T(8,128)S(1)}, bf16[64,16,256]{2,1,0:T(8,128)(2,1)S(1)}) custom-call(f32[32,16,256]{2,1,0:T(8,128)S(1)} %get-tuple-element.39.cur.prev, bf16[512,256]{1,0:T(8,128)(2,1)S(1)} %get-tuple-element.40.toeplitz, ...), custom_call_target="tpu_custom_call" | custom-call | flops 7864320 | bytes 4521984 | tf_op jit(solution)/shard_map/pallas_call | solution.py:26
  10.0 1.6 %collective-permute-start.3 = (bf16[96,256]{1,0:T(8,128)(2,1)S(1)}, bf16[96,256]{1,0:T(8,128)(2,1)S(1)}, u32[]{:S(2)}, u32[]{:S(2)}) collective-permute-start(bf16[96,256]{1,0:T(8,128)(2,1)S(1)} %pad_maximum_fusion), channel_id=1, source_target_pairs={{0,16},{16,0},{1,17},{17,1},{2,18},{18,2},{3,19},{19,3},{4,20},{20... | collective-permute-start | bytes 147464 | tf_op jit(solution)/shard_map/ppermute | solution.py:432
  11.5 2.6 %collective-permute-done.3.refs_2_ = bf16[96,256]{1,0:T(8,128)(2,1)S(1)} collective-permute-done((bf16[96,256]{1,0:T(8,128)(2,1)S(1)}, bf16[96,256]{1,0:T(8,128)(2,1)S(1)}, u32[]{:S(2)}, u32[]{:S(2)}) %collective-permute-start.3) | collective-permute-done | bytes 49184 | tf_op jit(solution)/shard_map/ppermute | solution.py:432
  14.1 0.8 %shard_map.114 = (f32[32,16,256]{2,1,0:T(8,128)S(1)}, bf16[4,192,256]{2,1,0:T(8,128)(2,1)S(1)}, bf16[160,256]{1,0:T(8,128)(2,1)S(1)}, bf16[160,256]{1,0:T(8,128)(2,1)S(1)}, bf16[80,256]{1,0:T(8,128)(2,1)S(1)}) custom-call(s32[64,128]{1,0:T(8,128)S(1)} %get-tuple-element.38.owners, bf16[64,16,256]{2,1,0:T(8,128)(2,1)S(1)} %get-tuple-element.42.weights, ...), custom_call_target="tpu_custom_call" | custom-call | bytes 3145728 | tf_op jit(solution)/shard_map/pallas_call | solution.py:26
  15.5 2.0 %collective-permute-start.6 = (bf16[80,256]{1,0:T(8,128)(2,1)S(1)}, bf16[80,256]{1,0:T(8,128)(2,1)S(1)}, u32[]{:S(2)}, u32[]{:S(2)}) collective-permute-start(bf16[80,256]{1,0:T(8,128)(2,1)S(1)} %get-tuple-element.55), channel_id=1, source_target_pairs={{0,16},{16,0},{1,17},{17,1},{2,18},{18,2},{3,19},{19,3},{4,20},{20... | collective-permute-start | bytes 122888 | tf_op jit(solution)/shard_map/ppermute | solution.py:432
  17.5 0.8 %shard_map.115 = (f32[32,16,256]{2,1,0:T(8,128)S(1)}, f32[32,16,256]{2,1,0:T(8,128)S(1)}) custom-call(f32[32,16,256]{2,1,0:T(8,128)S(1)} %get-tuple-element.50.cur.prev, f32[32,16,256]{2,1,0:T(8,128)S(1)} %get-tuple-element.39.cur.prev, f32[32,16,256]{2,1,0:T(8,128)S(1)} %get-tuple-element.45.c2, bf16[512,256]{1,0:T(8,128)(2,1)S(1)} %get-tuple-element.40.toeplitz, ...), custom_call_target="tpu_custom_call" | custom-call | flops 7864320 | bytes 4587520 | tf_op jit(solution)/shard_map/pallas_call | solution.py:26
  18.3 1.2 %collective-permute-done.6.refs_2_ = bf16[80,256]{1,0:T(8,128)(2,1)S(1)} collective-permute-done((bf16[80,256]{1,0:T(8,128)(2,1)S(1)}, bf16[80,256]{1,0:T(8,128)(2,1)S(1)}, u32[]{:S(2)}, u32[]{:S(2)}) %collective-permute-start.6) | collective-permute-done | bytes 40992 | tf_op jit(solution)/shard_map/ppermute | solution.py:432
  20.1 1.5 %collective-permute-start.8 = (bf16[160,256]{1,0:T(8,128)(2,1)S(1)}, bf16[160,256]{1,0:T(8,128)(2,1)S(1)}, u32[]{:S(2)}, u32[]{:S(2)}) collective-permute-start(bf16[160,256]{1,0:T(8,128)(2,1)S(1)} %get-tuple-element.60), channel_id=1, source_target_pairs={{0,1},{12,13},{4,8},{8,4},{1,0},{13,12},{5,9},{9,5},{2,3},{14,15},... | collective-permute-start | bytes 245768 | tf_op jit(solution)/shard_map/ppermute | solution.py:63
  21.5 1.5 %collective-permute-start.9 = (bf16[80,256]{1,0:T(8,128)(2,1)S(1)}, bf16[80,256]{1,0:T(8,128)(2,1)S(1)}, u32[]{:S(2)}, u32[]{:S(2)}) collective-permute-start(bf16[80,256]{1,0:T(8,128)(2,1)S(1)} %get-tuple-element.61), channel_id=1, source_target_pairs={{0,16},{16,0},{1,17},{17,1},{2,18},{18,2},{3,19},{19,3},{4,20},{20... | collective-permute-start | bytes 122888 | tf_op jit(solution)/shard_map/ppermute | solution.py:432
  23.1 0.8 %shard_map.117 = (f32[32,16,256]{2,1,0:T(8,128)S(1)}, f32[32,16,256]{2,1,0:T(8,128)S(1)}) custom-call(f32[32,16,256]{2,1,0:T(8,128)S(1)} %get-tuple-element.56.cur.prev, f32[32,16,256]{2,1,0:T(8,128)S(1)} %get-tuple-element.50.cur.prev, f32[32,16,256]{2,1,0:T(8,128)S(1)} %get-tuple-element.45.c2, bf16[512,256]{1,0:T(8,128)(2,1)S(1)} %get-tuple-element.40.toeplitz, ...), custom_call_target="tpu_custom_call" | custom-call | flops 7864320 | bytes 5111808 | tf_op jit(solution)/shard_map/pallas_call | solution.py:26
  23.9 1.6 %collective-permute-done.9.refs_2_ = bf16[80,256]{1,0:T(8,128)(2,1)S(1)} collective-permute-done((bf16[80,256]{1,0:T(8,128)(2,1)S(1)}, bf16[80,256]{1,0:T(8,128)(2,1)S(1)}, u32[]{:S(2)}, u32[]{:S(2)}) %collective-permute-start.9) | collective-permute-done | bytes 40992 | tf_op jit(solution)/shard_map/ppermute | solution.py:432
  25.9 0.6 %collective-permute-start.11 = (bf16[160,256]{1,0:T(8,128)(2,1)S(1)}, bf16[160,256]{1,0:T(8,128)(2,1)S(1)}, u32[]{:S(2)}, u32[]{:S(2)}) collective-permute-start(bf16[160,256]{1,0:T(8,128)(2,1)S(1)} %get-tuple-element.67), channel_id=1, source_target_pairs={{0,1},{12,13},{4,8},{8,4},{1,0},{13,12},{5,9},{9,5},{2,3},{14,15},... | collective-permute-start | bytes 245768 | tf_op jit(solution)/shard_map/ppermute | solution.py:63
  26.6 1.8 %collective-permute-start.12 = (bf16[80,256]{1,0:T(8,128)(2,1)S(1)}, bf16[80,256]{1,0:T(8,128)(2,1)S(1)}, u32[]{:S(2)}, u32[]{:S(2)}) collective-permute-start(bf16[80,256]{1,0:T(8,128)(2,1)S(1)} %get-tuple-element.68), channel_id=1, source_target_pairs={{0,16},{16,0},{1,17},{17,1},{2,18},{18,2},{3,19},{19,3},{4,20},{20... | collective-permute-start | bytes 122888 | tf_op jit(solution)/shard_map/ppermute | solution.py:432
  28.4 0.8 %shard_map.119 = (f32[32,16,256]{2,1,0:T(8,128)S(1)}, f32[32,16,256]{2,1,0:T(8,128)S(1)}) custom-call(f32[32,16,256]{2,1,0:T(8,128)S(1)} %get-tuple-element.62.cur.a_in, f32[32,16,256]{2,1,0:T(8,128)S(1)} %get-tuple-element.56.cur.prev, f32[32,16,256]{2,1,0:T(8,128)S(1)} %get-tuple-element.45.c2, bf16[512,256]{1,0:T(8,128)(2,1)S(1)} %get-tuple-element.40.toeplitz, ...), custom_call_target="tpu_custom_call" | custom-call | flops 7864320 | bytes 5111808 | tf_op jit(solution)/shard_map/pallas_call | solution.py:26
  29.2 1.4 %collective-permute-done.12.refs_2_ = bf16[80,256]{1,0:T(8,128)(2,1)S(1)} collective-permute-done((bf16[80,256]{1,0:T(8,128)(2,1)S(1)}, bf16[80,256]{1,0:T(8,128)(2,1)S(1)}, u32[]{:S(2)}, u32[]{:S(2)}) %collective-permute-start.12) | collective-permute-done | bytes 40992 | tf_op jit(solution)/shard_map/ppermute | solution.py:432
  31.0 3.5 %collective-permute-start.15 = (f32[16,8,128]{2,1,0:T(8,128)S(1)}, f32[16,8,128]{2,1,0:T(8,128)S(1)}, u32[]{:S(2)}, u32[]{:S(2)}) collective-permute-start(f32[16,8,128]{2,1,0:T(8,128)S(1)} %get-tuple-element.72), channel_id=1, source_target_pairs={{0,3},{1,2},{2,1},{3,0},{4,7},{5,6},{6,5},{7,4},{8,11},{9,10},{10,... | collective-permute-start | bytes 196616 | tf_op jit(solution)/shard_map/ppermute | solution.py:432
  34.5 0.9 %collective-permute-start.13 = (f32[16,8,128]{2,1,0:T(8,128)S(1)}, f32[16,8,128]{2,1,0:T(8,128)S(1)}, u32[]{:S(2)}, u32[]{:S(2)}) collective-permute-start(f32[16,8,128]{2,1,0:T(8,128)S(1)} %get-tuple-element.72), channel_id=1, source_target_pairs={{0,1},{1,0},{2,3},{3,2},{4,5},{5,4},{6,7},{7,6},{8,9},{9,8},{10,11... | collective-permute-start | bytes 196616 | tf_op jit(solution)/shard_map/ppermute | solution.py:432
  35.4 1.0 %shard_map.121 = (f32[32,16,256]{2,1,0:T(8,128)}, f32[32,16,256]{2,1,0:T(8,128)}) custom-call(f32[32,16,256]{2,1,0:T(8,128)S(1)} %get-tuple-element.62.cur.a_in, f32[32,16,256]{2,1,0:T(8,128)S(1)} %get-tuple-element.69.b_in), custom_call_target="tpu_custom_call" | custom-call | bytes 2097152 | tf_op jit(solution)/shard_map/pallas_call | solution.py:26
  36.4 0.9 %collective-permute-done.15 = f32[16,8,128]{2,1,0:T(8,128)S(1)} collective-permute-done((f32[16,8,128]{2,1,0:T(8,128)S(1)}, f32[16,8,128]{2,1,0:T(8,128)S(1)}, u32[]{:S(2)}, u32[]{:S(2)}) %collective-permute-start.15) | collective-permute-done | bytes 65568 | tf_op jit(solution)/shard_map/ppermute | solution.py:432
  37.3 3.1 %collective-permute-done.14 = f32[16,8,128]{2,1,0:T(8,128)S(1)} collective-permute-done((f32[16,8,128]{2,1,0:T(8,128)S(1)}, f32[16,8,128]{2,1,0:T(8,128)S(1)}, u32[]{:S(2)}, u32[]{:S(2)}) %collective-permute-start.14) | collective-permute-done | bytes 65568 | tf_op jit(solution)/shard_map/ppermute | solution.py:432
  40.4 0.6 %add_add_fusion = f32[16,8,128]{2,1,0:T(8,128)} fusion(f32[16,8,128]{2,1,0:T(8,128)S(1)} %collective-permute-done.14, f32[16,8,128]{2,1,0:T(8,128)S(1)} %collective-permute-done.15, f32[16,8,128]{2,1,0:T(8,128)S(1)} %get-tuple-element.72, f32[16,8,128]{2,1,0:T(8,128)S(1)} %collective-permute-done.13), kind=kLoop, calls=%fused_computation.1 | loop fusion | flops 49152 | bytes 327680 | tf_op jit(solution)/shard_map/add | solution.py:542
  (27 shorter events, 2.0 us)
Async XLA Ops:
  0.6 4.9 %collective-permute-start = (bf16[1,4,64]{2,1,0:T(4,128)(2,1)}, bf16[1,4,64]{2,1,0:T(4,128)(2,1)S(1)}, u32[]{:S(2)}, u32[]{:S(2)}) collective-permute-start(bf16[1,4,64]{2,1,0:T(4,128)(2,1)} %traces_in.1), channel_id=1, source_target_pairs={{0,8},{4,12},{8,0},{12,4},{1,9},{5,13},{9,1},{13,5},{2,10},{6,14},... | collective-permute-start | bytes 1544 | tf_op jit(solution)/shard_map/ppermute | solution.py:432
  5.6 4.3 %collective-permute-start.1 = (bf16[168,256]{1,0:T(8,128)(2,1)S(1)}, bf16[168,256]{1,0:T(8,128)(2,1)S(1)}, u32[]{:S(2)}, u32[]{:S(2)}) collective-permute-start(bf16[168,256]{1,0:T(8,128)(2,1)S(1)} %maximum_maximum_fusion), channel_id=1, source_target_pairs={{0,4},{4,0},{8,12},{12,8},{1,5},{5,1},{9,13},{13,9},{2,6},{6,2},{1... | collective-permute-start | bytes 258056 | tf_op jit(solution)/shard_map/ppermute | solution.py:432
  5.7 5.9 %collective-permute-start.2 = (bf16[160,256]{1,0:T(8,128)(2,1)S(1)}, bf16[160,256]{1,0:T(8,128)(2,1)S(1)}, u32[]{:S(2)}, u32[]{:S(2)}) collective-permute-start(bf16[160,256]{1,0:T(8,128)(2,1)S(1)} %get-tuple-element.48), channel_id=1, source_target_pairs={{0,1},{12,13},{4,8},{8,4},{1,0},{13,12},{5,9},{9,5},{2,3},{14,15},... | collective-permute-start | bytes 245768 | tf_op jit(solution)/shard_map/ppermute | solution.py:63
  10.0 4.2 %collective-permute-start.3 = (bf16[96,256]{1,0:T(8,128)(2,1)S(1)}, bf16[96,256]{1,0:T(8,128)(2,1)S(1)}, u32[]{:S(2)}, u32[]{:S(2)}) collective-permute-start(bf16[96,256]{1,0:T(8,128)(2,1)S(1)} %pad_maximum_fusion), channel_id=1, source_target_pairs={{0,16},{16,0},{1,17},{17,1},{2,18},{18,2},{3,19},{19,3},{4,20},{20... | collective-permute-start | bytes 147464 | tf_op jit(solution)/shard_map/ppermute | solution.py:432
  14.1 3.4 %copy-start = (bf16[1,4,32,16,256]{4,3,2,1,0:T(8,128)(2,1)S(1)}, bf16[1,4,32,16,256]{4,3,2,1,0:T(8,128)(2,1)}, u32[]{:S(2)}) copy-start(bf16[1,4,32,16,256]{4,3,2,1,0:T(8,128)(2,1)} %param.11) | copy-start | bytes 3145732
  14.9 4.6 %collective-permute-start.4 = (bf16[160,256]{1,0:T(8,128)(2,1)S(1)}, bf16[160,256]{1,0:T(8,128)(2,1)S(1)}, u32[]{:S(2)}, u32[]{:S(2)}) collective-permute-start(bf16[160,256]{1,0:T(8,128)(2,1)S(1)} %get-tuple-element.53), channel_id=1, source_target_pairs={{0,4},{4,0},{8,12},{12,8},{1,5},{5,1},{9,13},{13,9},{2,6},{6,2},{1... | collective-permute-start | bytes 245768 | tf_op jit(solution)/shard_map/ppermute | solution.py:432
  15.0 4.5 %collective-permute-start.5 = (bf16[160,256]{1,0:T(8,128)(2,1)S(1)}, bf16[160,256]{1,0:T(8,128)(2,1)S(1)}, u32[]{:S(2)}, u32[]{:S(2)}) collective-permute-start(bf16[160,256]{1,0:T(8,128)(2,1)S(1)} %get-tuple-element.54), channel_id=1, source_target_pairs={{0,1},{12,13},{4,8},{8,4},{1,0},{13,12},{5,9},{9,5},{2,3},{14,15},... | collective-permute-start | bytes 245768 | tf_op jit(solution)/shard_map/ppermute | solution.py:63
  15.5 4.0 %collective-permute-start.6 = (bf16[80,256]{1,0:T(8,128)(2,1)S(1)}, bf16[80,256]{1,0:T(8,128)(2,1)S(1)}, u32[]{:S(2)}, u32[]{:S(2)}) collective-permute-start(bf16[80,256]{1,0:T(8,128)(2,1)S(1)} %get-tuple-element.55), channel_id=1, source_target_pairs={{0,16},{16,0},{1,17},{17,1},{2,18},{18,2},{3,19},{19,3},{4,20},{20... | collective-permute-start | bytes 122888 | tf_op jit(solution)/shard_map/ppermute | solution.py:432
  19.8 5.7 %collective-permute-start.7 = (bf16[160,256]{1,0:T(8,128)(2,1)S(1)}, bf16[160,256]{1,0:T(8,128)(2,1)S(1)}, u32[]{:S(2)}, u32[]{:S(2)}) collective-permute-start(bf16[160,256]{1,0:T(8,128)(2,1)S(1)} %get-tuple-element.59), channel_id=1, source_target_pairs={{0,4},{4,0},{8,12},{12,8},{1,5},{5,1},{9,13},{13,9},{2,6},{6,2},{1... | collective-permute-start | bytes 245768 | tf_op jit(solution)/shard_map/ppermute | solution.py:432
  20.1 5.5 %collective-permute-start.8 = (bf16[160,256]{1,0:T(8,128)(2,1)S(1)}, bf16[160,256]{1,0:T(8,128)(2,1)S(1)}, u32[]{:S(2)}, u32[]{:S(2)}) collective-permute-start(bf16[160,256]{1,0:T(8,128)(2,1)S(1)} %get-tuple-element.60), channel_id=1, source_target_pairs={{0,1},{12,13},{4,8},{8,4},{1,0},{13,12},{5,9},{9,5},{2,3},{14,15},... | collective-permute-start | bytes 245768 | tf_op jit(solution)/shard_map/ppermute | solution.py:63
  21.5 4.0 %collective-permute-start.9 = (bf16[80,256]{1,0:T(8,128)(2,1)S(1)}, bf16[80,256]{1,0:T(8,128)(2,1)S(1)}, u32[]{:S(2)}, u32[]{:S(2)}) collective-permute-start(bf16[80,256]{1,0:T(8,128)(2,1)S(1)} %get-tuple-element.61), channel_id=1, source_target_pairs={{0,16},{16,0},{1,17},{17,1},{2,18},{18,2},{3,19},{19,3},{4,20},{20... | collective-permute-start | bytes 122888 | tf_op jit(solution)/shard_map/ppermute | solution.py:432
  25.8 4.7 %collective-permute-start.10 = (bf16[160,256]{1,0:T(8,128)(2,1)S(1)}, bf16[160,256]{1,0:T(8,128)(2,1)S(1)}, u32[]{:S(2)}, u32[]{:S(2)}) collective-permute-start(bf16[160,256]{1,0:T(8,128)(2,1)S(1)} %get-tuple-element.66), channel_id=1, source_target_pairs={{0,4},{4,0},{8,12},{12,8},{1,5},{5,1},{9,13},{13,9},{2,6},{6,2},{1... | collective-permute-start | bytes 245768 | tf_op jit(solution)/shard_map/ppermute | solution.py:432
  25.9 4.7 %collective-permute-start.11 = (bf16[160,256]{1,0:T(8,128)(2,1)S(1)}, bf16[160,256]{1,0:T(8,128)(2,1)S(1)}, u32[]{:S(2)}, u32[]{:S(2)}) collective-permute-start(bf16[160,256]{1,0:T(8,128)(2,1)S(1)} %get-tuple-element.67), channel_id=1, source_target_pairs={{0,1},{12,13},{4,8},{8,4},{1,0},{13,12},{5,9},{9,5},{2,3},{14,15},... | collective-permute-start | bytes 245768 | tf_op jit(solution)/shard_map/ppermute | solution.py:63
  26.6 4.0 %collective-permute-start.12 = (bf16[80,256]{1,0:T(8,128)(2,1)S(1)}, bf16[80,256]{1,0:T(8,128)(2,1)S(1)}, u32[]{:S(2)}, u32[]{:S(2)}) collective-permute-start(bf16[80,256]{1,0:T(8,128)(2,1)S(1)} %get-tuple-element.68), channel_id=1, source_target_pairs={{0,16},{16,0},{1,17},{17,1},{2,18},{18,2},{3,19},{19,3},{4,20},{20... | collective-permute-start | bytes 122888 | tf_op jit(solution)/shard_map/ppermute | solution.py:432
  31.0 6.3 %collective-permute-start.15 = (f32[16,8,128]{2,1,0:T(8,128)S(1)}, f32[16,8,128]{2,1,0:T(8,128)S(1)}, u32[]{:S(2)}, u32[]{:S(2)}) collective-permute-start(f32[16,8,128]{2,1,0:T(8,128)S(1)} %get-tuple-element.72), channel_id=1, source_target_pairs={{0,3},{1,2},{2,1},{3,0},{4,7},{5,6},{6,5},{7,4},{8,11},{9,10},{10,... | collective-permute-start | bytes 196616 | tf_op jit(solution)/shard_map/ppermute | solution.py:432
  34.5 5.9 %collective-permute-start.14 = (f32[16,8,128]{2,1,0:T(8,128)S(1)}, f32[16,8,128]{2,1,0:T(8,128)S(1)}, u32[]{:S(2)}, u32[]{:S(2)}) collective-permute-start(f32[16,8,128]{2,1,0:T(8,128)S(1)} %get-tuple-element.72), channel_id=1, source_target_pairs={{0,2},{1,3},{2,0},{3,1},{4,6},{5,7},{6,4},{7,5},{8,10},{9,11},{10,... | collective-permute-start | bytes 196616 | tf_op jit(solution)/shard_map/ppermute | solution.py:432
  34.5 5.9 %collective-permute-start.13 = (f32[16,8,128]{2,1,0:T(8,128)S(1)}, f32[16,8,128]{2,1,0:T(8,128)S(1)}, u32[]{:S(2)}, u32[]{:S(2)}) collective-permute-start(f32[16,8,128]{2,1,0:T(8,128)S(1)} %get-tuple-element.72), channel_id=1, source_target_pairs={{0,1},{1,0},{2,3},{3,2},{4,5},{5,4},{6,7},{7,6},{8,9},{9,8},{10,11... | collective-permute-start | bytes 196616 | tf_op jit(solution)/shard_map/ppermute | solution.py:432

commit v5 on v4

--- a/solution.py
+++ b/solution.py
@@ -156,28 +156,28 @@
         nxt[x, :, :] = nxt[x, :, :] + c2[x, :, :] * total
 
 
-def add_halos(nxt, c2, gx_index, gy_index, ye, yo, xe, xo, stage):
-    for axis, index, even, odd, add in (("gy", gy_index, ye, yo, add_y_halo), ("gx", gx_index, xe, xo, add_x_halo)):
-        is_even = index % 2 == 0
-        inner = jnp.logical_and(index > 0, index < lax.axis_size(axis) - 1)
-
-        @pl.when(is_even)
-        def _(even=even, add=add):
-            add(nxt, c2, even, stage, True)
-
-        @pl.when(jnp.logical_not(is_even))
-        def _(even=even, add=add):
-            add(nxt, c2, even, stage, False)
-
-        if odd is not None:
-
-            @pl.when(jnp.logical_and(inner, is_even))
-            def _(odd=odd, add=add):
-                add(nxt, c2, odd, stage, False)
-
-            @pl.when(jnp.logical_and(inner, jnp.logical_not(is_even)))
-            def _(odd=odd, add=add):
-                add(nxt, c2, odd, stage, True)
+def add_halos(nxt, c2, name, even, odd, stage):
+    index, add = lax.axis_index(name), add_y_halo if name == "gy" else add_x_halo
+    is_even = index % 2 == 0
+    inner = jnp.logical_and(index > 0, index < lax.axis_size(name) - 1)
+
+    @pl.when(is_even)
+    def _():
+        add(nxt, c2, even, stage, True)
+
+    @pl.when(jnp.logical_not(is_even))
+    def _():
+        add(nxt, c2, even, stage, False)
+
+    if odd is not None:
+
+        @pl.when(jnp.logical_and(inner, is_even))
+        def _():
+            add(nxt, c2, odd, stage, False)
+
+        @pl.when(jnp.logical_and(inner, jnp.logical_not(is_even)))
+        def _():
+            add(nxt, c2, odd, stage, True)
 
 
 def put_band(out, size, span, centre):
@@ -353,7 +353,7 @@
 
 def first_correct_kernel(owners, weights, select, part, c2, *refs, with_yo, with_xo, patterns):
     gx_index, gy_index = lax.axis_index("gx"), lax.axis_index("gy")
-    ye, yo, xe, xo, refs = unpack(refs, with_yo, with_xo)
+    ye, _, xe, xo, refs = unpack(refs, with_yo, with_xo)
     pairs, refs = refs[0], refs[1:]
     nxt, contrib, refs = refs[0], refs[1], refs[2:]
     oye, oyo, oxe, oxo, refs = unpack(refs, with_yo, with_xo)
@@ -374,27 +374,33 @@
         src = dot(select[m * rows : (m + 1) * rows, :], contrib[0])
         at = slice(m * chunk, (m + 1) * chunk)
         nxt[at, :, :] = part[at, :, :] + src.reshape(chunk, cy, nz)
-    add_halos(nxt, c2, gx_index, gy_index, ye, yo, xe, xo, stage)
+    add_halos(nxt, c2, "gx", xe, xo, stage)
     put_faces(nxt, gx_index, gy_index, oye, oyo, oxe, oxo, stage)
+
+
+def correct_y_kernel(part, c2, *refs):
+    out, stage = refs[-2:]
+    out[...] = part[...]
+    add_halos(out, c2, "gy", refs[0], refs[1] if len(refs) == 4 else None, stage)
 
 
 def correct_kernel(part, c2, *refs, with_yo, with_xo):
     gx_index, gy_index = lax.axis_index("gx"), lax.axis_index("gy")
-    ye, yo, xe, xo, refs = unpack(refs, with_yo, with_xo)
+    xe, xo = refs[0], refs[1] if with_xo else None
+    refs = refs[1 + with_xo :]
     nxt, refs = refs[0], refs[1:]
     oye, oyo, oxe, oxo, (stage,) = unpack(refs, with_yo, with_xo)
     nxt[...] = part[...]
-    add_halos(nxt, c2, gx_index, gy_index, ye, yo, xe, xo, stage)
+    add_halos(nxt, c2, "gx", xe, xo, stage)
     put_faces(nxt, gx_index, gy_index, oye, oyo, oxe, oxo, stage)
 
 
-def last_kernel(part, c2, accel, fine, *refs, with_yo, with_xo, step):
-    gx_index, gy_index = lax.axis_index("gx"), lax.axis_index("gy")
-    ye, yo, xe, xo, refs = unpack(refs, with_yo, with_xo)
-    nxt, coarse, middle, stage = refs
+def last_kernel(part, c2, accel, fine, *refs, with_xo, step):
+    xe, xo = refs[0], refs[1] if with_xo else None
+    nxt, coarse, middle, stage = refs[1 + with_xo :]
     cx, cy, nz = nxt.shape
     nxt[...] = part[...]
-    add_halos(nxt, c2, gx_index, gy_index, ye, yo, xe, xo, stage)
+    add_halos(nxt, c2, "gx", xe, xo, stage)
     pairs = lax.div(lax.broadcasted_iota(jnp.int32, (nz, nz // 2), 0), jnp.int32(2)) == lax.broadcasted_iota(
         jnp.int32, (nz, nz // 2), 1
     )
@@ -494,6 +500,10 @@
         hbm_in=(3, 4, 5), flops=cells * 60,
     )
 
+    def correct_y(part, ye, yo):
+        return vmem_call(correct_y_kernel, [sds(tile)], [part, c2] + [a for a in (ye, yo) if a is not None], [stage])[0]
+
+    part = correct_y(part, rye, ryo)
     nxt, contrib, *faces = vmem_call(
         functools.partial(
             first_correct_kernel, with_yo=with_yo, with_xo=with_xo, patterns=tuple(patterns)
@@ -517,7 +527,8 @@
             functools.partial(update_kernel, step=step), [sds(tile), sds(tile)], args,
             flops=cells * 60,
         )
-        halos = given(rye, ryo, rxe, rxo)
+        part = correct_y(part, rye, ryo)
+        halos = [a for a in (rxe, rxo) if a is not None]
         if step < steps - 1:
             nxt, *faces = vmem_call(
                 functools.partial(correct_kernel, with_yo=with_yo, with_xo=with_xo),
@@ -527,7 +538,7 @@
             )
         else:
             nxt, coarse = vmem_call(
-                functools.partial(last_kernel, with_yo=with_yo, with_xo=with_xo, step=step),
+                functools.partial(last_kernel, with_xo=with_xo, step=step),
                 [sds(tile), sds((cx // 2, cy // 2, nz // 2))],
                 [part, c2, accel, fine] + halos,
                 [pltpu.VMEM((cx * cy // 2, nz // 2), F32), stage],

time: 41.2 us -> 40.8 us (level)
    ppermute x12, waiting for transfers between devices: 10.8 us -> 7.16 us  [swap(): return odd_swap(x, axis) if pairs is None else lax.ppermute(x, axis, pairs)]
    ppermute x4, waiting for transfers between devices: 0.01 us -> 3.35 us  [odd_swap(): return lax.ppermute(x, (axis, 'shot'), pairs)]
    pallas_call x10 -> x14, Pallas kernels: 8.64 us -> 8.7 us  [vmem_call(): pl.pallas_call(kernel, out_shape=tuple(outs), in_specs=in_specs, out_spec...]
  transfers between devices with their start and end apart: 16 -> 16, of which waited for: 6 -> 8; matrix products, arithmetic and copies ran while one was open for 0% -> 0% of each run, Pallas kernels for 17% -> 18%
where the time goes in v5:
time: 40.8 us; the launch traced here: 40.6 us
  starting transfers between devices  19.2 us (47%)
  waiting for transfers between devices  10.5 us (26%)
  Pallas kernels  8.7 us (21%)
  between operations  1.5 us (4%)
  other arithmetic  0.67 us (2%)
    ppermute x12, starting transfers between devices, swap(): return odd_swap(x, axis) if pairs is None else lax.ppermute(x, axis, pairs)  14.6 us
    pallas_call x14, Pallas kernels, vmem_call(): pl.pallas_call(kernel, out_shape=tuple(outs), in_specs=in_specs, out_spec...  8.7 us
    ppermute x12, waiting for transfers between devices, swap(): return odd_swap(x, axis) if pairs is None else lax.ppermute(x, axis, pairs)  7.16 us
    ppermute x4, starting transfers between devices, odd_swap(): return lax.ppermute(x, (axis, 'shot'), pairs)  4.62 us
    ppermute x4, waiting for transfers between devices, odd_swap(): return lax.ppermute(x, (axis, 'shot'), pairs)  3.35 us
  transfers between devices with their start and end apart: 16, of which 8 were waited for; matrix products, arithmetic and copies ran while one was open for 0% of the time, Pallas kernels for 18%

profile of v5, /device:TPU:0, one launch (start us, length us, event | category | flops | bytes accessed | tf_op | source)
XLA Modules:
  0.0 40.6 jit_solution(8886036554597565610)
XLA Ops:
  0.6 3.0 %collective-permute-start = (bf16[1,4,64]{2,1,0:T(4,128)(2,1)}, bf16[1,4,64]{2,1,0:T(4,128)(2,1)S(1)}, u32[]{:S(2)}, u32[]{:S(2)}) collective-permute-start(bf16[1,4,64]{2,1,0:T(4,128)(2,1)} %traces_in.1), channel_id=1, source_target_pairs={{0,8},{4,12},{8,0},{12,4},{1,9},{5,13},{9,1},{13,5},{2,10},{6,14},... | collective-permute-start | bytes 1544 | tf_op jit(solution)/shard_map/ppermute | solution.py:438
  4.3 1.2 %shard_map.112 = (f32[32,16,256]{2,1,0:T(8,128)S(1)}, bf16[512,256]{1,0:T(8,128)(2,1)S(1)}, bf16[256,128]{1,0:T(8,128)(2,1)S(1)}, bf16[512,192]{1,0:T(8,128)(2,1...) custom-call(f32[32,16,256]{2,1,0:T(8,128)} %bitcast.18, ...), custom_call_target="tpu_custom_call" | custom-call | bytes 1815556 | tf_op jit(solution)/shard_map/pallas_call | solution.py:26
  5.7 2.0 %collective-permute-start.2 = (bf16[160,256]{1,0:T(8,128)(2,1)S(1)}, bf16[160,256]{1,0:T(8,128)(2,1)S(1)}, u32[]{:S(2)}, u32[]{:S(2)}) collective-permute-start(bf16[160,256]{1,0:T(8,128)(2,1)S(1)} %get-tuple-element.48), channel_id=1, source_target_pairs={{0,1},{12,13},{4,8},{8,4},{1,0},{13,12},{5,9},{9,5},{2,3},{14,15},... | collective-permute-start | bytes 245768 | tf_op jit(solution)/shard_map/ppermute | solution.py:63
  7.7 2.2 %shard_map.113 = (f32[32,16,256]{2,1,0:T(8,128)S(1)}, f32[32,16,256]{2,1,0:T(8,128)}, f32[32,16,256]{2,1,0:T(8,128)S(1)}, bf16[64,16,256]{2,1,0:T(8,128)(2,1)S(1)}) custom-call(f32[32,16,256]{2,1,0:T(8,128)S(1)} %get-tuple-element.39.cur.prev, bf16[512,256]{1,0:T(8,128)(2,1)S(1)} %get-tuple-element.40.toeplitz, ...), custom_call_target="tpu_custom_call" | custom-call | flops 7864320 | bytes 4521984 | tf_op jit(solution)/shard_map/pallas_call | solution.py:26
  10.0 1.6 %collective-permute-start.3 = (bf16[96,256]{1,0:T(8,128)(2,1)S(1)}, bf16[96,256]{1,0:T(8,128)(2,1)S(1)}, u32[]{:S(2)}, u32[]{:S(2)}) collective-permute-start(bf16[96,256]{1,0:T(8,128)(2,1)S(1)} %pad_maximum_fusion), channel_id=1, source_target_pairs={{0,16},{16,0},{1,17},{17,1},{2,18},{18,2},{3,19},{19,3},{4,20},{20... | collective-permute-start | bytes 147464 | tf_op jit(solution)/shard_map/ppermute | solution.py:438
  11.7 2.4 %collective-permute-done.3.refs_2_ = bf16[96,256]{1,0:T(8,128)(2,1)S(1)} collective-permute-done((bf16[96,256]{1,0:T(8,128)(2,1)S(1)}, bf16[96,256]{1,0:T(8,128)(2,1)S(1)}, u32[]{:S(2)}, u32[]{:S(2)}) %collective-permute-start.3) | collective-permute-done | bytes 49184 | tf_op jit(solution)/shard_map/ppermute | solution.py:438
  14.1 0.7 %shard_map.115 = (f32[32,16,256]{2,1,0:T(8,128)S(1)}, bf16[4,192,256]{2,1,0:T(8,128)(2,1)S(1)}, bf16[160,256]{1,0:T(8,128)(2,1)S(1)}, bf16[160,256]{1,0:T(8,128)(2,1)S(1)}, bf16[80,256]{1,0:T(8,128)(2,1)S(1)}) custom-call(s32[64,128]{1,0:T(8,128)S(1)} %get-tuple-element.38.owners, bf16[64,16,256]{2,1,0:T(8,128)(2,1)S(1)} %get-tuple-element.42.weights, ...), custom_call_target="tpu_custom_call" | custom-call | bytes 3145728 | tf_op jit(solution)/shard_map/pallas_call | solution.py:26
  15.4 2.0 %collective-permute-start.6 = (bf16[80,256]{1,0:T(8,128)(2,1)S(1)}, bf16[80,256]{1,0:T(8,128)(2,1)S(1)}, u32[]{:S(2)}, u32[]{:S(2)}) collective-permute-start(bf16[80,256]{1,0:T(8,128)(2,1)S(1)} %get-tuple-element.55), channel_id=1, source_target_pairs={{0,16},{16,0},{1,17},{17,1},{2,18},{18,2},{3,19},{19,3},{4,20},{20... | collective-permute-start | bytes 122888 | tf_op jit(solution)/shard_map/ppermute | solution.py:438
  17.3 0.8 %shard_map.116 = (f32[32,16,256]{2,1,0:T(8,128)S(1)}, f32[32,16,256]{2,1,0:T(8,128)S(1)}) custom-call(f32[32,16,256]{2,1,0:T(8,128)S(1)} %get-tuple-element.50.cur.prev, f32[32,16,256]{2,1,0:T(8,128)S(1)} %get-tuple-element.39.cur.prev, f32[32,16,256]{2,1,0:T(8,128)S(1)} %get-tuple-element.45.c2, bf16[512,256]{1,0:T(8,128)(2,1)S(1)} %get-tuple-element.40.toeplitz, ...), custom_call_target="tpu_custom_call" | custom-call | flops 7864320 | bytes 4587520 | tf_op jit(solution)/shard_map/pallas_call | solution.py:26
  18.2 1.3 %collective-permute-done.5.refs_1_ = bf16[160,256]{1,0:T(8,128)(2,1)S(1)} collective-permute-done((bf16[160,256]{1,0:T(8,128)(2,1)S(1)}, bf16[160,256]{1,0:T(8,128)(2,1)S(1)}, u32[]{:S(2)}, u32[]{:S(2)}) %collective-permute-start.5) | collective-permute-done | bytes 81952 | tf_op jit(solution)/shard_map/ppermute | solution.py:63
  20.0 1.3 %collective-permute-start.8 = (bf16[160,256]{1,0:T(8,128)(2,1)S(1)}, bf16[160,256]{1,0:T(8,128)(2,1)S(1)}, u32[]{:S(2)}, u32[]{:S(2)}) collective-permute-start(bf16[160,256]{1,0:T(8,128)(2,1)S(1)} %get-tuple-element.60), channel_id=1, source_target_pairs={{0,1},{12,13},{4,8},{8,4},{1,0},{13,12},{5,9},{9,5},{2,3},{14,15},... | collective-permute-start | bytes 245768 | tf_op jit(solution)/shard_map/ppermute | solution.py:63
  21.3 1.5 %collective-permute-start.9 = (bf16[80,256]{1,0:T(8,128)(2,1)S(1)}, bf16[80,256]{1,0:T(8,128)(2,1)S(1)}, u32[]{:S(2)}, u32[]{:S(2)}) collective-permute-start(bf16[80,256]{1,0:T(8,128)(2,1)S(1)} %get-tuple-element.61), channel_id=1, source_target_pairs={{0,16},{16,0},{1,17},{17,1},{2,18},{18,2},{3,19},{19,3},{4,20},{20... | collective-permute-start | bytes 122888 | tf_op jit(solution)/shard_map/ppermute | solution.py:438
  22.8 0.8 %shard_map.119 = (f32[32,16,256]{2,1,0:T(8,128)S(1)}, f32[32,16,256]{2,1,0:T(8,128)S(1)}) custom-call(f32[32,16,256]{2,1,0:T(8,128)S(1)} %get-tuple-element.56.cur.prev, f32[32,16,256]{2,1,0:T(8,128)S(1)} %get-tuple-element.50.cur.prev, f32[32,16,256]{2,1,0:T(8,128)S(1)} %get-tuple-element.45.c2, bf16[512,256]{1,0:T(8,128)(2,1)S(1)} %get-tuple-element.40.toeplitz, ...), custom_call_target="tpu_custom_call" | custom-call | flops 7864320 | bytes 5111808 | tf_op jit(solution)/shard_map/pallas_call | solution.py:26
  23.7 0.8 %collective-permute-done.8.refs_1_ = bf16[160,256]{1,0:T(8,128)(2,1)S(1)} collective-permute-done((bf16[160,256]{1,0:T(8,128)(2,1)S(1)}, bf16[160,256]{1,0:T(8,128)(2,1)S(1)}, u32[]{:S(2)}, u32[]{:S(2)}) %collective-permute-start.8) | collective-permute-done | bytes 81952 | tf_op jit(solution)/shard_map/ppermute | solution.py:63
  24.6 0.7 %collective-permute-done.9.refs_0_ = bf16[80,256]{1,0:T(8,128)(2,1)S(1)} collective-permute-done((bf16[80,256]{1,0:T(8,128)(2,1)S(1)}, bf16[80,256]{1,0:T(8,128)(2,1)S(1)}, u32[]{:S(2)}, u32[]{:S(2)}) %collective-permute-start.9) | collective-permute-done | bytes 40992 | tf_op jit(solution)/shard_map/ppermute | solution.py:438
  25.6 0.8 %collective-permute-start.11 = (bf16[160,256]{1,0:T(8,128)(2,1)S(1)}, bf16[160,256]{1,0:T(8,128)(2,1)S(1)}, u32[]{:S(2)}, u32[]{:S(2)}) collective-permute-start(bf16[160,256]{1,0:T(8,128)(2,1)S(1)} %get-tuple-element.66), channel_id=1, source_target_pairs={{0,1},{12,13},{4,8},{8,4},{1,0},{13,12},{5,9},{9,5},{2,3},{14,15},... | collective-permute-start | bytes 245768 | tf_op jit(solution)/shard_map/ppermute | solution.py:63
  26.4 1.6 %collective-permute-start.12 = (bf16[80,256]{1,0:T(8,128)(2,1)S(1)}, bf16[80,256]{1,0:T(8,128)(2,1)S(1)}, u32[]{:S(2)}, u32[]{:S(2)}) collective-permute-start(bf16[80,256]{1,0:T(8,128)(2,1)S(1)} %get-tuple-element.68), channel_id=1, source_target_pairs={{0,16},{16,0},{1,17},{17,1},{2,18},{18,2},{3,19},{19,3},{4,20},{20... | collective-permute-start | bytes 122888 | tf_op jit(solution)/shard_map/ppermute | solution.py:438
  28.0 0.8 %shard_map.122 = (f32[32,16,256]{2,1,0:T(8,128)S(1)}, f32[32,16,256]{2,1,0:T(8,128)S(1)}) custom-call(f32[32,16,256]{2,1,0:T(8,128)S(1)} %get-tuple-element.62.cur.a_in, f32[32,16,256]{2,1,0:T(8,128)S(1)} %get-tuple-element.56.cur.prev, f32[32,16,256]{2,1,0:T(8,128)S(1)} %get-tuple-element.45.c2, bf16[512,256]{1,0:T(8,128)(2,1)S(1)} %get-tuple-element.40.toeplitz, ...), custom_call_target="tpu_custom_call" | custom-call | flops 7864320 | bytes 5111808 | tf_op jit(solution)/shard_map/pallas_call | solution.py:26
  28.8 1.3 %collective-permute-done.11.refs_1_ = bf16[160,256]{1,0:T(8,128)(2,1)S(1)} collective-permute-done((bf16[160,256]{1,0:T(8,128)(2,1)S(1)}, bf16[160,256]{1,0:T(8,128)(2,1)S(1)}, u32[]{:S(2)}, u32[]{:S(2)}) %collective-permute-start.11) | collective-permute-done | bytes 81952 | tf_op jit(solution)/shard_map/ppermute | solution.py:63
  30.7 3.4 %collective-permute-start.15 = (f32[16,8,128]{2,1,0:T(8,128)S(1)}, f32[16,8,128]{2,1,0:T(8,128)S(1)}, u32[]{:S(2)}, u32[]{:S(2)}) collective-permute-start(f32[16,8,128]{2,1,0:T(8,128)S(1)} %get-tuple-element.72), channel_id=1, source_target_pairs={{0,3},{1,2},{2,1},{3,0},{4,7},{5,6},{6,5},{7,4},{8,11},{9,10},{10,... | collective-permute-start | bytes 196616 | tf_op jit(solution)/shard_map/ppermute | solution.py:438
  34.1 1.1 %collective-permute-start.13 = (f32[16,8,128]{2,1,0:T(8,128)S(1)}, f32[16,8,128]{2,1,0:T(8,128)S(1)}, u32[]{:S(2)}, u32[]{:S(2)}) collective-permute-start(f32[16,8,128]{2,1,0:T(8,128)S(1)} %get-tuple-element.72), channel_id=1, source_target_pairs={{0,1},{1,0},{2,3},{3,2},{4,5},{5,4},{6,7},{7,6},{8,9},{9,8},{10,11... | collective-permute-start | bytes 196616 | tf_op jit(solution)/shard_map/ppermute | solution.py:438
  35.2 1.0 %shard_map.125 = (f32[32,16,256]{2,1,0:T(8,128)}, f32[32,16,256]{2,1,0:T(8,128)}) custom-call(f32[32,16,256]{2,1,0:T(8,128)S(1)} %get-tuple-element.62.cur.a_in, f32[32,16,256]{2,1,0:T(8,128)S(1)} %get-tuple-element.69.b_in), custom_call_target="tpu_custom_call" | custom-call | bytes 2097152 | tf_op jit(solution)/shard_map/pallas_call | solution.py:26
  36.1 0.9 %collective-permute-done.15 = f32[16,8,128]{2,1,0:T(8,128)S(1)} collective-permute-done((f32[16,8,128]{2,1,0:T(8,128)S(1)}, f32[16,8,128]{2,1,0:T(8,128)S(1)}, u32[]{:S(2)}, u32[]{:S(2)}) %collective-permute-start.15) | collective-permute-done | bytes 65568 | tf_op jit(solution)/shard_map/ppermute | solution.py:438
  37.0 3.0 %collective-permute-done.14 = f32[16,8,128]{2,1,0:T(8,128)S(1)} collective-permute-done((f32[16,8,128]{2,1,0:T(8,128)S(1)}, f32[16,8,128]{2,1,0:T(8,128)S(1)}, u32[]{:S(2)}, u32[]{:S(2)}) %collective-permute-start.14) | collective-permute-done | bytes 65568 | tf_op jit(solution)/shard_map/ppermute | solution.py:438
  (31 shorter events, 3.0 us)
Async XLA Ops:
  0.6 4.9 %collective-permute-start = (bf16[1,4,64]{2,1,0:T(4,128)(2,1)}, bf16[1,4,64]{2,1,0:T(4,128)(2,1)S(1)}, u32[]{:S(2)}, u32[]{:S(2)}) collective-permute-start(bf16[1,4,64]{2,1,0:T(4,128)(2,1)} %traces_in.1), channel_id=1, source_target_pairs={{0,8},{4,12},{8,0},{12,4},{1,9},{5,13},{9,1},{13,5},{2,10},{6,14},... | collective-permute-start | bytes 1544 | tf_op jit(solution)/shard_map/ppermute | solution.py:438
  5.6 4.3 %collective-permute-start.1 = (bf16[168,256]{1,0:T(8,128)(2,1)S(1)}, bf16[168,256]{1,0:T(8,128)(2,1)S(1)}, u32[]{:S(2)}, u32[]{:S(2)}) collective-permute-start(bf16[168,256]{1,0:T(8,128)(2,1)S(1)} %maximum_maximum_fusion), channel_id=1, source_target_pairs={{0,4},{4,0},{8,12},{12,8},{1,5},{5,1},{9,13},{13,9},{2,6},{6,2},{1... | collective-permute-start | bytes 258056 | tf_op jit(solution)/shard_map/ppermute | solution.py:438
  5.7 5.9 %collective-permute-start.2 = (bf16[160,256]{1,0:T(8,128)(2,1)S(1)}, bf16[160,256]{1,0:T(8,128)(2,1)S(1)}, u32[]{:S(2)}, u32[]{:S(2)}) collective-permute-start(bf16[160,256]{1,0:T(8,128)(2,1)S(1)} %get-tuple-element.48), channel_id=1, source_target_pairs={{0,1},{12,13},{4,8},{8,4},{1,0},{13,12},{5,9},{9,5},{2,3},{14,15},... | collective-permute-start | bytes 245768 | tf_op jit(solution)/shard_map/ppermute | solution.py:63
  10.0 4.2 %collective-permute-start.3 = (bf16[96,256]{1,0:T(8,128)(2,1)S(1)}, bf16[96,256]{1,0:T(8,128)(2,1)S(1)}, u32[]{:S(2)}, u32[]{:S(2)}) collective-permute-start(bf16[96,256]{1,0:T(8,128)(2,1)S(1)} %pad_maximum_fusion), channel_id=1, source_target_pairs={{0,16},{16,0},{1,17},{17,1},{2,18},{18,2},{3,19},{19,3},{4,20},{20... | collective-permute-start | bytes 147464 | tf_op jit(solution)/shard_map/ppermute | solution.py:438
  14.1 3.2 %copy-start = (bf16[1,4,32,16,256]{4,3,2,1,0:T(8,128)(2,1)S(1)}, bf16[1,4,32,16,256]{4,3,2,1,0:T(8,128)(2,1)}, u32[]{:S(2)}) copy-start(bf16[1,4,32,16,256]{4,3,2,1,0:T(8,128)(2,1)} %param.11) | copy-start | bytes 3145732
  14.8 3.3 %collective-permute-start.4 = (bf16[160,256]{1,0:T(8,128)(2,1)S(1)}, bf16[160,256]{1,0:T(8,128)(2,1)S(1)}, u32[]{:S(2)}, u32[]{:S(2)}) collective-permute-start(bf16[160,256]{1,0:T(8,128)(2,1)S(1)} %get-tuple-element.53), channel_id=1, source_target_pairs={{0,4},{4,0},{8,12},{12,8},{1,5},{5,1},{9,13},{13,9},{2,6},{6,2},{1... | collective-permute-start | bytes 245768 | tf_op jit(solution)/shard_map/ppermute | solution.py:438
  14.9 4.5 %collective-permute-start.5 = (bf16[160,256]{1,0:T(8,128)(2,1)S(1)}, bf16[160,256]{1,0:T(8,128)(2,1)S(1)}, u32[]{:S(2)}, u32[]{:S(2)}) collective-permute-start(bf16[160,256]{1,0:T(8,128)(2,1)S(1)} %get-tuple-element.54), channel_id=1, source_target_pairs={{0,1},{12,13},{4,8},{8,4},{1,0},{13,12},{5,9},{9,5},{2,3},{14,15},... | collective-permute-start | bytes 245768 | tf_op jit(solution)/shard_map/ppermute | solution.py:63
  15.4 4.2 %collective-permute-start.6 = (bf16[80,256]{1,0:T(8,128)(2,1)S(1)}, bf16[80,256]{1,0:T(8,128)(2,1)S(1)}, u32[]{:S(2)}, u32[]{:S(2)}) collective-permute-start(bf16[80,256]{1,0:T(8,128)(2,1)S(1)} %get-tuple-element.55), channel_id=1, source_target_pairs={{0,16},{16,0},{1,17},{17,1},{2,18},{18,2},{3,19},{19,3},{4,20},{20... | collective-permute-start | bytes 122888 | tf_op jit(solution)/shard_map/ppermute | solution.py:438
  19.7 3.9 %collective-permute-start.7 = (bf16[160,256]{1,0:T(8,128)(2,1)S(1)}, bf16[160,256]{1,0:T(8,128)(2,1)S(1)}, u32[]{:S(2)}, u32[]{:S(2)}) collective-permute-start(bf16[160,256]{1,0:T(8,128)(2,1)S(1)} %get-tuple-element.59), channel_id=1, source_target_pairs={{0,4},{4,0},{8,12},{12,8},{1,5},{5,1},{9,13},{13,9},{2,6},{6,2},{1... | collective-permute-start | bytes 245768 | tf_op jit(solution)/shard_map/ppermute | solution.py:438
  20.0 4.4 %collective-permute-start.8 = (bf16[160,256]{1,0:T(8,128)(2,1)S(1)}, bf16[160,256]{1,0:T(8,128)(2,1)S(1)}, u32[]{:S(2)}, u32[]{:S(2)}) collective-permute-start(bf16[160,256]{1,0:T(8,128)(2,1)S(1)} %get-tuple-element.60), channel_id=1, source_target_pairs={{0,1},{12,13},{4,8},{8,4},{1,0},{13,12},{5,9},{9,5},{2,3},{14,15},... | collective-permute-start | bytes 245768 | tf_op jit(solution)/shard_map/ppermute | solution.py:63
  21.3 4.0 %collective-permute-start.9 = (bf16[80,256]{1,0:T(8,128)(2,1)S(1)}, bf16[80,256]{1,0:T(8,128)(2,1)S(1)}, u32[]{:S(2)}, u32[]{:S(2)}) collective-permute-start(bf16[80,256]{1,0:T(8,128)(2,1)S(1)} %get-tuple-element.61), channel_id=1, source_target_pairs={{0,16},{16,0},{1,17},{17,1},{2,18},{18,2},{3,19},{19,3},{4,20},{20... | collective-permute-start | bytes 122888 | tf_op jit(solution)/shard_map/ppermute | solution.py:438
  25.5 3.3 %collective-permute-start.10 = (bf16[160,256]{1,0:T(8,128)(2,1)S(1)}, bf16[160,256]{1,0:T(8,128)(2,1)S(1)}, u32[]{:S(2)}, u32[]{:S(2)}) collective-permute-start(bf16[160,256]{1,0:T(8,128)(2,1)S(1)} %get-tuple-element.65), channel_id=1, source_target_pairs={{0,4},{4,0},{8,12},{12,8},{1,5},{5,1},{9,13},{13,9},{2,6},{6,2},{1... | collective-permute-start | bytes 245768 | tf_op jit(solution)/shard_map/ppermute | solution.py:438
  25.6 4.5 %collective-permute-start.11 = (bf16[160,256]{1,0:T(8,128)(2,1)S(1)}, bf16[160,256]{1,0:T(8,128)(2,1)S(1)}, u32[]{:S(2)}, u32[]{:S(2)}) collective-permute-start(bf16[160,256]{1,0:T(8,128)(2,1)S(1)} %get-tuple-element.66), channel_id=1, source_target_pairs={{0,1},{12,13},{4,8},{8,4},{1,0},{13,12},{5,9},{9,5},{2,3},{14,15},... | collective-permute-start | bytes 245768 | tf_op jit(solution)/shard_map/ppermute | solution.py:63
  26.4 4.0 %collective-permute-start.12 = (bf16[80,256]{1,0:T(8,128)(2,1)S(1)}, bf16[80,256]{1,0:T(8,128)(2,1)S(1)}, u32[]{:S(2)}, u32[]{:S(2)}) collective-permute-start(bf16[80,256]{1,0:T(8,128)(2,1)S(1)} %get-tuple-element.68), channel_id=1, source_target_pairs={{0,16},{16,0},{1,17},{17,1},{2,18},{18,2},{3,19},{19,3},{4,20},{20... | collective-permute-start | bytes 122888 | tf_op jit(solution)/shard_map/ppermute | solution.py:438
  30.7 6.3 %collective-permute-start.15 = (f32[16,8,128]{2,1,0:T(8,128)S(1)}, f32[16,8,128]{2,1,0:T(8,128)S(1)}, u32[]{:S(2)}, u32[]{:S(2)}) collective-permute-start(f32[16,8,128]{2,1,0:T(8,128)S(1)} %get-tuple-element.72), channel_id=1, source_target_pairs={{0,3},{1,2},{2,1},{3,0},{4,7},{5,6},{6,5},{7,4},{8,11},{9,10},{10,... | collective-permute-start | bytes 196616 | tf_op jit(solution)/shard_map/ppermute | solution.py:438
  34.1 5.9 %collective-permute-start.14 = (f32[16,8,128]{2,1,0:T(8,128)S(1)}, f32[16,8,128]{2,1,0:T(8,128)S(1)}, u32[]{:S(2)}, u32[]{:S(2)}) collective-permute-start(f32[16,8,128]{2,1,0:T(8,128)S(1)} %get-tuple-element.72), channel_id=1, source_target_pairs={{0,2},{1,3},{2,0},{3,1},{4,6},{5,7},{6,4},{7,5},{8,10},{9,11},{10,... | collective-permute-start | bytes 196616 | tf_op jit(solution)/shard_map/ppermute | solution.py:438
  34.1 5.9 %collective-permute-start.13 = (f32[16,8,128]{2,1,0:T(8,128)S(1)}, f32[16,8,128]{2,1,0:T(8,128)S(1)}, u32[]{:S(2)}, u32[]{:S(2)}) collective-permute-start(f32[16,8,128]{2,1,0:T(8,128)S(1)} %get-tuple-element.72), channel_id=1, source_target_pairs={{0,1},{1,0},{2,3},{3,2},{4,5},{5,4},{6,7},{7,6},{8,9},{9,8},{10,11... | collective-permute-start | bytes 196616 | tf_op jit(solution)/shard_map/ppermute | solution.py:438

commit v6 on v5

--- a/solution.py
+++ b/solution.py
@@ -16,7 +16,7 @@
 BF16 = jnp.bfloat16
 
 
-def vmem_call(kernel, outs, args, scratch=(), flops=0, hbm_in=(), hbm_out=(), smem_in=()):
+def vmem_call(kernel, outs, args, scratch=(), flops=0, hbm_in=(), hbm_out=(), smem_in=(), aliases=None):
     in_specs = [
         pl.BlockSpec(memory_space=pltpu.HBM if i in hbm_in else pltpu.SMEM if i in smem_in else pltpu.VMEM)
         for i in range(len(args))
@@ -31,6 +31,7 @@
             pl.BlockSpec(memory_space=pltpu.HBM if i in hbm_out else pltpu.VMEM) for i in range(len(outs))
         ),
         scratch_shapes=list(scratch),
+        input_output_aliases=aliases or {},
         cost_estimate=pl.CostEstimate(flops=flops, bytes_accessed=moved, transcendentals=0),
         compiler_params=pltpu.CompilerParams(vmem_limit_bytes=VMEM_LIMIT),
     )(*args)
@@ -380,7 +381,6 @@
 
 def correct_y_kernel(part, c2, *refs):
     out, stage = refs[-2:]
-    out[...] = part[...]
     add_halos(out, c2, "gy", refs[0], refs[1] if len(refs) == 4 else None, stage)
 
 
@@ -390,7 +390,6 @@
     refs = refs[1 + with_xo :]
     nxt, refs = refs[0], refs[1:]
     oye, oyo, oxe, oxo, (stage,) = unpack(refs, with_yo, with_xo)
-    nxt[...] = part[...]
     add_halos(nxt, c2, "gx", xe, xo, stage)
     put_faces(nxt, gx_index, gy_index, oye, oyo, oxe, oxo, stage)
 
@@ -399,7 +398,6 @@
     xe, xo = refs[0], refs[1] if with_xo else None
     nxt, coarse, middle, stage = refs[1 + with_xo :]
     cx, cy, nz = nxt.shape
-    nxt[...] = part[...]
     add_halos(nxt, c2, "gx", xe, xo, stage)
     pairs = lax.div(lax.broadcasted_iota(jnp.int32, (nz, nz // 2), 0), jnp.int32(2)) == lax.broadcasted_iota(
         jnp.int32, (nz, nz // 2), 1
@@ -501,7 +499,10 @@
     )
 
     def correct_y(part, ye, yo):
-        return vmem_call(correct_y_kernel, [sds(tile)], [part, c2] + [a for a in (ye, yo) if a is not None], [stage])[0]
+        return vmem_call(
+            correct_y_kernel, [sds(tile)], [part, c2] + [a for a in (ye, yo) if a is not None], [stage],
+            aliases={0: 0},
+        )[0]
 
     part = correct_y(part, rye, ryo)
     nxt, contrib, *faces = vmem_call(
@@ -535,6 +536,7 @@
                 [sds(tile)] + face_shapes(),
                 [part, c2] + halos,
                 [stage],
+                aliases={0: 0},
             )
         else:
             nxt, coarse = vmem_call(
@@ -542,6 +544,7 @@
                 [sds(tile), sds((cx // 2, cy // 2, nz // 2))],
                 [part, c2, accel, fine] + halos,
                 [pltpu.VMEM((cx * cy // 2, nz // 2), F32), stage],
+                aliases={0: 0},
             )
         previous, current = current, nxt
     bit = 1

time: 40.8 us -> 40.7 us (level)
  no operation moved by 1% of the time
where the time goes in v6:
time: 40.7 us; the launch traced here: 40.5 us
  starting transfers between devices  19.2 us (47%)
  waiting for transfers between devices  10.6 us (26%)
  Pallas kernels  8.46 us (21%)
  between operations  1.5 us (4%)
  other arithmetic  0.67 us (2%)
    ppermute x12, starting transfers between devices, swap(): return odd_swap(x, axis) if pairs is None else lax.ppermute(x, axis, pairs)  14.6 us
    pallas_call x14, Pallas kernels, vmem_call(): pl.pallas_call(kernel, out_shape=tuple(outs), in_specs=in_specs, out_spec...  8.46 us
    ppermute x12, waiting for transfers between devices, swap(): return odd_swap(x, axis) if pairs is None else lax.ppermute(x, axis, pairs)  7.29 us
    ppermute x4, starting transfers between devices, odd_swap(): return lax.ppermute(x, (axis, 'shot'), pairs)  4.61 us
    ppermute x4, waiting for transfers between devices, odd_swap(): return lax.ppermute(x, (axis, 'shot'), pairs)  3.35 us
  transfers between devices with their start and end apart: 16, of which 8 were waited for; matrix products, arithmetic and copies ran while one was open for 0% of the time, Pallas kernels for 18%

profile of v6, /device:TPU:0, one launch (start us, length us, event | category | flops | bytes accessed | tf_op | source)
XLA Modules:
  0.0 40.5 jit_solution(3703806893718485645)
XLA Ops:
  0.6 3.0 %collective-permute-start = (bf16[1,4,64]{2,1,0:T(4,128)(2,1)}, bf16[1,4,64]{2,1,0:T(4,128)(2,1)S(1)}, u32[]{:S(2)}, u32[]{:S(2)}) collective-permute-start(bf16[1,4,64]{2,1,0:T(4,128)(2,1)} %traces_in.1), channel_id=1, source_target_pairs={{0,8},{4,12},{8,0},{12,4},{1,9},{5,13},{9,1},{13,5},{2,10},{6,14},... | collective-permute-start | bytes 1544 | tf_op jit(solution)/shard_map/ppermute | solution.py:436
  4.3 1.2 %shard_map.112 = (f32[32,16,256]{2,1,0:T(8,128)S(1)}, bf16[512,256]{1,0:T(8,128)(2,1)S(1)}, bf16[256,128]{1,0:T(8,128)(2,1)S(1)}, bf16[512,192]{1,0:T(8,128)(2,1...) custom-call(f32[32,16,256]{2,1,0:T(8,128)} %bitcast.18, ...), custom_call_target="tpu_custom_call" | custom-call | bytes 1815556 | tf_op jit(solution)/shard_map/pallas_call | solution.py:26
  5.7 2.0 %collective-permute-start.2 = (bf16[160,256]{1,0:T(8,128)(2,1)S(1)}, bf16[160,256]{1,0:T(8,128)(2,1)S(1)}, u32[]{:S(2)}, u32[]{:S(2)}) collective-permute-start(bf16[160,256]{1,0:T(8,128)(2,1)S(1)} %get-tuple-element.48), channel_id=1, source_target_pairs={{0,1},{12,13},{4,8},{8,4},{1,0},{13,12},{5,9},{9,5},{2,3},{14,15},... | collective-permute-start | bytes 245768 | tf_op jit(solution)/shard_map/ppermute | solution.py:64
  7.7 2.2 %shard_map.113 = (f32[32,16,256]{2,1,0:T(8,128)S(1)}, f32[32,16,256]{2,1,0:T(8,128)}, f32[32,16,256]{2,1,0:T(8,128)S(1)}, bf16[64,16,256]{2,1,0:T(8,128)(2,1)S(1)}) custom-call(f32[32,16,256]{2,1,0:T(8,128)S(1)} %get-tuple-element.39.cur.prev, bf16[512,256]{1,0:T(8,128)(2,1)S(1)} %get-tuple-element.40.toeplitz, ...), custom_call_target="tpu_custom_call" | custom-call | flops 7864320 | bytes 4521984 | tf_op jit(solution)/shard_map/pallas_call | solution.py:26
  10.0 1.6 %collective-permute-start.3 = (bf16[96,256]{1,0:T(8,128)(2,1)S(1)}, bf16[96,256]{1,0:T(8,128)(2,1)S(1)}, u32[]{:S(2)}, u32[]{:S(2)}) collective-permute-start(bf16[96,256]{1,0:T(8,128)(2,1)S(1)} %pad_maximum_fusion), channel_id=1, source_target_pairs={{0,16},{16,0},{1,17},{17,1},{2,18},{18,2},{3,19},{19,3},{4,20},{20... | collective-permute-start | bytes 147464 | tf_op jit(solution)/shard_map/ppermute | solution.py:436
  11.7 2.5 %collective-permute-done.3.refs_2_ = bf16[96,256]{1,0:T(8,128)(2,1)S(1)} collective-permute-done((bf16[96,256]{1,0:T(8,128)(2,1)S(1)}, bf16[96,256]{1,0:T(8,128)(2,1)S(1)}, u32[]{:S(2)}, u32[]{:S(2)}) %collective-permute-start.3) | collective-permute-done | bytes 49184 | tf_op jit(solution)/shard_map/ppermute | solution.py:436
  14.1 0.7 %shard_map.115 = (f32[32,16,256]{2,1,0:T(8,128)S(1)}, bf16[4,192,256]{2,1,0:T(8,128)(2,1)S(1)}, bf16[160,256]{1,0:T(8,128)(2,1)S(1)}, bf16[160,256]{1,0:T(8,128)(2,1)S(1)}, bf16[80,256]{1,0:T(8,128)(2,1)S(1)}) custom-call(s32[64,128]{1,0:T(8,128)S(1)} %get-tuple-element.38.owners, bf16[64,16,256]{2,1,0:T(8,128)(2,1)S(1)} %get-tuple-element.42.weights, ...), custom_call_target="tpu_custom_call" | custom-call | bytes 3145728 | tf_op jit(solution)/shard_map/pallas_call | solution.py:26
  15.4 2.0 %collective-permute-start.6 = (bf16[80,256]{1,0:T(8,128)(2,1)S(1)}, bf16[80,256]{1,0:T(8,128)(2,1)S(1)}, u32[]{:S(2)}, u32[]{:S(2)}) collective-permute-start(bf16[80,256]{1,0:T(8,128)(2,1)S(1)} %get-tuple-element.55), channel_id=1, source_target_pairs={{0,16},{16,0},{1,17},{17,1},{2,18},{18,2},{3,19},{19,3},{4,20},{20... | collective-permute-start | bytes 122888 | tf_op jit(solution)/shard_map/ppermute | solution.py:436
  17.3 0.8 %shard_map.116 = (f32[32,16,256]{2,1,0:T(8,128)S(1)}, f32[32,16,256]{2,1,0:T(8,128)S(1)}) custom-call(f32[32,16,256]{2,1,0:T(8,128)S(1)} %get-tuple-element.50.cur.prev, f32[32,16,256]{2,1,0:T(8,128)S(1)} %get-tuple-element.39.cur.prev, f32[32,16,256]{2,1,0:T(8,128)S(1)} %get-tuple-element.45.c2, bf16[512,256]{1,0:T(8,128)(2,1)S(1)} %get-tuple-element.40.toeplitz, ...), custom_call_target="tpu_custom_call" | custom-call | flops 7864320 | bytes 4587520 | tf_op jit(solution)/shard_map/pallas_call | solution.py:26
  18.2 1.3 %collective-permute-done.5.refs_1_ = bf16[160,256]{1,0:T(8,128)(2,1)S(1)} collective-permute-done((bf16[160,256]{1,0:T(8,128)(2,1)S(1)}, bf16[160,256]{1,0:T(8,128)(2,1)S(1)}, u32[]{:S(2)}, u32[]{:S(2)}) %collective-permute-start.5) | collective-permute-done | bytes 81952 | tf_op jit(solution)/shard_map/ppermute | solution.py:64
  20.0 1.3 %collective-permute-start.8 = (bf16[160,256]{1,0:T(8,128)(2,1)S(1)}, bf16[160,256]{1,0:T(8,128)(2,1)S(1)}, u32[]{:S(2)}, u32[]{:S(2)}) collective-permute-start(bf16[160,256]{1,0:T(8,128)(2,1)S(1)} %get-tuple-element.60), channel_id=1, source_target_pairs={{0,1},{12,13},{4,8},{8,4},{1,0},{13,12},{5,9},{9,5},{2,3},{14,15},... | collective-permute-start | bytes 245768 | tf_op jit(solution)/shard_map/ppermute | solution.py:64
  21.3 1.5 %collective-permute-start.9 = (bf16[80,256]{1,0:T(8,128)(2,1)S(1)}, bf16[80,256]{1,0:T(8,128)(2,1)S(1)}, u32[]{:S(2)}, u32[]{:S(2)}) collective-permute-start(bf16[80,256]{1,0:T(8,128)(2,1)S(1)} %get-tuple-element.61), channel_id=1, source_target_pairs={{0,16},{16,0},{1,17},{17,1},{2,18},{18,2},{3,19},{19,3},{4,20},{20... | collective-permute-start | bytes 122888 | tf_op jit(solution)/shard_map/ppermute | solution.py:436
  22.8 0.8 %shard_map.119 = (f32[32,16,256]{2,1,0:T(8,128)S(1)}, f32[32,16,256]{2,1,0:T(8,128)S(1)}) custom-call(f32[32,16,256]{2,1,0:T(8,128)S(1)} %get-tuple-element.56.cur.prev, f32[32,16,256]{2,1,0:T(8,128)S(1)} %get-tuple-element.50.cur.prev, f32[32,16,256]{2,1,0:T(8,128)S(1)} %get-tuple-element.45.c2, bf16[512,256]{1,0:T(8,128)(2,1)S(1)} %get-tuple-element.40.toeplitz, ...), custom_call_target="tpu_custom_call" | custom-call | flops 7864320 | bytes 5111808 | tf_op jit(solution)/shard_map/pallas_call | solution.py:26
  23.6 0.8 %collective-permute-done.8.refs_1_ = bf16[160,256]{1,0:T(8,128)(2,1)S(1)} collective-permute-done((bf16[160,256]{1,0:T(8,128)(2,1)S(1)}, bf16[160,256]{1,0:T(8,128)(2,1)S(1)}, u32[]{:S(2)}, u32[]{:S(2)}) %collective-permute-start.8) | collective-permute-done | bytes 81952 | tf_op jit(solution)/shard_map/ppermute | solution.py:64
  24.5 0.8 %collective-permute-done.9.refs_0_ = bf16[80,256]{1,0:T(8,128)(2,1)S(1)} collective-permute-done((bf16[80,256]{1,0:T(8,128)(2,1)S(1)}, bf16[80,256]{1,0:T(8,128)(2,1)S(1)}, u32[]{:S(2)}, u32[]{:S(2)}) %collective-permute-start.9) | collective-permute-done | bytes 40992 | tf_op jit(solution)/shard_map/ppermute | solution.py:436
  25.5 0.8 %collective-permute-start.11 = (bf16[160,256]{1,0:T(8,128)(2,1)S(1)}, bf16[160,256]{1,0:T(8,128)(2,1)S(1)}, u32[]{:S(2)}, u32[]{:S(2)}) collective-permute-start(bf16[160,256]{1,0:T(8,128)(2,1)S(1)} %get-tuple-element.66), channel_id=1, source_target_pairs={{0,1},{12,13},{4,8},{8,4},{1,0},{13,12},{5,9},{9,5},{2,3},{14,15},... | collective-permute-start | bytes 245768 | tf_op jit(solution)/shard_map/ppermute | solution.py:64
  26.3 1.6 %collective-permute-start.12 = (bf16[80,256]{1,0:T(8,128)(2,1)S(1)}, bf16[80,256]{1,0:T(8,128)(2,1)S(1)}, u32[]{:S(2)}, u32[]{:S(2)}) collective-permute-start(bf16[80,256]{1,0:T(8,128)(2,1)S(1)} %get-tuple-element.68), channel_id=1, source_target_pairs={{0,16},{16,0},{1,17},{17,1},{2,18},{18,2},{3,19},{19,3},{4,20},{20... | collective-permute-start | bytes 122888 | tf_op jit(solution)/shard_map/ppermute | solution.py:436
  27.9 0.8 %shard_map.122 = (f32[32,16,256]{2,1,0:T(8,128)S(1)}, f32[32,16,256]{2,1,0:T(8,128)S(1)}) custom-call(f32[32,16,256]{2,1,0:T(8,128)S(1)} %get-tuple-element.62.cur.a_in, f32[32,16,256]{2,1,0:T(8,128)S(1)} %get-tuple-element.56.cur.prev, f32[32,16,256]{2,1,0:T(8,128)S(1)} %get-tuple-element.45.c2, bf16[512,256]{1,0:T(8,128)(2,1)S(1)} %get-tuple-element.40.toeplitz, ...), custom_call_target="tpu_custom_call" | custom-call | flops 7864320 | bytes 5111808 | tf_op jit(solution)/shard_map/pallas_call | solution.py:26
  28.7 1.3 %collective-permute-done.11.refs_1_ = bf16[160,256]{1,0:T(8,128)(2,1)S(1)} collective-permute-done((bf16[160,256]{1,0:T(8,128)(2,1)S(1)}, bf16[160,256]{1,0:T(8,128)(2,1)S(1)}, u32[]{:S(2)}, u32[]{:S(2)}) %collective-permute-start.11) | collective-permute-done | bytes 81952 | tf_op jit(solution)/shard_map/ppermute | solution.py:64
  30.6 3.4 %collective-permute-start.15 = (f32[16,8,128]{2,1,0:T(8,128)S(1)}, f32[16,8,128]{2,1,0:T(8,128)S(1)}, u32[]{:S(2)}, u32[]{:S(2)}) collective-permute-start(f32[16,8,128]{2,1,0:T(8,128)S(1)} %get-tuple-element.72), channel_id=1, source_target_pairs={{0,3},{1,2},{2,1},{3,0},{4,7},{5,6},{6,5},{7,4},{8,11},{9,10},{10,... | collective-permute-start | bytes 196616 | tf_op jit(solution)/shard_map/ppermute | solution.py:436
  34.0 1.1 %collective-permute-start.13 = (f32[16,8,128]{2,1,0:T(8,128)S(1)}, f32[16,8,128]{2,1,0:T(8,128)S(1)}, u32[]{:S(2)}, u32[]{:S(2)}) collective-permute-start(f32[16,8,128]{2,1,0:T(8,128)S(1)} %get-tuple-element.72), channel_id=1, source_target_pairs={{0,1},{1,0},{2,3},{3,2},{4,5},{5,4},{6,7},{7,6},{8,9},{9,8},{10,11... | collective-permute-start | bytes 196616 | tf_op jit(solution)/shard_map/ppermute | solution.py:436
  35.0 1.0 %shard_map.125 = (f32[32,16,256]{2,1,0:T(8,128)}, f32[32,16,256]{2,1,0:T(8,128)}) custom-call(f32[32,16,256]{2,1,0:T(8,128)S(1)} %get-tuple-element.62.cur.a_in, f32[32,16,256]{2,1,0:T(8,128)S(1)} %get-tuple-element.69.b_in), custom_call_target="tpu_custom_call" | custom-call | bytes 2097152 | tf_op jit(solution)/shard_map/pallas_call | solution.py:26
  36.0 0.9 %collective-permute-done.15 = f32[16,8,128]{2,1,0:T(8,128)S(1)} collective-permute-done((f32[16,8,128]{2,1,0:T(8,128)S(1)}, f32[16,8,128]{2,1,0:T(8,128)S(1)}, u32[]{:S(2)}, u32[]{:S(2)}) %collective-permute-start.15) | collective-permute-done | bytes 65568 | tf_op jit(solution)/shard_map/ppermute | solution.py:436
  36.9 3.0 %collective-permute-done.14 = f32[16,8,128]{2,1,0:T(8,128)S(1)} collective-permute-done((f32[16,8,128]{2,1,0:T(8,128)S(1)}, f32[16,8,128]{2,1,0:T(8,128)S(1)}, u32[]{:S(2)}, u32[]{:S(2)}) %collective-permute-start.14) | collective-permute-done | bytes 65568 | tf_op jit(solution)/shard_map/ppermute | solution.py:436
  (31 shorter events, 2.8 us)
Async XLA Ops:
  0.6 4.9 %collective-permute-start = (bf16[1,4,64]{2,1,0:T(4,128)(2,1)}, bf16[1,4,64]{2,1,0:T(4,128)(2,1)S(1)}, u32[]{:S(2)}, u32[]{:S(2)}) collective-permute-start(bf16[1,4,64]{2,1,0:T(4,128)(2,1)} %traces_in.1), channel_id=1, source_target_pairs={{0,8},{4,12},{8,0},{12,4},{1,9},{5,13},{9,1},{13,5},{2,10},{6,14},... | collective-permute-start | bytes 1544 | tf_op jit(solution)/shard_map/ppermute | solution.py:436
  5.6 4.3 %collective-permute-start.1 = (bf16[168,256]{1,0:T(8,128)(2,1)S(1)}, bf16[168,256]{1,0:T(8,128)(2,1)S(1)}, u32[]{:S(2)}, u32[]{:S(2)}) collective-permute-start(bf16[168,256]{1,0:T(8,128)(2,1)S(1)} %maximum_maximum_fusion), channel_id=1, source_target_pairs={{0,4},{4,0},{8,12},{12,8},{1,5},{5,1},{9,13},{13,9},{2,6},{6,2},{1... | collective-permute-start | bytes 258056 | tf_op jit(solution)/shard_map/ppermute | solution.py:436
  5.7 5.9 %collective-permute-start.2 = (bf16[160,256]{1,0:T(8,128)(2,1)S(1)}, bf16[160,256]{1,0:T(8,128)(2,1)S(1)}, u32[]{:S(2)}, u32[]{:S(2)}) collective-permute-start(bf16[160,256]{1,0:T(8,128)(2,1)S(1)} %get-tuple-element.48), channel_id=1, source_target_pairs={{0,1},{12,13},{4,8},{8,4},{1,0},{13,12},{5,9},{9,5},{2,3},{14,15},... | collective-permute-start | bytes 245768 | tf_op jit(solution)/shard_map/ppermute | solution.py:64
  10.0 4.2 %collective-permute-start.3 = (bf16[96,256]{1,0:T(8,128)(2,1)S(1)}, bf16[96,256]{1,0:T(8,128)(2,1)S(1)}, u32[]{:S(2)}, u32[]{:S(2)}) collective-permute-start(bf16[96,256]{1,0:T(8,128)(2,1)S(1)} %pad_maximum_fusion), channel_id=1, source_target_pairs={{0,16},{16,0},{1,17},{17,1},{2,18},{18,2},{3,19},{19,3},{4,20},{20... | collective-permute-start | bytes 147464 | tf_op jit(solution)/shard_map/ppermute | solution.py:436
  14.1 3.2 %copy-start = (bf16[1,4,32,16,256]{4,3,2,1,0:T(8,128)(2,1)S(1)}, bf16[1,4,32,16,256]{4,3,2,1,0:T(8,128)(2,1)}, u32[]{:S(2)}) copy-start(bf16[1,4,32,16,256]{4,3,2,1,0:T(8,128)(2,1)} %param.11) | copy-start | bytes 3145732
  14.8 3.3 %collective-permute-start.4 = (bf16[160,256]{1,0:T(8,128)(2,1)S(1)}, bf16[160,256]{1,0:T(8,128)(2,1)S(1)}, u32[]{:S(2)}, u32[]{:S(2)}) collective-permute-start(bf16[160,256]{1,0:T(8,128)(2,1)S(1)} %get-tuple-element.53), channel_id=1, source_target_pairs={{0,4},{4,0},{8,12},{12,8},{1,5},{5,1},{9,13},{13,9},{2,6},{6,2},{1... | collective-permute-start | bytes 245768 | tf_op jit(solution)/shard_map/ppermute | solution.py:436
  14.9 4.5 %collective-permute-start.5 = (bf16[160,256]{1,0:T(8,128)(2,1)S(1)}, bf16[160,256]{1,0:T(8,128)(2,1)S(1)}, u32[]{:S(2)}, u32[]{:S(2)}) collective-permute-start(bf16[160,256]{1,0:T(8,128)(2,1)S(1)} %get-tuple-element.54), channel_id=1, source_target_pairs={{0,1},{12,13},{4,8},{8,4},{1,0},{13,12},{5,9},{9,5},{2,3},{14,15},... | collective-permute-start | bytes 245768 | tf_op jit(solution)/shard_map/ppermute | solution.py:64
  15.4 4.2 %collective-permute-start.6 = (bf16[80,256]{1,0:T(8,128)(2,1)S(1)}, bf16[80,256]{1,0:T(8,128)(2,1)S(1)}, u32[]{:S(2)}, u32[]{:S(2)}) collective-permute-start(bf16[80,256]{1,0:T(8,128)(2,1)S(1)} %get-tuple-element.55), channel_id=1, source_target_pairs={{0,16},{16,0},{1,17},{17,1},{2,18},{18,2},{3,19},{19,3},{4,20},{20... | collective-permute-start | bytes 122888 | tf_op jit(solution)/shard_map/ppermute | solution.py:436
  19.7 3.9 %collective-permute-start.7 = (bf16[160,256]{1,0:T(8,128)(2,1)S(1)}, bf16[160,256]{1,0:T(8,128)(2,1)S(1)}, u32[]{:S(2)}, u32[]{:S(2)}) collective-permute-start(bf16[160,256]{1,0:T(8,128)(2,1)S(1)} %get-tuple-element.59), channel_id=1, source_target_pairs={{0,4},{4,0},{8,12},{12,8},{1,5},{5,1},{9,13},{13,9},{2,6},{6,2},{1... | collective-permute-start | bytes 245768 | tf_op jit(solution)/shard_map/ppermute | solution.py:436
  20.0 4.4 %collective-permute-start.8 = (bf16[160,256]{1,0:T(8,128)(2,1)S(1)}, bf16[160,256]{1,0:T(8,128)(2,1)S(1)}, u32[]{:S(2)}, u32[]{:S(2)}) collective-permute-start(bf16[160,256]{1,0:T(8,128)(2,1)S(1)} %get-tuple-element.60), channel_id=1, source_target_pairs={{0,1},{12,13},{4,8},{8,4},{1,0},{13,12},{5,9},{9,5},{2,3},{14,15},... | collective-permute-start | bytes 245768 | tf_op jit(solution)/shard_map/ppermute | solution.py:64
  21.3 4.0 %collective-permute-start.9 = (bf16[80,256]{1,0:T(8,128)(2,1)S(1)}, bf16[80,256]{1,0:T(8,128)(2,1)S(1)}, u32[]{:S(2)}, u32[]{:S(2)}) collective-permute-start(bf16[80,256]{1,0:T(8,128)(2,1)S(1)} %get-tuple-element.61), channel_id=1, source_target_pairs={{0,16},{16,0},{1,17},{17,1},{2,18},{18,2},{3,19},{19,3},{4,20},{20... | collective-permute-start | bytes 122888 | tf_op jit(solution)/shard_map/ppermute | solution.py:436
  25.4 3.3 %collective-permute-start.10 = (bf16[160,256]{1,0:T(8,128)(2,1)S(1)}, bf16[160,256]{1,0:T(8,128)(2,1)S(1)}, u32[]{:S(2)}, u32[]{:S(2)}) collective-permute-start(bf16[160,256]{1,0:T(8,128)(2,1)S(1)} %get-tuple-element.65), channel_id=1, source_target_pairs={{0,4},{4,0},{8,12},{12,8},{1,5},{5,1},{9,13},{13,9},{2,6},{6,2},{1... | collective-permute-start | bytes 245768 | tf_op jit(solution)/shard_map/ppermute | solution.py:436
  25.5 4.5 %collective-permute-start.11 = (bf16[160,256]{1,0:T(8,128)(2,1)S(1)}, bf16[160,256]{1,0:T(8,128)(2,1)S(1)}, u32[]{:S(2)}, u32[]{:S(2)}) collective-permute-start(bf16[160,256]{1,0:T(8,128)(2,1)S(1)} %get-tuple-element.66), channel_id=1, source_target_pairs={{0,1},{12,13},{4,8},{8,4},{1,0},{13,12},{5,9},{9,5},{2,3},{14,15},... | collective-permute-start | bytes 245768 | tf_op jit(solution)/shard_map/ppermute | solution.py:64
  26.3 4.0 %collective-permute-start.12 = (bf16[80,256]{1,0:T(8,128)(2,1)S(1)}, bf16[80,256]{1,0:T(8,128)(2,1)S(1)}, u32[]{:S(2)}, u32[]{:S(2)}) collective-permute-start(bf16[80,256]{1,0:T(8,128)(2,1)S(1)} %get-tuple-element.68), channel_id=1, source_target_pairs={{0,16},{16,0},{1,17},{17,1},{2,18},{18,2},{3,19},{19,3},{4,20},{20... | collective-permute-start | bytes 122888 | tf_op jit(solution)/shard_map/ppermute | solution.py:436
  30.6 6.3 %collective-permute-start.15 = (f32[16,8,128]{2,1,0:T(8,128)S(1)}, f32[16,8,128]{2,1,0:T(8,128)S(1)}, u32[]{:S(2)}, u32[]{:S(2)}) collective-permute-start(f32[16,8,128]{2,1,0:T(8,128)S(1)} %get-tuple-element.72), channel_id=1, source_target_pairs={{0,3},{1,2},{2,1},{3,0},{4,7},{5,6},{6,5},{7,4},{8,11},{9,10},{10,... | collective-permute-start | bytes 196616 | tf_op jit(solution)/shard_map/ppermute | solution.py:436
  34.0 5.9 %collective-permute-start.14 = (f32[16,8,128]{2,1,0:T(8,128)S(1)}, f32[16,8,128]{2,1,0:T(8,128)S(1)}, u32[]{:S(2)}, u32[]{:S(2)}) collective-permute-start(f32[16,8,128]{2,1,0:T(8,128)S(1)} %get-tuple-element.72), channel_id=1, source_target_pairs={{0,2},{1,3},{2,0},{3,1},{4,6},{5,7},{6,4},{7,5},{8,10},{9,11},{10,... | collective-permute-start | bytes 196616 | tf_op jit(solution)/shard_map/ppermute | solution.py:436
  34.0 5.9 %collective-permute-start.13 = (f32[16,8,128]{2,1,0:T(8,128)S(1)}, f32[16,8,128]{2,1,0:T(8,128)S(1)}, u32[]{:S(2)}, u32[]{:S(2)}) collective-permute-start(f32[16,8,128]{2,1,0:T(8,128)S(1)} %get-tuple-element.72), channel_id=1, source_target_pairs={{0,1},{1,0},{2,3},{3,2},{4,5},{5,4},{6,7},{7,6},{8,9},{9,8},{10,11... | collective-permute-start | bytes 196616 | tf_op jit(solution)/shard_map/ppermute | solution.py:436
